TPU v7x, 32 devices: a whole 2x2x4 slice. The times are simulated.
32 devices in a mesh: dp: 8 (over y, x, core), head: 4 (over z).
Axes of the slice: x: 2, y: 2, z: 4, core: 2. Of those that a mesh axis runs over, the one named last changes fastest.
Arguments:
- tokens: bfloat16 [16384, 1024], P(('dp', 'head')), may hold values from -6 to 6
- first_values: bfloat16 [16384, 1024], P('dp', 'head'), may hold values from -6 to 6
- mixer_in: float32 [3, 1024, 1024], P(None, 'dp', 'head'), may hold values from -0.1875 to 0.1875
- mixer_out: float32 [1024, 1024], P('head', 'dp'), may hold values from -0.75 to 0.75
- gate_up: float32 [2, 1024, 2816], P(None, 'dp', 'head'), may hold values from -0.1875 to 0.1875
- down_weight: float32 [2816, 1024], P('head', 'dp'), may hold values from -0.109375 to 0.109375
- norm_gains: float32 [2, 1024], P(None, 'dp'), may hold values from 0.5 to 1.5
- lengths: int32 [8], P('dp'), may hold values from 128 to 2048, as said below
- cotangent: bfloat16 [16384, 1024], P(('dp', 'head')), may hold values from -6 to 6
Outputs:
- block_out: bfloat16 [16384, 1024], P(('dp', 'head'))
- tokens_grad: float32 [16384, 1024], P(('dp', 'head'))
- first_grad: float32 [16384, 1024], P('dp', 'head')
- mixer_in_grad: float32 [3, 1024, 1024], P(None, 'dp', 'head')
- mixer_out_grad: float32 [1024, 1024], P('head', 'dp')
- gate_up_grad: float32 [2, 1024, 2816], P(None, 'dp', 'head')
- down_grad: float32 [2816, 1024], P('head', 'dp')
- gains_grad: float32 [2, 1024], P(None, 'dp')
Inputs may be any that keep to these rules, and one draw needn't show every extreme that they name: `lengths`: positions from a sequence's length on are padding; some sequence has exactly 2048 real tokens in every draw.
All inputs are finite; a program needn't handle non-finite values.
Results may differ from a plain program's by a relative error of at most 0.013.
The roundings to bfloat16 on the way count: a program that leaves them out, or rounds other values in their place, can miss the bound.
Values may be sent and summed in bfloat16 or wider, within the bound.
No kernel may reach another device: no remote copies, remote signals or barrier semaphores. Data moves between devices by JAX's collectives and lax.ppermute only.
A program may use at most 128 MiB of HBM per device.

v0:
```python
import functools

import jax
import jax.numpy as jnp
from jax import lax
from jax.experimental import pallas as pl
from jax.experimental.pallas import tpu as pltpu
from jax.sharding import PartitionSpec as P

HDIM = 64
SEQ = 2048
LANES = 128
GAIN_ROWS = 16

epsilon = 1e-05
far_below = -1e30
rope_base = 10000.0
low = jnp.bfloat16
wide = jnp.float32
VMEM_BYTES = 60 * 1024 * 1024


def dot_nn(a, b):
    return lax.dot_general(a, b, (((1,), (0,)), ((), ())), preferred_element_type=wide)


def dot_nt(a, b):
    return lax.dot_general(a, b, (((1,), (1,)), ((), ())), preferred_element_type=wide)


def dot_tn(a, b):
    return lax.dot_general(a, b, (((0,), (0,)), ((), ())), preferred_element_type=wide)


def rope_tables():
    half = HDIM // 2
    rates = rope_base ** (-jnp.arange(half, dtype=wide) * 2.0 / HDIM)
    angles = jnp.arange(SEQ, dtype=wide)[:, None] * rates[None, :]
    cosine, sine = jnp.cos(angles), jnp.sin(angles)
    pair = LANES // HDIM
    return (
        jnp.concatenate([cosine, cosine] * pair, axis=1),
        jnp.concatenate([-sine, sine] * pair, axis=1),
    )


def swap_halves(field):
    half = HDIM // 2
    lane = lax.broadcasted_iota(jnp.int32, field.shape, 1)
    ahead = pltpu.roll(field, LANES - half, 1)
    behind = pltpu.roll(field, half, 1)
    return jnp.where(lane % HDIM < half, ahead, behind)


def rms_parts(field, gain):
    factor = lax.rsqrt(jnp.mean(field * field, axis=-1, keepdims=True) + epsilon)
    unit = field * factor
    return (unit * gain, unit, factor)


def rms_back(normed_grad, unit, factor, gain):
    scaled = normed_grad * gain
    return factor * (scaled - unit * jnp.mean(scaled * unit, axis=-1, keepdims=True))


def project_kernel(place, x_ref, w_ref, gain_ref, first_ref, cos_ref, sin_ref, *refs):
    q_ref, k_ref, v_ref, normed_ref = refs[-4:]
    rows, depth = normed_ref.shape
    width = x_ref.shape[1]
    if width == depth:
        width = depth // 4
        blocks = [x_ref[:, start : start + width].astype(wide) for start in range(0, depth, width)]
    else:
        starts = range(0, x_ref.shape[0], rows)
        blocks = [x_ref[start : start + rows, :].astype(wide) for start in starts]
    squares = sum(jnp.sum(block * block, axis=-1, keepdims=True) for block in blocks)
    factor = lax.rsqrt(squares / depth + epsilon)
    for number, block in enumerate(blocks):
        cols = slice(number * width, (number + 1) * width)
        normed_ref[:, cols] = (block * factor * gain_ref[0:1, cols].astype(wide)).astype(low)
    normed = normed_ref[...]
    cosine, sine = cos_ref[...], sin_ref[...]
    for pair in range(q_ref.shape[1] // LANES):
        cols = slice(pair * LANES, (pair + 1) * LANES)
        start = pair * 3 * LANES
        mixed = dot_nt(normed, w_ref[start : start + 3 * LANES, :])
        for part, out_ref in ((0, q_ref), (1, k_ref)):
            piece = mixed[:, part * LANES : (part + 1) * LANES]
            out_ref[:, cols] = (piece * cosine + swap_halves(piece) * sine).astype(low)
        first = first_ref[:, cols].astype(wide)
        v_ref[:, cols] = (0.5 * mixed[:, 2 * LANES :] + 0.5 * first).astype(low)


def project(index, x, pack, first_values, cosine, sine, made):
    total, cols = first_values.shape
    depth = pack.shape[1]
    rows = x.shape[0] * x.shape[1] // depth
    gain_block = pack.shape[0] // GAIN_ROWS - 1
    fixed = lambda i, p: (0, 0)
    natural = lambda width: pl.BlockSpec((rows, width), lambda i, p: (p[0], 0))
    shapes = [cols, cols, cols, depth]
    spec = pltpu.PrefetchScalarGridSpec(
        num_scalar_prefetch=1,
        grid=(1,),
        in_specs=[
            pl.BlockSpec(x.shape, fixed),
            pl.BlockSpec((3 * cols, depth), fixed),
            pl.BlockSpec((GAIN_ROWS, depth), lambda i, p: (gain_block, 0)),
            natural(cols),
            natural(LANES),
            natural(LANES),
        ]
        + [pl.BlockSpec(memory_space=pl.ANY)] * len(made),
        out_specs=[natural(width) for width in shapes],
    )
    return pl.pallas_call(
        project_kernel,
        grid_spec=spec,
        out_shape=[jax.ShapeDtypeStruct((total, width), low) for width in shapes],
        input_output_aliases={7 + number: number for number in range(len(made))},
        compiler_params=pltpu.CompilerParams(vmem_limit_bytes=VMEM_BYTES),
        cost_estimate=pl.CostEstimate(
            flops=2 * rows * depth * 3 * cols, bytes_accessed=5 << 20, transcendentals=0
        ),
        name="project",
    )(index, x, pack, pack, first_values, cosine, sine, *made)


BLOCK = 512


def both_heads(array):
    lane = lax.broadcasted_iota(jnp.int32, array.shape, 1)
    zero = jnp.zeros_like(array)
    return jnp.concatenate(
        [jnp.where(lane < HDIM, array, zero), jnp.where(lane < HDIM, zero, array)], axis=0
    )


def attend_kernel(len_ref, q_ref, k_ref, v_ref, out_ref, full_ref, lse_ref, acc_ref, max_ref, sum_ref):
    i = pl.program_id(0)
    own = both_heads(q_ref[...] * jnp.asarray(HDIM**-0.5, low))
    max_ref[...] = jnp.full_like(max_ref, far_below)
    sum_ref[...] = jnp.zeros_like(sum_ref)
    acc_ref[...] = jnp.zeros_like(acc_ref)

    def step(j, diagonal):
        at = pl.ds(pl.multiple_of(j * BLOCK, BLOCK), BLOCK)
        scores = dot_nt(own, k_ref[at, :])
        if diagonal:
            q_at = lax.broadcasted_iota(jnp.int32, (BLOCK, BLOCK), 0)
            k_at = lax.broadcasted_iota(jnp.int32, (BLOCK, BLOCK), 1)
            allowed = k_at <= q_at
            allowed = jnp.concatenate([allowed, allowed], axis=0)
            scores = jnp.where(allowed, scores, far_below)
        old = max_ref[...]
        peak = jnp.maximum(old, jnp.max(scores, axis=1, keepdims=True))
        decay = jnp.exp(old - peak)
        max_ref[...] = peak
        total = sum_ref[...] * decay
        powers = []
        for start in range(0, BLOCK, LANES):
            power = jnp.exp(scores[:, start : start + LANES] - peak)
            total += power
            powers.append(power.astype(low))
        sum_ref[...] = total
        acc_ref[...] = acc_ref[...] * decay + dot_nn(jnp.concatenate(powers, axis=1), v_ref[at, :])

    @pl.loop(0, i)
    def _(j):
        step(j, False)

    step(i, True)
    total = jnp.sum(sum_ref[...], axis=1, keepdims=True)
    log_total = max_ref[...] + jnp.log(total)
    for head in range(LANES // HDIM):
        rows = slice(head * BLOCK, (head + 1) * BLOCK)
        lse_ref[head : head + 1, :] = jnp.transpose(log_total[rows])[0:1, :]
    result = acc_ref[...] / total
    lane = lax.broadcasted_iota(jnp.int32, (BLOCK, LANES), 1)
    valid = i * BLOCK + lax.broadcasted_iota(jnp.int32, (BLOCK, 1), 0) < len_ref[0]
    result = jnp.where(valid, jnp.where(lane < HDIM, result[:BLOCK], result[BLOCK:]), 0.0)
    out_ref[...] = result.astype(low)
    full_ref[...] = result


def attend(pair, lengths, query, keys, values):
    rows = query.shape[0]
    block = pl.BlockSpec((BLOCK, LANES), lambda i, n: (i, pair))
    whole = pl.BlockSpec((rows, LANES), lambda i, n: (0, pair))
    result = pl.BlockSpec((BLOCK, LANES), lambda i, n: (i, 0))
    spec = pltpu.PrefetchScalarGridSpec(
        num_scalar_prefetch=1,
        grid=(rows // BLOCK,),
        in_specs=[block, whole, whole],
        out_specs=[result, result, pl.BlockSpec((8, BLOCK), lambda i, n: (0, i))],
        scratch_shapes=[pltpu.VMEM((2 * BLOCK, LANES), wide)] * 3,
    )
    return pl.pallas_call(
        attend_kernel,
        grid_spec=spec,
        out_shape=[
            jax.ShapeDtypeStruct((rows, LANES), low),
            jax.ShapeDtypeStruct((rows, LANES), wide),
            jax.ShapeDtypeStruct((8, rows), wide),
        ],
        compiler_params=pltpu.CompilerParams(vmem_limit_bytes=VMEM_BYTES),
        cost_estimate=pl.CostEstimate(
            flops=8 * rows * rows * LANES, bytes_accessed=4 << 20, transcendentals=rows * rows
        ),
        name="attend",
    )(lengths, query, keys, values)


def attend_back_kernel(
    len_ref, q_ref, k_ref, v_ref, grad_ref, full_ref, lse_ref, cos_ref, sin_ref,
    mixed_ref, first_ref, dk_acc, dv_acc, dq_acc, keys_t,
):
    i = pl.program_id(0)
    count = pl.num_programs(0)
    heads = range(LANES // HDIM)

    @pl.when(i == 0)
    def _():
        dk_acc[...] = jnp.zeros_like(dk_acc)
        dv_acc[...] = jnp.zeros_like(dv_acc)
        for start in range(0, k_ref.shape[0], BLOCK):
            keys_t[:, start : start + BLOCK] = jnp.transpose(k_ref[start : start + BLOCK, :])

    grad = grad_ref[...]
    own = both_heads(q_ref[...] * jnp.asarray(HDIM**-0.5, low))
    own_grad = both_heads(grad)
    columns = [slice(head * HDIM, (head + 1) * HDIM) for head in heads]
    products = jnp.transpose(grad.astype(wide) * full_ref[...])
    offset = jnp.concatenate(
        [jnp.sum(products[rows], axis=0, keepdims=True) for rows in columns], axis=1
    )
    log_total = jnp.concatenate([lse_ref[head : head + 1, :] for head in heads], axis=1)
    dq_acc[...] = jnp.zeros_like(dq_acc)

    def step(j, diagonal):
        at = pl.ds(pl.multiple_of(j * BLOCK, BLOCK), BLOCK)
        scores = dot_nt(k_ref[at, :], own)
        if diagonal:
            k_at = lax.broadcasted_iota(jnp.int32, (BLOCK, BLOCK), 0)
            q_at = lax.broadcasted_iota(jnp.int32, (BLOCK, BLOCK), 1)
            allowed = k_at <= q_at
            allowed = jnp.concatenate([allowed, allowed], axis=1)
            scores = jnp.where(allowed, scores, far_below)
        probs = jnp.exp(scores - log_total)
        prob_grad = dot_nt(v_ref[at, :], own_grad)
        dv_acc[at, :] += dot_nn(probs.astype(low), own_grad)
        raw_grad = (probs * (prob_grad - offset)).astype(low)
        dk_acc[at, :] += dot_nn(raw_grad, own)
        for head, rows in zip(heads, columns):
            dq_acc[rows, :] += dot_nn(
                keys_t[rows, at], raw_grad[:, head * BLOCK : (head + 1) * BLOCK]
            )

    @pl.loop(0, i)
    def _(j):
        step(j, False)

    step(i, True)
    at = pl.ds(pl.multiple_of(i * BLOCK, BLOCK), BLOCK)
    query_grad = jnp.transpose(dq_acc[...]) * HDIM**-0.5
    mixed_ref[at, :LANES] = (
        query_grad * cos_ref[at, :] - swap_halves(query_grad) * sin_ref[at, :]
    ).astype(low)

    @pl.when(i == count - 1)
    def _():
        @pl.loop(0, count)
        def _(j):
            at = pl.ds(pl.multiple_of(j * BLOCK, BLOCK), BLOCK)
            keys_grad = dk_acc[at, :]
            mixed_ref[at, LANES : 2 * LANES] = (
                keys_grad * cos_ref[at, :] - swap_halves(keys_grad) * sin_ref[at, :]
            ).astype(low)
            half_grad = 0.5 * dv_acc[at, :]
            first_ref[at, :] = half_grad
            mixed_ref[at, 2 * LANES :] = half_grad.astype(low)


def attend_back(pair, lengths, query, keys, values, grad, full, lse, cosine, sine):
    rows = query.shape[0]
    block = pl.BlockSpec((BLOCK, LANES), lambda i, n: (i, pair))
    whole = pl.BlockSpec((rows, LANES), lambda i, n: (0, pair))
    given = pl.BlockSpec((BLOCK, LANES), lambda i, n: (i, 0))
    fixed = lambda i, n: (0, 0)
    table = pl.BlockSpec((rows, LANES), fixed)
    spec = pltpu.PrefetchScalarGridSpec(
        num_scalar_prefetch=1,
        grid=(rows // BLOCK,),
        in_specs=[
            block, whole, whole, given, given,
            pl.BlockSpec((8, BLOCK), lambda i, n: (0, i)),
            table, table,
        ],
        out_specs=[pl.BlockSpec((rows, 3 * LANES), fixed), pl.BlockSpec((rows, LANES), fixed)],
        scratch_shapes=[
            pltpu.VMEM((rows, LANES), wide),
            pltpu.VMEM((rows, LANES), wide),
            pltpu.VMEM((LANES, BLOCK), wide),
            pltpu.VMEM((LANES, rows), low),
        ],
    )
    return pl.pallas_call(
        attend_back_kernel,
        grid_spec=spec,
        out_shape=[
            jax.ShapeDtypeStruct((rows, 3 * LANES), low),
            jax.ShapeDtypeStruct((rows, LANES), wide),
        ],
        compiler_params=pltpu.CompilerParams(vmem_limit_bytes=VMEM_BYTES),
        cost_estimate=pl.CostEstimate(
            flops=20 * rows * rows * LANES, bytes_accessed=6 << 20, transcendentals=rows * rows
        ),
        name="attend_back",
    )(lengths, query, keys, values, grad, full, lse, cosine, sine)


def feed_kernel(order, which, *refs):
    given, (x_own, x_other, c_own, c_other) = refs[:-17], refs[-17:-13]
    outs, grads, dgate_ref, ddown_ref = refs[-13:-11], refs[-11:-9], refs[-9], refs[-8]
    weights, x_ref, c_ref, inner_s, mlp_s, weight_sems, row_sems = refs[-7:]
    step = pl.program_id(0)
    parts, depth3, depth = weights.shape
    pieces = len(given) // parts
    width = depth // pieces
    units = depth3 // 3
    rows = x_own.shape[0]
    skipped = given[0].shape[0] - depth3
    chunk = min(512, rows)
    sides = (slice(0, rows), slice(rows, 2 * rows))
    fetches = [
        [
            pltpu.make_async_copy(
                given[number * pieces + c].at[skipped:, :],
                weights.at[number, :, pl.ds(pl.multiple_of(which[c] * width, LANES), width)],
                weight_sems.at[number, c],
            )
            for c in range(pieces)
        ]
        for number in range(parts)
    ]
    loads = [
        pltpu.make_async_copy(source, target.at[side, :], row_sems.at[number])
        for number, (source, target, side) in enumerate(
            zip((x_own, x_other, c_own, c_other), (x_ref, x_ref, c_ref, c_ref), sides * 2)
        )
    ]

    @pl.when(step == 0)
    def _():
        for fetch in fetches[0]:
            fetch.start()
        for load in loads:
            load.start()
        for fetch in sum(fetches[1:], []):
            fetch.start()
        for ref in (*outs, *grads):
            ref[...] = jnp.zeros_like(ref)
        for load in loads:
            load.wait()

    for number in range(parts):

        @pl.when(step == number)
        def _(number=number):
            for fetch in fetches[number]:
                fetch.wait()

    w_ref = weights.at[step]
    for half, (out_ref, grad_ref) in enumerate(zip(outs, grads)):

        @pl.loop(0, rows // chunk)
        def _(t, half=half, out_ref=out_ref, grad_ref=grad_ref):
            at = pl.ds(pl.multiple_of(t * chunk, chunk), chunk)
            along = pl.ds(pl.multiple_of(half * rows + t * chunk, chunk), chunk)
            gated = dot_nt(w_ref[: 2 * units, :], x_ref[along, :])
            inner_grad = dot_nt(w_ref[2 * units :, :], c_ref[along, :])
            gate, up = gated[:units], gated[units:]
            sigmoid = jax.nn.sigmoid(gate)
            silu = gate * sigmoid
            inner = (silu * up).astype(low)
            gate_grad = (inner_grad * up * sigmoid * (1.0 + gate * (1.0 - sigmoid))).astype(low)
            up_grad = (inner_grad * silu).astype(low)
            inner_s[:, along] = inner
            mlp_s[:units, along] = gate_grad
            mlp_s[units:, along] = up_grad
            mlp_grad = jnp.concatenate([gate_grad, up_grad], axis=0)
            out_ref[at, :] += dot_tn(inner, w_ref[2 * units :, :])
            grad_ref[at, :] += dot_tn(mlp_grad, w_ref[: 2 * units, :])

    for c in range(pieces):
        cols = slice(c * width, (c + 1) * width)
        dgate_ref[c, 0, skipped:, :] = dot_nn(mlp_s[...], x_ref[:, cols]).astype(low)
        ddown_ref[c, 0] = dot_nn(inner_s[...], c_ref[:, cols]).astype(low)


def feed(order, which, slots, units, x_own, x_other, c_own, c_other):
    rows, depth = x_own.shape
    parts, pieces, width = len(slots), len(slots[0]), slots[0][0].shape[1]
    gates = slots[0][0].shape[0] - units
    anywhere = pl.BlockSpec(memory_space=pl.ANY)
    activations = pl.BlockSpec((rows, depth), lambda h, o, c: (0, 0), pipeline_mode=pl.Buffered(1))
    block = lambda height: pl.BlockSpec((pieces, 1, height, width), lambda h, o, c: (0, o[h], 0, 0))
    spec = pltpu.PrefetchScalarGridSpec(
        num_scalar_prefetch=2,
        grid=(parts,),
        in_specs=[anywhere] * (parts * pieces + 4),
        out_specs=[activations] * 4 + [block(gates), block(units)],
        scratch_shapes=[
            pltpu.VMEM((parts, 3 * units, depth), low),
            pltpu.VMEM((2 * rows, depth), low),
            pltpu.VMEM((2 * rows, depth), low),
            pltpu.VMEM((units, 2 * rows), low),
            pltpu.VMEM((2 * units, 2 * rows), low),
            pltpu.SemaphoreType.DMA((parts, pieces)),
            pltpu.SemaphoreType.DMA((4,)),
        ],
    )
    return pl.pallas_call(
        feed_kernel,
        grid_spec=spec,
        out_shape=[jax.ShapeDtypeStruct((rows, depth), wide)] * 4
        + [
            jax.ShapeDtypeStruct((pieces, parts, gates, width), low),
            jax.ShapeDtypeStruct((pieces, parts, units, width), low),
        ],
        compiler_params=pltpu.CompilerParams(vmem_limit_bytes=VMEM_BYTES),
        cost_estimate=pl.CostEstimate(
            flops=36 * rows * depth * units * parts,
            bytes_accessed=30 << 20,
            transcendentals=2 * rows * units * parts,
        ),
        name="feed",
    )(order, which, *sum(slots, []), x_own, x_other, c_own, c_other)


def collect_kernel(order, which, *refs):
    out_ref = refs[-1]
    height, width = refs[0].shape
    pieces = out_ref.shape[1] // width
    for number, ref in enumerate(refs[:-1]):
        part, piece = divmod(number, pieces)
        rows = pl.ds(pl.multiple_of(order[part] * height, height), height)
        out_ref[rows, pl.ds(pl.multiple_of(which[piece] * width, LANES), width)] = ref[...]


def collect(order, which, slots, height):
    parts, pieces, width = len(slots), len(slots[0]), slots[0][0].shape[1]
    spec = pltpu.PrefetchScalarGridSpec(
        num_scalar_prefetch=2,
        grid=(1,),
        in_specs=[pl.BlockSpec((height, width), lambda i, o, c: (0, 0))] * (parts * pieces),
        out_specs=pl.BlockSpec((parts * height, pieces * width), lambda i, o, c: (0, 0)),
    )
    return pl.pallas_call(
        collect_kernel,
        grid_spec=spec,
        out_shape=jax.ShapeDtypeStruct((parts * height, pieces * width), low),
        compiler_params=pltpu.CompilerParams(vmem_limit_bytes=VMEM_BYTES),
        cost_estimate=pl.CostEstimate(flops=0, bytes_accessed=2 << 20, transcendentals=0),
        name="collect",
    )(order, which, *sum(slots, []))


def line_up_kernel(order, *refs):
    out_ref = refs[-1]
    height, width = refs[0].shape
    pairs = out_ref.shape[0] // height // (len(refs) - 1)
    each = width // pairs
    for number, ref in enumerate(refs[:-1]):
        for pair in range(pairs):
            start = (order[number] * pairs + pair) * height
            rows = pl.ds(pl.multiple_of(start, height), height)
            out_ref[rows, :] = ref[:, pair * each : (pair + 1) * each]


def line_up(order, arrived, pairs):
    height, width = arrived[0].shape
    shape = (len(arrived) * pairs * height, width // pairs)
    spec = pltpu.PrefetchScalarGridSpec(
        num_scalar_prefetch=1,
        grid=(1,),
        in_specs=[pl.BlockSpec((height, width), lambda i, o: (0, 0))] * len(arrived),
        out_specs=pl.BlockSpec(shape, lambda i, o: (0, 0)),
    )
    return pl.pallas_call(
        line_up_kernel,
        grid_spec=spec,
        out_shape=jax.ShapeDtypeStruct(shape, low),
        compiler_params=pltpu.CompilerParams(vmem_limit_bytes=VMEM_BYTES),
        cost_estimate=pl.CostEstimate(flops=0, bytes_accessed=2 << 20, transcendentals=0),
        name="line_up",
    )(order, *arrived)


def unproject_kernel(normed_ref, *refs):
    mixed_refs, (dw_ref, acc_ref) = refs[:-2], refs[-2:]
    step = pl.program_id(0)

    @pl.when(step == 0)
    def _():
        acc_ref[...] = jnp.zeros_like(acc_ref)

    height = mixed_refs[0].shape[1]
    for number, ref in enumerate(mixed_refs):
        acc_ref[number * height : (number + 1) * height, :] += dot_tn(ref[...], normed_ref[...])

    @pl.when(step == pl.num_programs(0) - 1)
    def _():
        dw_ref[...] = acc_ref[...].astype(low)


def unproject(normed, mixed_grads):
    tokens, depth = normed.shape
    rows = 512
    height = mixed_grads[0].shape[1]
    total = height * len(mixed_grads)
    block = lambda width: pl.BlockSpec((rows, width), lambda o: (o, 0))
    return pl.pallas_call(
        unproject_kernel,
        grid=(tokens // rows,),
        in_specs=[block(depth)] + [block(height)] * len(mixed_grads),
        out_specs=pl.BlockSpec((total, depth), lambda o: (0, 0)),
        scratch_shapes=[pltpu.VMEM((total, depth), wide)],
        out_shape=jax.ShapeDtypeStruct((total, depth), low),
        compiler_params=pltpu.CompilerParams(vmem_limit_bytes=VMEM_BYTES),
        cost_estimate=pl.CostEstimate(
            flops=2 * tokens * depth * total, bytes_accessed=9 << 20, transcendentals=0
        ),
        name="unproject",
    )(normed, *mixed_grads)


def arrival_order(place):
    ways = jnp.where(place < 2, 1, -1)
    far = jnp.where(place % 2 == 0, 3, 0)
    return jnp.stack([place, place + ways, place + 2 * ways, far]).astype(jnp.int32)


def gather_all(tokens, weights, end, place, chips, use, then):
    near = place < 2
    rows, depth = tokens.shape
    width = weights.shape[1]
    cut = rows * depth // width

    def hop(ends):
        return (
            lax.ppermute(ends[0], "head", [(0, 1), (1, 2), (2, 3)]),
            lax.ppermute(ends[1], "head", [(1, 0), (2, 1), (3, 2)]),
        )

    def nearest(hops):
        return jnp.where(near, hops[-1][1], hops[-1][0])

    def farthest(hops):
        return jnp.where(
            place % 3 == 0, nearest(hops), jnp.where(near, hops[0][0], hops[0][1])
        )

    def in_blocks(tokens):
        return jnp.moveaxis(tokens.reshape(rows, -1, width), 1, 0).reshape(cut, width)

    def plane(slot):
        if chips != 4:
            return [lax.all_gather(slot[:end], "chip", axis=1, tiled=True)]
        return [slot[:end]] + [
            lax.ppermute(slot[:end], "chip", [(c, c ^ away) for c in range(chips)])
            for away in range(1, chips)
        ]

    barrier = lax.optimization_barrier
    slots, planes = [weights], []
    token_hops, weight_hops = [], []
    ends = barrier(hop((tokens, tokens)))
    first_block = nearest([ends])
    token_hops.append(tuple(in_blocks(end) for end in ends))

    ends = hop(tuple(jnp.concatenate([end, weights]) for end in token_hops[0]))
    planes.append(plane(weights))
    used = use(0, tokens, None)
    ends, planes, used = barrier((ends, planes, used))
    token_hops.append(tuple(end[:cut] for end in ends))
    weight_hops.append(tuple(end[cut:] for end in ends))
    slots.append(nearest(weight_hops))
    second_block = nearest(token_hops)

    ends = hop(ends)
    planes.append(plane(slots[1]))
    used = use(1, first_block, used)
    used = use(2, second_block, used)
    ends, planes, used = barrier((ends, planes, used))
    token_hops.append(tuple(end[:cut] for end in ends))
    weight_hops.append(tuple(end[cut:] for end in ends))
    slots.append(nearest(weight_hops))
    used = use(3, farthest(token_hops), used)

    ends = hop(weight_hops[-1])
    planes.append(plane(slots[2]))
    made, used = then(0, used)
    ends, planes, made, used = barrier((ends, planes, made, used))
    weight_hops.append(ends)
    slots.append(farthest(weight_hops))
    planes.append(plane(slots[3]))
    more, used = then(1, used)
    planes, more = barrier((planes, more))
    return planes, [slot[end:] for slot in slots], used, [made, more]


def exchange(pieces):
    return lax.all_to_all(pieces, "head", split_axis=0, concat_axis=0)


def exchange_turned(pieces, place):
    count = pieces.shape[0]
    came = []
    for j in range(count):
        piece = lax.dynamic_index_in_dim(pieces, (place + j) % count, 0, keepdims=False)
        came.append(
            lax.ppermute(piece, "head", [(k, (k + j) % count) for k in range(count)]) if j else piece
        )
    return came


def to_line(piece, count):
    return exchange(jnp.broadcast_to(piece[None], (count, *piece.shape)))


def other_core(array):
    return lax.ppermute(array, "core", [(0, 1), (1, 0)])


def by_core(core, own, came, axis):
    first = jnp.where(core == 0, own, came)
    second = jnp.where(core == 0, came, own)
    return jnp.concatenate([first, second], axis=axis)


def shards(
    tokens, first_values, mixer_in, mixer_out, gate_up, down_weight, norm_gains, lengths, cotangent
):
    line = lax.axis_size("head")
    chips = lax.axis_size("chip")
    place = lax.axis_index("head")
    core = lax.axis_index("core")
    rows, depth = tokens.shape
    cols = mixer_in.shape[2]
    width = mixer_in.shape[1]
    units = down_weight.shape[0] // 2
    pairs = cols // LANES
    after = lax.optimization_barrier

    def halves(array, axis):
        first, second = jnp.split(array, 2, axis=axis)
        return jnp.where(core == 0, first, second), jnp.where(core == 0, second, first)

    def chip_scatter(grad):
        grad = grad.reshape(*grad.shape[:-1], chips, 2 * width)
        return lax.psum_scatter(jnp.moveaxis(grad, -2, 0), "chip", scatter_dimension=0)

    def before(given, *results):
        return after((given, *results))[0]

    qkv_low = mixer_in.astype(low)
    gain_low = norm_gains.astype(low)
    gain_rows = jnp.pad(gain_low, ((0, GAIN_ROWS - 2), (0, 0)))
    qkv_rows = qkv_low.reshape(3, width, pairs, LANES).transpose(2, 0, 3, 1)
    qkv_rows = qkv_rows.reshape(3 * cols, width)
    pack = lax.all_gather(
        jnp.concatenate([qkv_rows, gain_rows], axis=0), ("chip", "core"), axis=1, tiled=True
    )
    gain_first = pack[3 * cols].astype(wide)
    gain_second = pack[3 * cols + 1].astype(wide)

    gates_low = gate_up.astype(low)
    feed_rows = jnp.concatenate(
        [gates_low.transpose(0, 2, 1), down_weight.astype(low)[None]], axis=0
    ).reshape(3, 2, units, width)
    out_low = mixer_out.astype(low).reshape(2, cols // 2, width)

    def half_rows(which):
        return jnp.concatenate([out_low[which], feed_rows[:, which].reshape(3 * units, width)])

    first_rows, second_rows = half_rows(0), half_rows(1)
    own_rows = jnp.where(core == 0, first_rows, second_rows)
    other_rows = jnp.where(core == 0, second_rows, first_rows)
    own_rows = by_core(core, own_rows, other_core(other_rows), -1)
    end = own_rows.shape[0]
    qkv_sides = jnp.concatenate(jnp.split(qkv_rows, pairs), axis=-1)
    weights = jnp.concatenate([own_rows, qkv_sides])

    order = arrival_order(place)
    place_one = place[None].astype(jnp.int32)
    chip = lax.axis_index("chip")
    which = (chip ^ jnp.arange(4) if chips == 4 else jnp.zeros(1)).astype(jnp.int32)
    cosine, sine = rope_tables()

    def use(number, x, made):
        index = order[number : number + 1]
        return project(index, x, pack, first_values, cosine, sine, made or [])

    def then(pair, made):
        return attend(pair, lengths, *made[:3]), made

    planes, qkv_line, made, attended_parts = gather_all(
        tokens, weights, end, place, chips, use, then
    )
    query, keys, values, normed_a = made
    cot_other = other_core(cotangent)
    out_half = collect(order, which, planes, cols // 2).reshape(line, 1, cols // 2, depth)
    out_heads = by_core(core, out_half, other_core(out_half), 1)
    out_full = out_heads.reshape(depth, depth)
    lined = chips == 4
    attended_pieces = [exchange(part[0].reshape(line, rows, LANES)) for part in attended_parts]
    attended_wide = [part[1] for part in attended_parts]
    log_total = [part[2] for part in attended_parts]
    attended = jnp.stack(attended_pieces, axis=1).transpose(2, 0, 1, 3).reshape(rows, depth)

    qkv_line = line_up(order, qkv_line, pairs)
    qkv_full = lax.all_gather(qkv_line, ("chip", "core"), axis=1, tiled=True)
    qkv_full = qkv_full.reshape(line, pairs, 3 * LANES, depth)

    token_rows = tokens.astype(wide)
    hidden_state = token_rows + dot_nn(attended, out_full)
    normed_b, unit_b, factor_b = rms_parts(hidden_state, gain_second)
    normed_b = before(normed_b.astype(low), qkv_full)
    branch_own, branch_other, grad_own, grad_other, gate_grad, down_grad = feed(
        order, which, planes, units, normed_b, other_core(normed_b), cotangent, cot_other
    )
    normed_b_grad = grad_own + other_core(grad_other)
    branch_b = branch_own + other_core(branch_other)
    block_out = (hidden_state + branch_b).astype(low)

    state_part = rms_back(normed_b_grad, unit_b, factor_b, gain_second)
    state_grad = cotangent.astype(wide) + state_part
    branch_grad = state_grad.astype(low)

    def spread(grad):
        if not lined:
            grad = grad.reshape(line, -1, chips, 2 * width).transpose(2, 0, 1, 3)
        return grad

    down_sum = lax.psum_scatter(spread(down_grad), "chip", scatter_dimension=0)
    positions = place * rows + jnp.arange(rows)
    valid = (positions < lengths[0]).astype(wide)[None, :, None]
    outs = out_full.reshape(line, pairs, LANES, depth)
    asked = [
        (valid * jnp.einsum("td,zcd->ztc", branch_grad, outs[:, pair], preferred_element_type=wide)).astype(low)
        for pair in range(pairs)
    ]

    def back(pair, came):
        return attend_back(
            pair, lengths, query, keys, values, came.reshape(line * rows, LANES),
            attended_wide[pair], log_total[pair], cosine, sine,
        )

    came = exchange(asked[0])
    out_grad = dot_tn(attended, branch_grad).astype(low).reshape(line, cols, depth)
    kept, given = halves(out_grad, 1)
    out_grad = (kept.astype(wide) + other_core(given).astype(wide)).astype(low)
    out_grad = jnp.moveaxis(out_grad.reshape(line, cols // 2, chips, 2 * width), 2, 0)
    gate_grad = spread(gate_grad).at[:, :, : cols // 2].set(out_grad)
    came, gate_grad, asked, down_sum = after((came, gate_grad, asked, down_sum))

    gate_sum = lax.psum_scatter(gate_grad, "chip", scatter_dimension=0)
    mixed_first = back(0, came)
    came = exchange(asked[1])
    down_came = exchange_turned(down_sum, place)
    came, mixed_first, down_came = after((came, mixed_first, down_came))

    mixed_second = back(1, came)
    mixed_rows = exchange(mixed_first[0].reshape(line, rows, 3 * LANES))
    mixed_rows, mixed_second, gate_sum = after((mixed_rows, mixed_second, gate_sum))

    came = exchange(mixed_second[0].reshape(line, rows, 3 * LANES))
    gate_came = exchange_turned(gate_sum, place)
    qkv_grad = unproject(normed_a, [mixed_first[0], mixed_second[0]])
    kept, given = halves(qkv_grad, 0)
    qkv_grad = (kept.astype(wide) + other_core(given).astype(wide)).astype(low)
    qkv_sum = chip_scatter(qkv_grad)
    normed_a_grad = jnp.einsum(
        "ztc,zcd->td", mixed_rows, qkv_full[:, 0], preferred_element_type=wide
    )
    normed_a_grad, came, gate_came, qkv_sum = after((normed_a_grad, came, gate_came, qkv_sum))
    normed_a_grad += jnp.einsum("ztc,zcd->td", came, qkv_full[:, 1], preferred_element_type=wide)
    first_grad = jnp.concatenate([mixed_first[1], mixed_second[1]], axis=1)

    def settle(grad):
        kept, given = halves(grad, -1)
        return by_core(core, kept[..., None, :, :], other_core(given)[..., None, :, :], -3)

    gate_sum = sum(piece.astype(wide) for piece in gate_came)
    down_sum = sum(piece.astype(wide) for piece in down_came)
    mixer_out_grad = settle(gate_sum[: cols // 2]).reshape(cols, width)
    gate_sum = settle(gate_sum[cols // 2 :].reshape(2, units, 2 * width)).reshape(2, 2 * units, width)
    down_grad = settle(down_sum).reshape(2 * units, width)
    qkv_sum = settle(qkv_sum.astype(wide)).reshape(pairs, 3, LANES, width)
    gate_up_grad = gate_sum.transpose(0, 2, 1)
    mixer_in_grad = qkv_sum.transpose(1, 3, 0, 2).reshape(3, width, cols)

    _, unit_a, factor_a = rms_parts(token_rows, gain_first)
    tokens_grad = state_grad + rms_back(normed_a_grad, unit_a, factor_a, gain_first)

    gain_wide = gain_low.astype(wide)
    gain_parts = jnp.stack(
        [
            jnp.sum(qkv_low.astype(wide) * mixer_in_grad, axis=(0, 2)),
            jnp.sum(gates_low.astype(wide) * gate_up_grad, axis=(0, 2)),
        ]
    )
    gains_grad = jnp.sum(to_line(gain_parts / gain_wide, line), axis=0)
    return (
        block_out,
        tokens_grad,
        first_grad,
        mixer_in_grad,
        mixer_out_grad,
        gate_up_grad,
        down_grad,
        gains_grad,
    )


def solution(mesh):
    groups, line = mesh.shape["dp"], mesh.shape["head"]
    fine = jax.sharding.Mesh(
        mesh.devices.reshape(groups // 2, 2, line), ("chip", "core", "head")
    )
    dp = ("chip", "core")
    return jax.shard_map(
        shards,
        mesh=fine,
        in_specs=(
            P(("chip", "core", "head"), None),
            P(dp, "head"),
            P(None, dp, "head"),
            P("head", dp),
            P(None, dp, "head"),
            P("head", dp),
            P(None, dp),
            P(dp),
            P(("chip", "core", "head"), None),
        ),
        out_specs=(
            P(("chip", "core", "head"), None),
            P(("chip", "core", "head"), None),
            P(dp, "head"),
            P(None, dp, "head"),
            P("head", dp),
            P(None, dp, "head"),
            P("head", dp),
            P(None, dp),
        ),
        check_vma=False,
    )
```

profile of v0, /device:TPU:0, one launch (start us, length us, event | category | flops | bytes accessed | tf_op | source)
XLA Modules:
  0.0 516.6 jit_solution(1265703597832059225)
XLA Ops:
  7.2 5.1 collective-permute-start
  22.3 12.7 %collective-permute-done = bf16[512,1024]{1,0:T(8,128)(2,1)S(1)} collective-permute-done((bf16[512,1024]{1,0:T(8,128)(2,1)}, bf16[512,1024]{1,0:T(8,128)(2,1)S(1)}, u32[]{:S(2)}, u32[]{:S(2)}) %collective-permute-start) | collective-permute-done | bytes 1048608 | tf_op jit(solution)/shard_map/ppermute | solution.py:553
  35.0 4.1 collective-permute-done.1
  41.5 8.5 %fusion.14 = (bf16[3616,256]{1,0:T(8,128)(2,1)}, bf16[3616,256]{1,0:T(8,128)(2,1)}) fusion(bf16[384,128]{1,0:T(8,128)(2,1)S(1)} %bitcast.189, bf16[384,128]{1,0:T(8,128)(2,1)S(1)} %bitcast.187, bf16[2048,256]{1,0:T(8,128)(2,1)S(1)} %bitcast.159, bf16[1184,128]{1,0:T(8,128)(2,1)S(1)} %get-tuple-element.282, bf16[1184,128]{1,0:T(8,128)(2,1)S(1)} %get-tuple-element.281, ...), kind=kLoop, calls=%fused_computation.30 | loop fusion | flops 12959744 | bytes 6602752 | tf_op jit(solution)/shard_map/concatenate | solution.py:583
  50.0 4.8 collective-permute-start.3
  60.5 4.8 fusion.30
  65.3 6.2 %pad_maximum_fusion.3 = (f32[2048,128]{1,0:T(8,128)}, f32[2048,128]{1,0:T(8,128)}) fusion(f32[2048,32]{1,0:T(8,128)} %get-tuple-element.301, f32[2048,32]{1,0:T(8,128)} %get-tuple-element.300, f32[2048,32]{1,0:T(8,128)S(1)} %get-tuple-element.299), kind=kLoop, calls=%fused_computation.43 | loop fusion | flops 1572864 | bytes 2883584 | tf_op jit(solution)/shard_map/concatenate | solution.py:42
  71.5 4.6 project.4
  76.1 9.2 %collective-permute-done.6.refs_2_ = bf16[1184,256]{1,0:T(8,128)(2,1)} collective-permute-done((bf16[1184,256]{1,0:T(8,128)(2,1)}, bf16[1184,256]{1,0:T(8,128)(2,1)}, u32[]{:S(2)}, u32[]{:S(2)}) %collective-permute-start.6) | collective-permute-done | bytes 606240 | tf_op jit(solution)/shard_map/ppermute | solution.py:572
  85.3 6.8 %collective-permute-done.3 = bf16[3616,256]{1,0:T(8,128)(2,1)} collective-permute-done((bf16[3616,256]{1,0:T(8,128)(2,1)}, bf16[3616,256]{1,0:T(8,128)(2,1)}, u32[]{:S(2)}, u32[]{:S(2)}) %collective-permute-start.3) | collective-permute-done | bytes 1851424 | tf_op jit(solution)/shard_map/ppermute | solution.py:553
  92.1 5.4 %collective-permute-done.4 = bf16[3616,256]{1,0:T(8,128)(2,1)} collective-permute-done((bf16[3616,256]{1,0:T(8,128)(2,1)}, bf16[3616,256]{1,0:T(8,128)(2,1)}, u32[]{:S(2)}, u32[]{:S(2)}) %collective-permute-start.4) | collective-permute-done | bytes 1851424 | tf_op jit(solution)/shard_map/ppermute | solution.py:554
  97.5 3.5 collective-permute-start.8
  104.7 2.3 broadcast_select_fusion.3.x_ref
  112.1 4.5 project.5
  117.3 2.6 slice_select_fusion.x_ref
  119.9 4.5 project.6
  125.3 10.1 %collective-permute-done.11.refs_6_ = bf16[1184,256]{1,0:T(8,128)(2,1)} collective-permute-done((bf16[1184,256]{1,0:T(8,128)(2,1)S(1)}, bf16[1184,256]{1,0:T(8,128)(2,1)}, u32[]{:S(2)}, u32[]{:S(2)}) %collective-permute-start.11) | collective-permute-done | bytes 606240 | tf_op jit(solution)/shard_map/ppermute | solution.py:572
  137.0 5.4 %collective-permute-done.9 = bf16[3616,256]{1,0:T(8,128)(2,1)} collective-permute-done((bf16[3616,256]{1,0:T(8,128)(2,1)}, bf16[3616,256]{1,0:T(8,128)(2,1)}, u32[]{:S(2)}, u32[]{:S(2)}) %collective-permute-start.9) | collective-permute-done | bytes 1851424 | tf_op jit(solution)/shard_map/ppermute | solution.py:554
  142.4 2.4 broadcast_select_fusion.4
  148.4 2.3 collective-permute-start.13
  152.1 2.7 select_select_fusion.x_ref
  155.4 4.5 project.7
  159.9 12.1 %attend.2 = (bf16[2048,128]{1,0:T(8,128)(2,1)}, f32[2048,128]{1,0:T(8,128)}, f32[8,2048]{1,0:T(8,128)}) custom-call(s32[1]{0:T(128)} %copy.149.len_ref, bf16[2048,256]{1,0:T(8,128)(2,1)} %get-tuple-element.201.q_ref, bf16[2048,256]{1,0:T(8,128)(2,1)} %get-tuple-element.202.k_ref, bf16[2048,256]{1,0:T(8,128)(2,1)} %get-tuple-element.203.v_ref), custom_call_target="tpu_custom_call" | custom-call | flops 4294967296 | bytes 4194304 | tf_op jit(solution)/shard_map/attend/pallas_call | solution.py:199
  174.5 2.9 line_up.1
  181.6 3.9 all-to-all-start
  185.5 12.1 %attend.3 = (bf16[2048,128]{1,0:T(8,128)(2,1)}, f32[2048,128]{1,0:T(8,128)}, f32[8,2048]{1,0:T(8,128)}) custom-call(s32[1]{0:T(128)} %copy.149.len_ref, bf16[2048,256]{1,0:T(8,128)(2,1)} %get-tuple-element.201.q_ref, bf16[2048,256]{1,0:T(8,128)(2,1)} %get-tuple-element.202.k_ref, bf16[2048,256]{1,0:T(8,128)(2,1)} %get-tuple-element.203.v_ref), custom_call_target="tpu_custom_call" | custom-call | flops 4294967296 | bytes 4194304 | tf_op jit(solution)/shard_map/attend/pallas_call | solution.py:199
  197.6 2.6 collective-permute-done.18.refs_13_
  200.2 9.7 %collective-permute-done.19.refs_14_ = bf16[1184,256]{1,0:T(8,128)(2,1)S(1)} collective-permute-done((bf16[1184,256]{1,0:T(8,128)(2,1)S(1)}, bf16[1184,256]{1,0:T(8,128)(2,1)S(1)}, u32[]{:S(2)}, u32[]{:S(2)}) %collective-permute-start.19) | collective-permute-done | bytes 606240 | tf_op jit(solution)/shard_map/ppermute | solution.py:572
  211.5 3.0 collect.1
  214.5 3.7 all-to-all-start.1
  219.4 3.1 broadcast_select_fusion.2
  222.5 10.9 %all-to-all-done.1 = bf16[4,512,128]{2,1,0:T(8,128)(2,1)S(1)} async-done(((bf16[4,512,128]{2,1,0:T(8,128)(2,1)}), bf16[4,512,128]{2,1,0:T(8,128)(2,1)S(1)}, u32[]{:S(2)}, u32[]{:S(2)}) %all-to-all-start.1) | async-done | bytes 524320 | tf_op jit(solution)/shard_map/all_to_all | solution.py:615
  234.2 3.6 multiply_reduce_fusion.1
  238.2 2.8 collective-permute-done.22.refs_17_
  240.9 38.5 %feed.1 = (f32[512,1024]{1,0:T(8,128)}, f32[512,1024]{1,0:T(8,128)}, f32[512,1024]{1,0:T(8,128)}, f32[512,1024]{1,0:T(8,128)}, bf16[4,4,832,256]{3,2,1,0:T(8,128)(2,1)}, /*index=5*/bf16[4,4,352,256]{3,2,1,0:T(8,128)(2,1)}) custom-call(s32[4]{0:T(128)} %pad_add_fusion.order, s32[4]{0:T(128)} %iota_xor_fusion.which, ...), custom_call_target="tpu_custom_call" | custom-call | flops 26575110144 | bytes 31457280 | tf_op jit(solution)/shard_map/feed/pallas_call | solution.py:424
  284.1 3.3 multiply_reduce_fusion
  288.0 5.0 multiply_add_fusion
  297.4 2.3 copy.124
  299.6 2.3 broadcast_select_fusion
  302.0 2.8 fusion.22
  304.7 4.1 all-to-all-start.2
  309.2 3.2 fusion.21
  312.3 2.6 add_convert_fusion
  317.6 6.8 %all-to-all-done.2 = bf16[4,512,128]{1,2,0:T(8,128)(2,1)} async-done(((bf16[4,512,128]{1,2,0:T(8,128)(2,1)}), bf16[4,512,128]{1,2,0:T(8,128)(2,1)}, u32[]{:S(2)}, u32[]{:S(2)}) %all-to-all-start.2) | async-done | bytes 524320 | tf_op jit(solution)/shard_map/all_to_all | solution.py:615
  324.4 2.1 copy.113
  327.3 2.0 collective-permute-start.28
  329.3 1.8 collective-permute-start.29
  331.1 3.5 all-to-all-start.3
  334.6 21.1 %attend_back.2 = (bf16[2048,384]{1,0:T(8,128)(2,1)}, f32[2048,128]{1,0:T(8,128)}) custom-call(s32[1]{0:T(128)} %copy.149.len_ref, bf16[2048,256]{1,0:T(8,128)(2,1)} %get-tuple-element.201.q_ref, bf16[2048,256]{1,0:T(8,128)(2,1)} %get-tuple-element.202.k_ref, bf16[2048,256]{1,0:T(8,128)(2,1)} %get-tuple-element.203.v_ref, bf16[2048,128]{1,0:T(8,128)(2,1)} %bitcast.196, ...), custom_call_target="tpu_custom_call" | custom-call | flops 10737418240 | bytes 6291456 | tf_op jit(solution)/shard_map/attend_back/pallas_call | solution.py:308
  357.2 4.3 all-to-all-start.4
  362.6 21.1 %attend_back.3 = (bf16[2048,384]{1,0:T(8,128)(2,1)}, f32[2048,128]{1,0:T(8,128)}) custom-call(s32[1]{0:T(128)} %copy.149.len_ref, bf16[2048,256]{1,0:T(8,128)(2,1)} %get-tuple-element.201.q_ref, bf16[2048,256]{1,0:T(8,128)(2,1)} %get-tuple-element.202.k_ref, bf16[2048,256]{1,0:T(8,128)(2,1)} %get-tuple-element.203.v_ref, bf16[2048,128]{1,0:T(8,128)(2,1)} %bitcast.197, ...), custom_call_target="tpu_custom_call" | custom-call | flops 10737418240 | bytes 6291456 | tf_op jit(solution)/shard_map/attend_back/pallas_call | solution.py:308
  383.7 14.3 %all-to-all-done.4 = bf16[4,512,384]{2,1,0:T(8,128)(2,1)} async-done(((bf16[4,512,384]{2,1,0:T(8,128)(2,1)}), bf16[4,512,384]{2,1,0:T(8,128)(2,1)}, u32[]{:S(2)}, u32[]{:S(2)}) %all-to-all-start.4) | async-done | bytes 1572896 | tf_op jit(solution)/shard_map/all_to_all | solution.py:615
  398.4 7.5 %unproject.1 = bf16[768,1024]{1,0:T(8,128)(2,1)} custom-call(bf16[2048,1024]{1,0:T(8,128)(2,1)} %get-tuple-element.248.normed_ref, bf16[2048,384]{1,0:T(8,128)(2,1)} %get-tuple-element.238.refs_0_, bf16[2048,384]{1,0:T(8,128)(2,1)} %get-tuple-element.246.refs_1_), custom_call_target="tpu_custom_call" | custom-call | flops 3221225472 | bytes 9437184 | tf_op jit(solution)/shard_map/unproject/pallas_call | solution.py:524
  406.0 2.3 broadcast_select_fusion.6
  408.3 4.8 all-to-all-start.5
  420.8 2.0 collective-permute-start.30
  422.8 2.4 collective-permute-start.31
  428.1 5.7 %fusion.18 = f32[512,1024]{1,0:T(8,128)} fusion(bf16[4,512,384]{2,1,0:T(8,128)(2,1)} %all-to-all-done.4, bf16[4,2,384,1024]{3,2,1,0:T(8,128)(2,1)} %bitcast.208), kind=kOutput, calls=%fused_computation.33 | convolution fusion | flops 1610612736 | bytes 6815744 | tf_op jit(solution)/shard_map/ztc,zcd->td/dot_general | solution.py:786
  433.7 19.5 %collective-permute-done.30 = bf16[832,256]{1,0:T(8,128)(2,1)} collective-permute-done((bf16[832,256]{1,0:T(8,128)(2,1)S(1)}, bf16[832,256]{1,0:T(8,128)(2,1)}, u32[]{:S(2)}, u32[]{:S(2)}) %collective-permute-start.30) | collective-permute-done | bytes 426016 | tf_op jit(solution)/shard_map/ppermute | solution.py:624
  453.3 25.6 %collective-permute-done.31 = bf16[832,256]{1,0:T(8,128)(2,1)} collective-permute-done((bf16[832,256]{1,0:T(8,128)(2,1)S(1)}, bf16[832,256]{1,0:T(8,128)(2,1)}, u32[]{:S(2)}, u32[]{:S(2)}) %collective-permute-start.31) | collective-permute-done | bytes 426016 | tf_op jit(solution)/shard_map/ppermute | solution.py:624
  483.0 4.4 fusion.4
  487.4 2.0 fusion.7
  492.5 11.0 %all-to-all-start.6 = ((f32[4,2,128]{2,1,0:T(2,128)}), f32[4,2,128]{2,1,0:T(2,128)S(1)}, u32[]{:S(2)}, u32[]{:S(2)}) async-start(f32[4,2,128]{2,1,0:T(2,128)} %broadcast_in_dim.2), calls=%async_computation.6 | async-start | bytes 8192 | tf_op jit(solution)/shard_map/all_to_all | solution.py:615
  504.2 4.9 all-to-all-done.6
  (219 shorter events, 80.4 us)
Async XLA Ops:
  7.2 12.1 %copy-start.21 = (f32[3,128,256]{2,1,0:T(8,128)S(1)}, f32[3,128,256]{2,1,0:T(8,128)}, u32[]{:S(2)}) copy-start(f32[3,128,256]{2,1,0:T(8,128)} %param.13) | copy-start | bytes 1179652
  7.2 64.3 %all-gather.3.cloned.1.call-start = ((), (), s32[]{:S(2)}) async-start(), calls=%async_computation.10 | async-start | bytes 1806336 | tf_op jit(solution)/shard_map/all_gather | solution.py:673
  7.2 27.8 %collective-permute-start = (bf16[512,1024]{1,0:T(8,128)(2,1)}, bf16[512,1024]{1,0:T(8,128)(2,1)S(1)}, u32[]{:S(2)}, u32[]{:S(2)}) collective-permute-start(bf16[512,1024]{1,0:T(8,128)(2,1)} %x_ref.1), channel_id=1, source_target_pairs={{0,1},{1,2},{2,3},{4,5},{5,6},{6,7},{8,9},{9,10},{10,11},{12,13},{... | collective-permute-start | bytes 3145736 | tf_op jit(solution)/shard_map/ppermute | solution.py:553
  12.4 26.7 %collective-permute-start.1 = (bf16[512,1024]{1,0:T(8,128)(2,1)}, bf16[512,1024]{1,0:T(8,128)(2,1)S(1)}, u32[]{:S(2)}, u32[]{:S(2)}) collective-permute-start(bf16[512,1024]{1,0:T(8,128)(2,1)} %x_ref.1), channel_id=1, source_target_pairs={{1,0},{2,1},{3,2},{5,4},{6,5},{7,6},{9,8},{10,9},{11,10},{13,12},{... | collective-permute-start | bytes 3145736 | tf_op jit(solution)/shard_map/ppermute | solution.py:554
  19.2 1.9 collective-permute-start.2
  20.2 217.8 %all-gather.5.cloned.1.call-start = ((), (), s32[]{:S(2)}) async-start(), calls=%async_computation.11 | async-start | bytes 7077888 | tf_op jit(solution)/shard_map/all_gather | solution.py:724
  50.0 42.1 %collective-permute-start.3 = (bf16[3616,256]{1,0:T(8,128)(2,1)}, bf16[3616,256]{1,0:T(8,128)(2,1)}, u32[]{:S(2)}, u32[]{:S(2)}) collective-permute-start(bf16[3616,256]{1,0:T(8,128)(2,1)} %get-tuple-element.284), channel_id=1, source_target_pairs={{0,1},{1,2},{2,3},{4,5},{5,6},{6,7},{8,9},{9,10},{10,11},{12,13},{... | collective-permute-start | bytes 5554184 | tf_op jit(solution)/shard_map/ppermute | solution.py:553
  54.8 42.7 %collective-permute-start.4 = (bf16[3616,256]{1,0:T(8,128)(2,1)}, bf16[3616,256]{1,0:T(8,128)(2,1)}, u32[]{:S(2)}, u32[]{:S(2)}) collective-permute-start(bf16[3616,256]{1,0:T(8,128)(2,1)} %get-tuple-element.283), channel_id=1, source_target_pairs={{1,0},{2,1},{3,2},{5,4},{6,5},{7,6},{9,8},{10,9},{11,10},{13,12},{... | collective-permute-start | bytes 5554184 | tf_op jit(solution)/shard_map/ppermute | solution.py:554
  57.0 19.1 %collective-permute-start.5 = (bf16[1184,256]{1,0:T(8,128)(2,1)}, bf16[1184,256]{1,0:T(8,128)(2,1)}, u32[]{:S(2)}, u32[]{:S(2)}) collective-permute-start(bf16[1184,256]{1,0:T(8,128)(2,1)} %pad_maximum_fusion.6.refs_0_), channel_id=1, source_target_pairs={{0,8},{8,0},{16,24},{24,16},{1,9},{9,1},{17,25},{25,17},{2,10},{10... | collective-permute-start | bytes 1818632 | tf_op jit(solution)/shard_map/ppermute | solution.py:572
  58.5 26.8 %collective-permute-start.6 = (bf16[1184,256]{1,0:T(8,128)(2,1)}, bf16[1184,256]{1,0:T(8,128)(2,1)}, u32[]{:S(2)}, u32[]{:S(2)}) collective-permute-start(bf16[1184,256]{1,0:T(8,128)(2,1)} %pad_maximum_fusion.6.refs_0_), channel_id=1, source_target_pairs={{0,16},{8,24},{16,0},{24,8},{1,17},{9,25},{17,1},{25,9},{2,18},{10... | collective-permute-start | bytes 1818632 | tf_op jit(solution)/shard_map/ppermute | solution.py:572
  60.0 25.3 %collective-permute-start.7 = (bf16[1184,256]{1,0:T(8,128)(2,1)}, bf16[1184,256]{1,0:T(8,128)(2,1)}, u32[]{:S(2)}, u32[]{:S(2)}) collective-permute-start(bf16[1184,256]{1,0:T(8,128)(2,1)} %pad_maximum_fusion.6.refs_0_), channel_id=1, source_target_pairs={{0,24},{8,16},{16,8},{24,0},{1,25},{9,17},{17,9},{25,1},{2,26},{10... | collective-permute-start | bytes 1818632 | tf_op jit(solution)/shard_map/ppermute | solution.py:572
  71.5 33.2 %copy-start.9 = (bf16[512,1024]{1,0:T(8,128)(2,1)S(1)}, bf16[512,1024]{1,0:T(8,128)(2,1)}, u32[]{:S(2)}) copy-start(bf16[512,1024]{1,0:T(8,128)(2,1)} %copy-done.8) | copy-start | bytes 3145732
  97.5 39.6 %collective-permute-start.8 = (bf16[3616,256]{1,0:T(8,128)(2,1)}, bf16[3616,256]{1,0:T(8,128)(2,1)}, u32[]{:S(2)}, u32[]{:S(2)}) collective-permute-start(bf16[3616,256]{1,0:T(8,128)(2,1)} %collective-permute-done.3), channel_id=1, source_target_pairs={{0,1},{1,2},{2,3},{4,5},{5,6},{6,7},{8,9},{9,10},{10,11},{12,13},{... | collective-permute-start | bytes 5554184 | tf_op jit(solution)/shard_map/ppermute | solution.py:553
  101.0 41.4 %collective-permute-start.9 = (bf16[3616,256]{1,0:T(8,128)(2,1)}, bf16[3616,256]{1,0:T(8,128)(2,1)}, u32[]{:S(2)}, u32[]{:S(2)}) collective-permute-start(bf16[3616,256]{1,0:T(8,128)(2,1)} %collective-permute-done.4), channel_id=1, source_target_pairs={{1,0},{2,1},{3,2},{5,4},{6,5},{7,6},{9,8},{10,9},{11,10},{13,12},{... | collective-permute-start | bytes 5554184 | tf_op jit(solution)/shard_map/ppermute | solution.py:554
  108.6 8.1 %copy-start.13 = (bf16[1184,256]{1,0:T(8,128)(2,1)}, bf16[1184,256]{1,0:T(8,128)(2,1)S(1)}, u32[]{:S(2)}) copy-start(bf16[1184,256]{1,0:T(8,128)(2,1)S(1)} %slice.139.refs_4_) | copy-start | bytes 1818628
  108.6 16.8 %collective-permute-start.10 = (bf16[1184,256]{1,0:T(8,128)(2,1)S(1)}, bf16[1184,256]{1,0:T(8,128)(2,1)}, u32[]{:S(2)}, u32[]{:S(2)}) collective-permute-start(bf16[1184,256]{1,0:T(8,128)(2,1)S(1)} %slice.139.refs_4_), channel_id=1, source_target_pairs={{0,8},{8,0},{16,24},{24,16},{1,9},{9,1},{17,25},{25,17},{2,10},{10... | collective-permute-start | bytes 1818632 | tf_op jit(solution)/shard_map/ppermute | solution.py:572
  110.1 25.4 %collective-permute-start.11 = (bf16[1184,256]{1,0:T(8,128)(2,1)S(1)}, bf16[1184,256]{1,0:T(8,128)(2,1)}, u32[]{:S(2)}, u32[]{:S(2)}) collective-permute-start(bf16[1184,256]{1,0:T(8,128)(2,1)S(1)} %slice.139.refs_4_), channel_id=1, source_target_pairs={{0,16},{8,24},{16,0},{24,8},{1,17},{9,25},{17,1},{25,9},{2,18},{10... | collective-permute-start | bytes 1818632 | tf_op jit(solution)/shard_map/ppermute | solution.py:572
  111.6 23.9 %collective-permute-start.12 = (bf16[1184,256]{1,0:T(8,128)(2,1)S(1)}, bf16[1184,256]{1,0:T(8,128)(2,1)}, u32[]{:S(2)}, u32[]{:S(2)}) collective-permute-start(bf16[1184,256]{1,0:T(8,128)(2,1)S(1)} %slice.139.refs_4_), channel_id=1, source_target_pairs={{0,24},{8,16},{16,8},{24,0},{1,25},{9,17},{17,9},{25,1},{2,26},{10... | collective-permute-start | bytes 1818632 | tf_op jit(solution)/shard_map/ppermute | solution.py:572
  144.9 9.9 %copy-start.14 = (bf16[1184,256]{1,0:T(8,128)(2,1)}, bf16[1184,256]{1,0:T(8,128)(2,1)S(1)}, u32[]{:S(2)}) copy-start(bf16[1184,256]{1,0:T(8,128)(2,1)S(1)} %slice.140.refs_8_) | copy-start | bytes 1818628
  144.9 27.1 %collective-permute-start.15 = (bf16[1184,256]{1,0:T(8,128)(2,1)S(1)}, bf16[1184,256]{1,0:T(8,128)(2,1)}, u32[]{:S(2)}, u32[]{:S(2)}) collective-permute-start(bf16[1184,256]{1,0:T(8,128)(2,1)S(1)} %slice.140.refs_8_), channel_id=1, source_target_pairs={{0,8},{8,0},{16,24},{24,16},{1,9},{9,1},{17,25},{25,17},{2,10},{10... | collective-permute-start | bytes 1818632 | tf_op jit(solution)/shard_map/ppermute | solution.py:572
  146.4 25.6 %collective-permute-start.16 = (bf16[1184,256]{1,0:T(8,128)(2,1)S(1)}, bf16[1184,256]{1,0:T(8,128)(2,1)}, u32[]{:S(2)}, u32[]{:S(2)}) collective-permute-start(bf16[1184,256]{1,0:T(8,128)(2,1)S(1)} %slice.140.refs_8_), channel_id=1, source_target_pairs={{0,16},{8,24},{16,0},{24,8},{1,17},{9,25},{17,1},{25,9},{2,18},{10... | collective-permute-start | bytes 1818632 | tf_op jit(solution)/shard_map/ppermute | solution.py:572
  148.0 24.0 %collective-permute-start.17 = (bf16[1184,256]{1,0:T(8,128)(2,1)S(1)}, bf16[1184,256]{1,0:T(8,128)(2,1)}, u32[]{:S(2)}, u32[]{:S(2)}) collective-permute-start(bf16[1184,256]{1,0:T(8,128)(2,1)S(1)} %slice.140.refs_8_), channel_id=1, source_target_pairs={{0,24},{8,16},{16,8},{24,0},{1,25},{9,17},{17,9},{25,1},{2,26},{10... | collective-permute-start | bytes 1818632 | tf_op jit(solution)/shard_map/ppermute | solution.py:572
  148.4 23.6 %collective-permute-start.13 = (bf16[1568,256]{1,0:T(8,128)(2,1)}, bf16[1568,256]{1,0:T(8,128)(2,1)}, u32[]{:S(2)}, u32[]{:S(2)}) collective-permute-start(bf16[1568,256]{1,0:T(8,128)(2,1)} %get-tuple-element.269), channel_id=1, source_target_pairs={{0,1},{1,2},{2,3},{4,5},{5,6},{6,7},{8,9},{9,10},{10,11},{12,13},{... | collective-permute-start | bytes 2408456 | tf_op jit(solution)/shard_map/ppermute | solution.py:553
  150.8 21.3 %collective-permute-start.14 = (bf16[1568,256]{1,0:T(8,128)(2,1)S(1)}, bf16[1568,256]{1,0:T(8,128)(2,1)}, u32[]{:S(2)}, u32[]{:S(2)}) collective-permute-start(bf16[1568,256]{1,0:T(8,128)(2,1)S(1)} %get-tuple-element.270), channel_id=1, source_target_pairs={{1,0},{2,1},{3,2},{5,4},{6,5},{7,6},{9,8},{10,9},{11,10},{13,12},{... | collective-permute-start | bytes 2408456 | tf_op jit(solution)/shard_map/ppermute | solution.py:554
  177.5 20.1 %copy-start.15 = (bf16[1184,256]{1,0:T(8,128)(2,1)}, bf16[1184,256]{1,0:T(8,128)(2,1)S(1)}, u32[]{:S(2)}) copy-start(bf16[1184,256]{1,0:T(8,128)(2,1)S(1)} %slice.141.refs_12_) | copy-start | bytes 1818628
  177.5 22.7 %collective-permute-start.18 = (bf16[1184,256]{1,0:T(8,128)(2,1)S(1)}, bf16[1184,256]{1,0:T(8,128)(2,1)S(1)}, u32[]{:S(2)}, u32[]{:S(2)}) collective-permute-start(bf16[1184,256]{1,0:T(8,128)(2,1)S(1)} %slice.141.refs_12_), channel_id=1, source_target_pairs={{0,8},{8,0},{16,24},{24,16},{1,9},{9,1},{17,25},{25,17},{2,10},{10... | collective-permute-start | bytes 1818632 | tf_op jit(solution)/shard_map/ppermute | solution.py:572
  179.1 30.8 %collective-permute-start.19 = (bf16[1184,256]{1,0:T(8,128)(2,1)S(1)}, bf16[1184,256]{1,0:T(8,128)(2,1)S(1)}, u32[]{:S(2)}, u32[]{:S(2)}) collective-permute-start(bf16[1184,256]{1,0:T(8,128)(2,1)S(1)} %slice.141.refs_12_), channel_id=1, source_target_pairs={{0,16},{8,24},{16,0},{24,8},{1,17},{9,25},{17,1},{25,9},{2,18},{10... | collective-permute-start | bytes 1818632 | tf_op jit(solution)/shard_map/ppermute | solution.py:572
  180.6 30.0 %collective-permute-start.20 = (bf16[1184,256]{1,0:T(8,128)(2,1)S(1)}, bf16[1184,256]{1,0:T(8,128)(2,1)S(1)}, u32[]{:S(2)}, u32[]{:S(2)}) collective-permute-start(bf16[1184,256]{1,0:T(8,128)(2,1)S(1)} %slice.141.refs_12_), channel_id=1, source_target_pairs={{0,24},{8,16},{16,8},{24,0},{1,25},{9,17},{17,9},{25,1},{2,26},{10... | collective-permute-start | bytes 1818632 | tf_op jit(solution)/shard_map/ppermute | solution.py:572
  181.6 32.9 %all-to-all-start = ((bf16[4,512,128]{2,1,0:T(8,128)(2,1)}), bf16[4,512,128]{2,1,0:T(8,128)(2,1)S(1)}, u32[]{:S(2)}, u32[]{:S(2)}) async-start(bf16[4,512,128]{2,1,0:T(8,128)(2,1)} %bitcast.195), calls=%async_computation | async-start | bytes 1048576 | tf_op jit(solution)/shard_map/all_to_all | solution.py:615
  200.2 10.4 %copy-start.29 = (bf16[1184,256]{1,0:T(8,128)(2,1)}, bf16[1184,256]{1,0:T(8,128)(2,1)S(1)}, u32[]{:S(2)}) copy-start(bf16[1184,256]{1,0:T(8,128)(2,1)S(1)} %collective-permute-done.18.refs_13_) | copy-start | bytes 1818628
  214.5 4.9 collective-permute-start.21
  214.5 8.0 %copy-start.17 = (bf16[4,512,128]{2,1,0:T(8,128)(2,1)}, bf16[4,512,128]{2,1,0:T(8,128)(2,1)S(1)}, u32[]{:S(2)}) copy-start(bf16[4,512,128]{2,1,0:T(8,128)(2,1)S(1)} %all-to-all-done) | copy-start | bytes 1572868
  214.5 18.9 %all-to-all-start.1 = ((bf16[4,512,128]{2,1,0:T(8,128)(2,1)}), bf16[4,512,128]{2,1,0:T(8,128)(2,1)S(1)}, u32[]{:S(2)}, u32[]{:S(2)}) async-start(bf16[4,512,128]{2,1,0:T(8,128)(2,1)} %bitcast.22), calls=%async_computation.1 | async-start | bytes 1048576 | tf_op jit(solution)/shard_map/all_to_all | solution.py:615
  218.2 106.2 %reduce-scatter.10.cloned.1.call-start = ((), (), s32[]{:S(2)}) async-start(), calls=%async_computation.12 | async-start | bytes 3604480
  218.2 20.0 %collective-permute-start.23 = (bf16[512,1024]{1,0:T(8,128)(2,1)}, bf16[512,1024]{1,0:T(8,128)(2,1)}, u32[]{:S(2)}, u32[]{:S(2)}) collective-permute-start(bf16[512,1024]{1,0:T(8,128)(2,1)} %refs_18_.1), channel_id=1, source_target_pairs={{0,4},{4,0},{1,5},{5,1},{2,6},{6,2},{3,7},{7,3},{8,12},{12,8},{9,1... | collective-permute-start | bytes 3145736 | tf_op jit(solution)/shard_map/ppermute | solution.py:634
  219.4 14.8 %copy-start.2 = (bf16[512,1024]{1,0:T(8,128)(2,1)S(1)}, bf16[512,1024]{1,0:T(8,128)(2,1)}, u32[]{:S(2)}) copy-start(bf16[512,1024]{1,0:T(8,128)(2,1)} %x_ref.1) | copy-start | bytes 3145732
  237.8 46.3 %copy-start = (f32[512,1024]{1,0:T(8,128)}, f32[512,1024]{1,0:T(8,128)S(1)}, u32[]{:S(2)}) copy-start(f32[512,1024]{1,0:T(8,128)S(1)} %get-tuple-element.303) | copy-start | bytes 6291460
  238.1 2.9 collective-permute-start.22
  279.5 4.6 collective-permute-start.25
  279.7 7.7 %collective-permute-start.24 = (f32[512,1024]{1,0:T(8,128)}, f32[512,1024]{1,0:T(8,128)}, u32[]{:S(2)}, u32[]{:S(2)}) collective-permute-start(f32[512,1024]{1,0:T(8,128)} %get-tuple-element.226), channel_id=1, source_target_pairs={{0,4},{4,0},{1,5},{5,1},{2,6},{6,2},{3,7},{7,3},{8,12},{12,8},{9,1... | collective-permute-start | bytes 6291464 | tf_op jit(solution)/shard_map/ppermute | solution.py:634
  301.9 10.4 %collective-permute-start.26 = (bf16[4,128,1024]{1,2,0:T(8,128)(2,1)}, bf16[4,128,1024]{1,2,0:T(8,128)(2,1)}, u32[]{:S(2)}, u32[]{:S(2)}) collective-permute-start(bf16[4,128,1024]{1,2,0:T(8,128)(2,1)} %broadcast_select_fusion), channel_id=1, source_target_pairs={{0,4},{4,0},{1,5},{5,1},{2,6},{6,2},{3,7},{7,3},{8,12},{12,8},{9,1... | collective-permute-start | bytes 3145736 | tf_op jit(solution)/shard_map/ppermute | solution.py:634
  304.7 19.6 %all-to-all-start.2 = ((bf16[4,512,128]{1,2,0:T(8,128)(2,1)}), bf16[4,512,128]{1,2,0:T(8,128)(2,1)}, u32[]{:S(2)}, u32[]{:S(2)}) async-start(bf16[4,512,128]{1,2,0:T(8,128)(2,1)} %fusion.22), calls=%async_computation.2 | async-start | bytes 1048576 | tf_op jit(solution)/shard_map/all_to_all | solution.py:615
  308.9 89.5 %reduce-scatter.12.cloned.1.call-start = ((), (), s32[]{:S(2)}) async-start(), calls=%async_computation.13 | async-start | bytes 8519680
  327.3 28.4 %collective-permute-start.27 = (bf16[352,256]{1,0:T(8,128)(2,1)}, bf16[352,256]{1,0:T(8,128)(2,1)S(1)}, u32[]{:S(2)}, u32[]{:S(2)}) collective-permute-start(bf16[352,256]{1,0:T(8,128)(2,1)} %get-tuple-element.287), channel_id=1, source_target_pairs={{0,1},{1,2},{2,3},{3,0},{4,5},{5,6},{6,7},{7,4},{8,9},{9,10},{10,1... | collective-permute-start | bytes 540680 | tf_op jit(solution)/shard_map/ppermute | solution.py:624
  327.3 28.4 %collective-permute-start.28 = (bf16[352,256]{1,0:T(8,128)(2,1)S(1)}, bf16[352,256]{1,0:T(8,128)(2,1)S(1)}, u32[]{:S(2)}, u32[]{:S(2)}) collective-permute-start(bf16[352,256]{1,0:T(8,128)(2,1)S(1)} %get-tuple-element.286), channel_id=1, source_target_pairs={{0,2},{1,3},{2,0},{3,1},{4,6},{5,7},{6,4},{7,5},{8,10},{9,11},{10,... | collective-permute-start | bytes 540680 | tf_op jit(solution)/shard_map/ppermute | solution.py:624
  329.3 26.4 %collective-permute-start.29 = (bf16[352,256]{1,0:T(8,128)(2,1)S(1)}, bf16[352,256]{1,0:T(8,128)(2,1)S(1)}, u32[]{:S(2)}, u32[]{:S(2)}) collective-permute-start(bf16[352,256]{1,0:T(8,128)(2,1)S(1)} %get-tuple-element.285), channel_id=1, source_target_pairs={{0,3},{1,0},{2,1},{3,2},{4,7},{5,4},{6,5},{7,6},{8,11},{9,8},{10,9... | collective-permute-start | bytes 540680 | tf_op jit(solution)/shard_map/ppermute | solution.py:624
  331.1 26.1 %all-to-all-start.3 = ((bf16[4,512,128]{1,2,0:T(8,128)(2,1)}), bf16[4,512,128]{1,2,0:T(8,128)(2,1)S(1)}, u32[]{:S(2)}, u32[]{:S(2)}) async-start(bf16[4,512,128]{1,2,0:T(8,128)(2,1)} %fusion.21), calls=%async_computation.3 | async-start | bytes 1048576 | tf_op jit(solution)/shard_map/all_to_all | solution.py:615
  355.7 6.9 %copy-start.33 = (bf16[352,256]{1,0:T(8,128)(2,1)}, bf16[352,256]{1,0:T(8,128)(2,1)S(1)}, u32[]{:S(2)}) copy-start(bf16[352,256]{1,0:T(8,128)(2,1)S(1)} %collective-permute-done.27) | copy-start | bytes 540676
  355.7 6.9 %copy-start.34 = (bf16[352,256]{1,0:T(8,128)(2,1)}, bf16[352,256]{1,0:T(8,128)(2,1)S(1)}, u32[]{:S(2)}) copy-start(bf16[352,256]{1,0:T(8,128)(2,1)S(1)} %collective-permute-done.28) | copy-start | bytes 540676
  357.2 40.7 %all-to-all-start.4 = ((bf16[4,512,384]{2,1,0:T(8,128)(2,1)}), bf16[4,512,384]{2,1,0:T(8,128)(2,1)}, u32[]{:S(2)}, u32[]{:S(2)}) async-start(bf16[4,512,384]{2,1,0:T(8,128)(2,1)} %bitcast.184), calls=%async_computation.4 | async-start | bytes 3145728 | tf_op jit(solution)/shard_map/all_to_all | solution.py:615
  408.3 6.7 %collective-permute-start.33 = (bf16[384,1024]{1,0:T(8,128)(2,1)}, bf16[384,1024]{1,0:T(8,128)(2,1)}, u32[]{:S(2)}, u32[]{:S(2)}) collective-permute-start(bf16[384,1024]{1,0:T(8,128)(2,1)} %broadcast_select_fusion.6), channel_id=1, source_target_pairs={{0,4},{4,0},{1,5},{5,1},{2,6},{6,2},{3,7},{7,3},{8,12},{12,8},{9,1... | collective-permute-start | bytes 2359304 | tf_op jit(solution)/shard_map/ppermute | solution.py:634
  408.3 70.6 %all-to-all-start.5 = ((bf16[4,512,384]{2,1,0:T(8,128)(2,1)}), bf16[4,512,384]{2,1,0:T(8,128)(2,1)}, u32[]{:S(2)}, u32[]{:S(2)}) async-start(bf16[4,512,384]{2,1,0:T(8,128)(2,1)} %bitcast.183), calls=%async_computation.5 | async-start | bytes 3145728 | tf_op jit(solution)/shard_map/all_to_all | solution.py:615
  413.0 65.9 %reduce-scatter.14.cloned.1.call-start = ((), (), s32[]{:S(2)}) async-start(), calls=%async_computation.14 | async-start | bytes 983040
  417.6 1.5 collective-permute-start.37
  419.1 7.5 %copy-start.26 = (f32[2048,128]{1,0:T(8,128)S(1)}, f32[2048,128]{1,0:T(8,128)}, u32[]{:S(2)}) copy-start(f32[2048,128]{1,0:T(8,128)} %get-tuple-element.251) | copy-start | bytes 3145732
  419.1 7.5 %copy-start.27 = (f32[2048,128]{1,0:T(8,128)S(1)}, f32[2048,128]{1,0:T(8,128)}, u32[]{:S(2)}) copy-start(f32[2048,128]{1,0:T(8,128)} %get-tuple-element.252) | copy-start | bytes 3145732
  420.8 32.5 %collective-permute-start.30 = (bf16[832,256]{1,0:T(8,128)(2,1)S(1)}, bf16[832,256]{1,0:T(8,128)(2,1)}, u32[]{:S(2)}, u32[]{:S(2)}) collective-permute-start(bf16[832,256]{1,0:T(8,128)(2,1)S(1)} %get-tuple-element.273), channel_id=1, source_target_pairs={{0,1},{1,2},{2,3},{3,0},{4,5},{5,6},{6,7},{7,4},{8,9},{9,10},{10,1... | collective-permute-start | bytes 1277960 | tf_op jit(solution)/shard_map/ppermute | solution.py:624
  422.8 56.1 %collective-permute-start.31 = (bf16[832,256]{1,0:T(8,128)(2,1)S(1)}, bf16[832,256]{1,0:T(8,128)(2,1)}, u32[]{:S(2)}, u32[]{:S(2)}) collective-permute-start(bf16[832,256]{1,0:T(8,128)(2,1)S(1)} %get-tuple-element.272), channel_id=1, source_target_pairs={{0,2},{1,3},{2,0},{3,1},{4,6},{5,7},{6,4},{7,5},{8,10},{9,11},{10,... | collective-permute-start | bytes 1277960 | tf_op jit(solution)/shard_map/ppermute | solution.py:624
  425.2 53.7 %collective-permute-start.32 = (bf16[832,256]{1,0:T(8,128)(2,1)S(1)}, bf16[832,256]{1,0:T(8,128)(2,1)}, u32[]{:S(2)}, u32[]{:S(2)}) collective-permute-start(bf16[832,256]{1,0:T(8,128)(2,1)S(1)} %get-tuple-element.271), channel_id=1, source_target_pairs={{0,3},{1,0},{2,1},{3,2},{4,7},{5,4},{6,5},{7,6},{8,11},{9,8},{10,9... | collective-permute-start | bytes 1277960 | tf_op jit(solution)/shard_map/ppermute | solution.py:624
  482.3 8.2 %collective-permute-start.36 = (f32[2,352,128]{2,1,0:T(8,128)}, f32[2,352,128]{2,1,0:T(8,128)S(1)}, u32[]{:S(2)}, u32[]{:S(2)}) collective-permute-start(f32[2,352,128]{2,1,0:T(8,128)} %slice_select_fusion.1), channel_id=1, source_target_pairs={{0,4},{4,0},{1,5},{5,1},{2,6},{6,2},{3,7},{7,3},{8,12},{12,8},{9,1... | collective-permute-start | bytes 1081352 | tf_op jit(solution)/shard_map/ppermute | solution.py:634
  482.3 7.1 %collective-permute-start.34 = (f32[384,128]{1,0:T(8,128)S(1)}, f32[384,128]{1,0:T(8,128)S(1)}, u32[]{:S(2)}, u32[]{:S(2)}) collective-permute-start(f32[384,128]{1,0:T(8,128)S(1)} %slice_select_fusion.3), channel_id=1, source_target_pairs={{0,4},{4,0},{1,5},{5,1},{2,6},{6,2},{3,7},{7,3},{8,12},{12,8},{9,1... | collective-permute-start | bytes 589832 | tf_op jit(solution)/shard_map/ppermute | solution.py:634
  482.9 6.5 %collective-permute-start.35 = (f32[128,128]{1,0:T(8,128)S(1)}, f32[128,128]{1,0:T(8,128)S(1)}, u32[]{:S(2)}, u32[]{:S(2)}) collective-permute-start(f32[128,128]{1,0:T(8,128)S(1)} %slice_select_fusion.7), channel_id=1, source_target_pairs={{0,4},{4,0},{1,5},{5,1},{2,6},{6,2},{3,7},{7,3},{8,12},{12,8},{9,1... | collective-permute-start | bytes 196616 | tf_op jit(solution)/shard_map/ppermute | solution.py:634
  491.7 18.0 %copy-start.12 = (f32[2,2,352,128]{3,2,1,0:T(8,128)}, f32[2,2,352,128]{3,2,1,0:T(8,128)S(1)}, u32[]{:S(2)}) copy-start(f32[2,2,352,128]{3,2,1,0:T(8,128)S(1)} %pad_maximum_fusion.5) | copy-start | bytes 2162692
  492.5 16.6 %all-to-all-start.6 = ((f32[4,2,128]{2,1,0:T(2,128)}), f32[4,2,128]{2,1,0:T(2,128)S(1)}, u32[]{:S(2)}, u32[]{:S(2)}) async-start(f32[4,2,128]{2,1,0:T(2,128)} %broadcast_in_dim.2), calls=%async_computation.6 | async-start | bytes 8192 | tf_op jit(solution)/shard_map/all_to_all | solution.py:615
  (23 other events, 62.7 us)
Sparse Core Ops, SparseCore 0:
  20.3 28.4 all-gather.2
  177.6 59.8 all-gather.4
  279.8 41.0 reduce-scatter.9
  324.5 73.8 reduce-scatter.11
  417.7 26.5 reduce-scatter.13
where the time goes:
time: 526 us; the launch traced here: 517 us
  waiting for transfers between devices  160 us (30%)
  Pallas kernels  136 us (26%)
  starting transfers between devices  83.1 us (16%)
  other arithmetic  75.6 us (14%)
  local copies, waits for them, and re-layouts  25.6 us (5%)
  matrix products  20.9 us (4%)
  between operations  15.6 us (3%)
    ppermute x6, waiting for transfers between devices, exchange_turned(): lax.ppermute(piece, 'head', [(k, (k + j) % count) for k in range(count)])  45.2 us
    pallas_call x2, Pallas kernels, attend_back(): pl.pallas_call(attend_back_kernel, grid_spec=spec, out_shape=[jax.ShapeDt...  42.2 us
    pallas_call x1, Pallas kernels, feed(): pl.pallas_call(feed_kernel, grid_spec=spec, out_shape=[jax.ShapeDtypeStru...  38.5 us
    all_to_all x7, waiting for transfers between devices, exchange(): return lax.all_to_all(pieces, 'head', split_axis=0, concat_axis=0)  38.3 us
    all_to_all x7, starting transfers between devices, exchange(): return lax.all_to_all(pieces, 'head', split_axis=0, concat_axis=0)  35.4 us
    ppermute x12, waiting for transfers between devices, plane(): lax.ppermute(slot[:end], 'chip', [(c, c ^ away) for c in range(chips)])  33.3 us
    pallas_call x2, Pallas kernels, attend(): pl.pallas_call(attend_kernel, grid_spec=spec, out_shape=[jax.ShapeDtypeSt...  24.2 us
    ppermute x4, waiting for transfers between devices, hop(): lax.ppermute(ends[0], 'head', [(0, 1), (1, 2), (2, 3)])  21.1 us
  transfers between devices with their start and end apart: 50, of which 24 were waited for; matrix products, arithmetic and copies ran while one was open for 20% of the time, Pallas kernels for 17%

commit v1 on v0

--- a/solution.py
+++ b/solution.py
@@ -18,6 +18,7 @@
 low = jnp.bfloat16
 wide = jnp.float32
 VMEM_BYTES = 60 * 1024 * 1024
+FINISH_FLOPS = 1 << 38
 
 
 def dot_nn(a, b):
@@ -467,6 +468,30 @@
     )(order, which, *sum(slots, []))
 
 
+def join_kernel(right_ref, left_ref, w_ref, *outs):
+    rows, depth = right_ref.shape
+    width = w_ref.shape[1]
+    cut = rows * depth // width
+    for ref, out_ref in zip((right_ref, left_ref), outs):
+        for number in range(depth // width):
+            cols = slice(number * width, (number + 1) * width)
+            out_ref[number * rows : (number + 1) * rows, :] = ref[:, cols]
+        out_ref[cut:, :] = w_ref[...]
+
+
+def join(right, left, weights):
+    rows, depth = right.shape
+    height, width = weights.shape
+    shape = jax.ShapeDtypeStruct((rows * depth // width + height, width), low)
+    return pl.pallas_call(
+        join_kernel,
+        out_shape=[shape] * 2,
+        compiler_params=pltpu.CompilerParams(vmem_limit_bytes=VMEM_BYTES),
+        cost_estimate=pl.CostEstimate(flops=0, bytes_accessed=7 << 20, transcendentals=0),
+        name="join",
+    )(right, left, weights)
+
+
 def line_up_kernel(order, *refs):
     out_ref = refs[-1]
     height, width = refs[0].shape
@@ -496,6 +521,57 @@
         cost_estimate=pl.CostEstimate(flops=0, bytes_accessed=2 << 20, transcendentals=0),
         name="line_up",
     )(order, *arrived)
+
+
+def turn_kernel(facts, own_ref, came_ref, state_ref, c_ref, gain_ref, w_ref, grad_ref, low_ref, *asked):
+    normed_grad = own_ref[...] + came_ref[...]
+    gain = gain_ref[1:2, :].astype(wide)
+    _, unit, factor = rms_parts(state_ref[...], gain)
+    state_grad = c_ref[...].astype(wide) + rms_back(normed_grad, unit, factor, gain)
+    branch_grad = state_grad.astype(low)
+    grad_ref[...] = state_grad
+    low_ref[...] = branch_grad
+    chunk = own_ref.shape[0]
+    start = facts[1] * chunk * pl.num_programs(0) + pl.program_id(0) * chunk
+    valid = start + lax.broadcasted_iota(jnp.int32, (chunk, 1), 0) < facts[0]
+    heads_grad = jnp.where(valid, dot_nt(branch_grad, w_ref[...]), 0.0).astype(low)
+    line = asked[0].shape[0]
+    for z in range(line):
+        for pair, ref in enumerate(asked):
+            column = (z * len(asked) + pair) * LANES
+            ref[z] = heads_grad[:, column : column + LANES]
+
+
+def turn(facts, own, came, hidden_state, cotangent, pack, out_full, line, pairs):
+    rows, depth = own.shape
+    chunk = rows // 2
+    gain_block = pack.shape[0] // GAIN_ROWS - 1
+    block = pl.BlockSpec((chunk, depth), lambda i, f: (i, 0))
+    piece = pl.BlockSpec((line, chunk, LANES), lambda i, f: (0, i, 0))
+    spec = pltpu.PrefetchScalarGridSpec(
+        num_scalar_prefetch=1,
+        grid=(rows // chunk,),
+        in_specs=[
+            block, block, block, block,
+            pl.BlockSpec((GAIN_ROWS, depth), lambda i, f: (gain_block, 0)),
+            pl.BlockSpec((depth, depth), lambda i, f: (0, 0)),
+        ],
+        out_specs=[block, block] + [piece] * pairs,
+    )
+    return pl.pallas_call(
+        turn_kernel,
+        grid_spec=spec,
+        out_shape=[
+            jax.ShapeDtypeStruct((rows, depth), wide),
+            jax.ShapeDtypeStruct((rows, depth), low),
+        ]
+        + [jax.ShapeDtypeStruct((line, rows, LANES), low)] * pairs,
+        compiler_params=pltpu.CompilerParams(vmem_limit_bytes=VMEM_BYTES),
+        cost_estimate=pl.CostEstimate(
+            flops=2 * rows * depth * depth, bytes_accessed=13 << 20, transcendentals=0
+        ),
+        name="turn",
+    )(facts, own, came, hidden_state, cotangent, pack, out_full)
 
 
 def unproject_kernel(normed_ref, *refs):
@@ -529,11 +605,45 @@
         scratch_shapes=[pltpu.VMEM((total, depth), wide)],
         out_shape=jax.ShapeDtypeStruct((total, depth), low),
         compiler_params=pltpu.CompilerParams(vmem_limit_bytes=VMEM_BYTES),
-        cost_estimate=pl.CostEstimate(
-            flops=2 * tokens * depth * total, bytes_accessed=9 << 20, transcendentals=0
-        ),
+        cost_estimate=pl.CostEstimate(flops=0, bytes_accessed=0, transcendentals=0),
         name="unproject",
     )(normed, *mixed_grads)
+
+
+def finish_kernel(came_ref, w_ref, part_ref, x_ref, gain_ref, state_ref, out_ref):
+    normed_grad = part_ref[...]
+    for number in range(came_ref.shape[0]):
+        normed_grad += dot_nn(came_ref[number], w_ref[number, 0])
+    gain = gain_ref[0:1, :].astype(wide)
+    _, unit, factor = rms_parts(x_ref[...].astype(wide), gain)
+    out_ref[...] = state_ref[...] + rms_back(normed_grad, unit, factor, gain)
+
+
+def finish(came, qkv_full, part, tokens, pack, state_grad):
+    line, rows, height = came.shape
+    pairs, depth = qkv_full.shape[1], qkv_full.shape[3]
+    gain_block = pack.shape[0] // GAIN_ROWS - 1
+    chunk = rows // 2
+    block = pl.BlockSpec((chunk, depth), lambda i: (i, 0))
+    return pl.pallas_call(
+        finish_kernel,
+        grid=(rows // chunk,),
+        in_specs=[
+            pl.BlockSpec((line, chunk, height), lambda i: (0, i, 0)),
+            pl.BlockSpec((line, 1, height, depth), lambda i: (0, pairs - 1, 0, 0)),
+            block,
+            block,
+            pl.BlockSpec((GAIN_ROWS, depth), lambda i: (gain_block, 0)),
+            block,
+        ],
+        out_specs=block,
+        out_shape=jax.ShapeDtypeStruct((rows, depth), wide),
+        compiler_params=pltpu.CompilerParams(vmem_limit_bytes=VMEM_BYTES),
+        cost_estimate=pl.CostEstimate(
+            flops=FINISH_FLOPS, bytes_accessed=10 << 20, transcendentals=0
+        ),
+        name="finish",
+    )(came, qkv_full, part, tokens, pack, state_grad)
 
 
 def arrival_order(place):
@@ -542,7 +652,7 @@
     return jnp.stack([place, place + ways, place + 2 * ways, far]).astype(jnp.int32)
 
 
-def gather_all(tokens, weights, end, place, chips, use, then):
+def gather_all(tokens, weights, end, place, chips, use, then, send):
     near = place < 2
     rows, depth = tokens.shape
     width = weights.shape[1]
@@ -561,9 +671,6 @@
         return jnp.where(
             place % 3 == 0, nearest(hops), jnp.where(near, hops[0][0], hops[0][1])
         )
-
-    def in_blocks(tokens):
-        return jnp.moveaxis(tokens.reshape(rows, -1, width), 1, 0).reshape(cut, width)
 
     def plane(slot):
         if chips != 4:
@@ -578,9 +685,10 @@
     token_hops, weight_hops = [], []
     ends = barrier(hop((tokens, tokens)))
     first_block = nearest([ends])
-    token_hops.append(tuple(in_blocks(end) for end in ends))
-
-    ends = hop(tuple(jnp.concatenate([end, weights]) for end in token_hops[0]))
+    ends = tuple(join(*ends, weights))
+    token_hops.append(tuple(end[:cut] for end in ends))
+
+    ends = hop(ends)
     planes.append(plane(weights))
     used = use(0, tokens, None)
     ends, planes, used = barrier((ends, planes, used))
@@ -603,12 +711,14 @@
     planes.append(plane(slots[2]))
     made, used = then(0, used)
     ends, planes, made, used = barrier((ends, planes, made, used))
+    sent = [send(made[0])]
     weight_hops.append(ends)
     slots.append(farthest(weight_hops))
     planes.append(plane(slots[3]))
     more, used = then(1, used)
-    planes, more = barrier((planes, more))
-    return planes, [slot[end:] for slot in slots], used, [made, more]
+    planes, more, sent = barrier((planes, more, sent))
+    sent.append(send(more[0]))
+    return planes, slots, used, [made, more], sent
 
 
 def exchange(pieces):
@@ -624,10 +734,6 @@
             lax.ppermute(piece, "head", [(k, (k + j) % count) for k in range(count)]) if j else piece
         )
     return came
-
-
-def to_line(piece, count):
-    return exchange(jnp.broadcast_to(piece[None], (count, *piece.shape)))
 
 
 def other_core(array):
@@ -673,7 +779,6 @@
     pack = lax.all_gather(
         jnp.concatenate([qkv_rows, gain_rows], axis=0), ("chip", "core"), axis=1, tiled=True
     )
-    gain_first = pack[3 * cols].astype(wide)
     gain_second = pack[3 * cols + 1].astype(wide)
 
     gates_low = gate_up.astype(low)
@@ -706,38 +811,57 @@
     def then(pair, made):
         return attend(pair, lengths, *made[:3]), made
 
-    planes, qkv_line, made, attended_parts = gather_all(
-        tokens, weights, end, place, chips, use, then
+    def send(result):
+        return exchange(result.reshape(line, rows, LANES))
+
+    planes, slots, made, attended_parts, attended_pieces = gather_all(
+        tokens, weights, end, place, chips, use, then, send
     )
     query, keys, values, normed_a = made
     cot_other = other_core(cotangent)
     out_half = collect(order, which, planes, cols // 2).reshape(line, 1, cols // 2, depth)
+    qkv_sides, out_half = after(([slot[end:] for slot in slots], out_half))
     out_heads = by_core(core, out_half, other_core(out_half), 1)
     out_full = out_heads.reshape(depth, depth)
     lined = chips == 4
-    attended_pieces = [exchange(part[0].reshape(line, rows, LANES)) for part in attended_parts]
     attended_wide = [part[1] for part in attended_parts]
     log_total = [part[2] for part in attended_parts]
     attended = jnp.stack(attended_pieces, axis=1).transpose(2, 0, 1, 3).reshape(rows, depth)
 
-    qkv_line = line_up(order, qkv_line, pairs)
+    qkv_line = line_up(order, qkv_sides, pairs)
     qkv_full = lax.all_gather(qkv_line, ("chip", "core"), axis=1, tiled=True)
     qkv_full = qkv_full.reshape(line, pairs, 3 * LANES, depth)
 
     token_rows = tokens.astype(wide)
     hidden_state = token_rows + dot_nn(attended, out_full)
-    normed_b, unit_b, factor_b = rms_parts(hidden_state, gain_second)
-    normed_b = before(normed_b.astype(low), qkv_full)
+    normed_b = rms_parts(hidden_state, gain_second)[0].astype(low)
     branch_own, branch_other, grad_own, grad_other, gate_grad, down_grad = feed(
         order, which, planes, units, normed_b, other_core(normed_b), cotangent, cot_other
     )
-    normed_b_grad = grad_own + other_core(grad_other)
+    facts = jnp.concatenate([lengths, place_one])
+    state_grad, branch_grad, *asked = turn(
+        facts, grad_own, before(other_core(grad_other), qkv_full), hidden_state, cotangent, pack,
+        out_full, line, pairs,
+    )
     branch_b = branch_own + other_core(branch_other)
     block_out = (hidden_state + branch_b).astype(low)
 
-    state_part = rms_back(normed_b_grad, unit_b, factor_b, gain_second)
-    state_grad = cotangent.astype(wide) + state_part
-    branch_grad = state_grad.astype(low)
+    def settle(grad):
+        kept, given = halves(grad, -1)
+        return by_core(core, kept[..., None, :, :], other_core(given)[..., None, :, :], -3)
+
+    def plane_sum(grad):
+        if chips != 4:
+            return chip_scatter(grad).astype(wide)
+        pieces = [
+            lax.dynamic_slice_in_dim(grad, (chip ^ away) * 2 * width, 2 * width, 1)
+            for away in range(chips)
+        ]
+        moved = [
+            lax.ppermute(pieces[away], "chip", [(c, c ^ away) for c in range(chips)])
+            for away in range(1, chips)
+        ]
+        return sum(piece.astype(wide) for piece in [pieces[0]] + moved)
 
     def spread(grad):
         if not lined:
@@ -745,14 +869,6 @@
         return grad
 
     down_sum = lax.psum_scatter(spread(down_grad), "chip", scatter_dimension=0)
-    positions = place * rows + jnp.arange(rows)
-    valid = (positions < lengths[0]).astype(wide)[None, :, None]
-    outs = out_full.reshape(line, pairs, LANES, depth)
-    asked = [
-        (valid * jnp.einsum("td,zcd->ztc", branch_grad, outs[:, pair], preferred_element_type=wide)).astype(low)
-        for pair in range(pairs)
-    ]
-
     def back(pair, came):
         return attend_back(
             pair, lengths, query, keys, values, came.reshape(line * rows, LANES),
@@ -765,7 +881,9 @@
     out_grad = (kept.astype(wide) + other_core(given).astype(wide)).astype(low)
     out_grad = jnp.moveaxis(out_grad.reshape(line, cols // 2, chips, 2 * width), 2, 0)
     gate_grad = spread(gate_grad).at[:, :, : cols // 2].set(out_grad)
-    came, gate_grad, asked, down_sum = after((came, gate_grad, asked, down_sum))
+    came, gate_grad, asked, down_sum, block_out = after(
+        (came, gate_grad, asked, down_sum, block_out)
+    )
 
     gate_sum = lax.psum_scatter(gate_grad, "chip", scatter_dimension=0)
     mixed_first = back(0, came)
@@ -775,45 +893,37 @@
 
     mixed_second = back(1, came)
     mixed_rows = exchange(mixed_first[0].reshape(line, rows, 3 * LANES))
-    mixed_rows, mixed_second, gate_sum = after((mixed_rows, mixed_second, gate_sum))
+    mixed_rows, mixed_second = after((mixed_rows, mixed_second))
 
     came = exchange(mixed_second[0].reshape(line, rows, 3 * LANES))
-    gate_came = exchange_turned(gate_sum, place)
+    gate_came = exchange_turned(after(gate_sum), place)
     qkv_grad = unproject(normed_a, [mixed_first[0], mixed_second[0]])
     kept, given = halves(qkv_grad, 0)
     qkv_grad = (kept.astype(wide) + other_core(given).astype(wide)).astype(low)
-    qkv_sum = chip_scatter(qkv_grad)
+    came, gate_came, qkv_grad = after((came, gate_came, qkv_grad))
+
+    qkv_sum = settle(plane_sum(qkv_grad)).reshape(pairs, 3, LANES, width)
+    mixer_in_grad = qkv_sum.transpose(1, 3, 0, 2).reshape(3, width, cols)
     normed_a_grad = jnp.einsum(
         "ztc,zcd->td", mixed_rows, qkv_full[:, 0], preferred_element_type=wide
     )
-    normed_a_grad, came, gate_came, qkv_sum = after((normed_a_grad, came, gate_came, qkv_sum))
-    normed_a_grad += jnp.einsum("ztc,zcd->td", came, qkv_full[:, 1], preferred_element_type=wide)
-    first_grad = jnp.concatenate([mixed_first[1], mixed_second[1]], axis=1)
-
-    def settle(grad):
-        kept, given = halves(grad, -1)
-        return by_core(core, kept[..., None, :, :], other_core(given)[..., None, :, :], -3)
-
-    gate_sum = sum(piece.astype(wide) for piece in gate_came)
+    tokens_grad = finish(came, qkv_full, normed_a_grad, tokens, pack, state_grad)
     down_sum = sum(piece.astype(wide) for piece in down_came)
-    mixer_out_grad = settle(gate_sum[: cols // 2]).reshape(cols, width)
-    gate_sum = settle(gate_sum[cols // 2 :].reshape(2, units, 2 * width)).reshape(2, 2 * units, width)
     down_grad = settle(down_sum).reshape(2 * units, width)
-    qkv_sum = settle(qkv_sum.astype(wide)).reshape(pairs, 3, LANES, width)
-    gate_up_grad = gate_sum.transpose(0, 2, 1)
-    mixer_in_grad = qkv_sum.transpose(1, 3, 0, 2).reshape(3, width, cols)
-
-    _, unit_a, factor_a = rms_parts(token_rows, gain_first)
-    tokens_grad = state_grad + rms_back(normed_a_grad, unit_a, factor_a, gain_first)
-
-    gain_wide = gain_low.astype(wide)
+    weights_sum = sum(piece.astype(wide) for piece in gate_came)
+    mixer_out_grad = settle(weights_sum[: cols // 2]).reshape(cols, width)
+    gate_up_grad = settle(weights_sum[cols // 2 :].reshape(2, units, 2 * width))
+    gate_up_grad = gate_up_grad.reshape(2, 2 * units, width).transpose(0, 2, 1)
+
     gain_parts = jnp.stack(
         [
             jnp.sum(qkv_low.astype(wide) * mixer_in_grad, axis=(0, 2)),
             jnp.sum(gates_low.astype(wide) * gate_up_grad, axis=(0, 2)),
         ]
     )
-    gains_grad = jnp.sum(to_line(gain_parts / gain_wide, line), axis=0)
+    gains_grad = sum(exchange_turned(jnp.broadcast_to(gain_parts, (line, 2, width)), place))
+    gains_grad = gains_grad / gain_low.astype(wide)
+    first_grad = jnp.concatenate([mixed_first[1], mixed_second[1]], axis=1)
     return (
         block_out,
         tokens_grad,

time: 526 us -> 503 us (0.956)
  Pallas kernels: 136 us -> 155 us
  other arithmetic: 75.6 us -> 59.8 us
  matrix products: 20.9 us -> 10.7 us
  waiting for transfers between devices: 160 us -> 151 us
  local copies, waits for them, and re-layouts: 25.6 us -> 18.2 us
    ppermute x6 -> x9, waiting for transfers between devices: 45.2 us -> 11.2 us  [exchange_turned(): lax.ppermute(piece, 'head', [(k, (k + j) % count) for k in range(count)])]
    all_to_all x7 -> x6, waiting for transfers between devices: 38.3 us -> 58.1 us  [exchange(): return lax.all_to_all(pieces, 'head', split_axis=0, concat_axis=0)]
    pallas_call x0 -> x3, Pallas kernels: none -> 18.1 us  [the longest x1 7.19 us: turn(): pl.pallas_call(turn_kernel, grid_spec=spec, out_shape=[jax.ShapeDtypeStru...]
    all_to_all x7 -> x6, starting transfers between devices: 35.4 us -> 23.5 us  [exchange(): return lax.all_to_all(pieces, 'head', split_axis=0, concat_axis=0)]
    ppermute x6 -> x9, starting transfers between devices: 9.67 us -> 21 us  [exchange_turned(): lax.ppermute(piece, 'head', [(k, (k + j) % count) for k in range(count)])]
    dot_general x3 -> x0, matrix products: 10.4 us -> none  [the longest x2 5.96 us: shards(): jnp.einsum('td,zcd->ztc', branch_grad, outs[:, pair], preferred_element_t...]
    concatenate x1 -> x2, other arithmetic: 8.53 us -> 1.56 us  [the longest x1 0.98 us: shards(): weights = jnp.concatenate([own_rows, qkv_sides])]
    add x3 -> x2, other arithmetic: 8.57 us -> 2.64 us  [the longest x1 1.33 us: shards(): weights_sum = sum((piece.astype(wide) for piece in gate_came))]
  transfers between devices with their start and end apart: 50 -> 54, of which waited for: 24 -> 24; matrix products, arithmetic and copies ran while one was open for 20% -> 16% of each run, Pallas kernels for 17% -> 30%
where the time goes in v1:
time: 503 us; the launch traced here: 494 us
  Pallas kernels  155 us (31%)
  waiting for transfers between devices  151 us (30%)
  starting transfers between devices  84.4 us (17%)
  other arithmetic  59.8 us (12%)
  local copies, waits for them, and re-layouts  18.2 us (4%)
  between operations  15.5 us (3%)
  matrix products  10.7 us (2%)
    all_to_all x6, waiting for transfers between devices, exchange(): return lax.all_to_all(pieces, 'head', split_axis=0, concat_axis=0)  58.1 us
    pallas_call x2, Pallas kernels, attend_back(): pl.pallas_call(attend_back_kernel, grid_spec=spec, out_shape=[jax.ShapeDt...  42.1 us
    pallas_call x1, Pallas kernels, feed(): pl.pallas_call(feed_kernel, grid_spec=spec, out_shape=[jax.ShapeDtypeStru...  38.7 us
    ppermute x12, waiting for transfers between devices, plane(): lax.ppermute(slot[:end], 'chip', [(c, c ^ away) for c in range(chips)])  30.4 us
    pallas_call x2, Pallas kernels, attend(): pl.pallas_call(attend_kernel, grid_spec=spec, out_shape=[jax.ShapeDtypeSt...  24.1 us
    all_to_all x6, starting transfers between devices, exchange(): return lax.all_to_all(pieces, 'head', split_axis=0, concat_axis=0)  23.5 us
    ppermute x4, waiting for transfers between devices, hop(): lax.ppermute(ends[0], 'head', [(0, 1), (1, 2), (2, 3)])  22.3 us
    ppermute x9, starting transfers between devices, exchange_turned(): lax.ppermute(piece, 'head', [(k, (k + j) % count) for k in range(count)])  21 us
  transfers between devices with their start and end apart: 54, of which 24 were waited for; matrix products, arithmetic and copies ran while one was open for 16% of the time, Pallas kernels for 30%

profile of v1, /device:TPU:0, one launch (start us, length us, event | category | flops | bytes accessed | tf_op | source)
XLA Modules:
  0.0 494.1 jit_solution(14012997856312875026)
XLA Ops:
  7.2 5.1 %collective-permute-start = (bf16[512,1024]{1,0:T(8,128)(2,1)}, bf16[512,1024]{1,0:T(8,128)(2,1)S(1)}, u32[]{:S(2)}, u32[]{:S(2)}) collective-permute-start(bf16[512,1024]{1,0:T(8,128)(2,1)} %x_ref.3), channel_id=1, source_target_pairs={{0,1},{1,2},{2,3},{4,5},{5,6},{6,7},{8,9},{9,10},{10,11},{12,13},{... | collective-permute-start | bytes 3145736 | tf_op jit(solution)/shard_map/ppermute | solution.py:663
  13.7 1.9 convert_element_type.95
  23.4 11.6 %collective-permute-done.right_ref = bf16[512,1024]{1,0:T(8,128)(2,1)S(1)} collective-permute-done((bf16[512,1024]{1,0:T(8,128)(2,1)}, bf16[512,1024]{1,0:T(8,128)(2,1)S(1)}, u32[]{:S(2)}, u32[]{:S(2)}) %collective-permute-start) | collective-permute-done | bytes 1048608 | tf_op jit(solution)/shard_map/ppermute | solution.py:663
  35.0 4.1 collective-permute-done.1.left_ref
  40.0 4.0 join.1
  44.0 4.7 collective-permute-start.3
  54.3 3.9 fusion.5
  58.2 3.0 pad_maximum_fusion.2
  61.3 4.6 project.4
  65.9 1.9 collective-permute-done.5.refs_1_
  67.8 11.3 %collective-permute-done.6.refs_2_ = bf16[1184,256]{1,0:T(8,128)(2,1)} collective-permute-done((bf16[1184,256]{1,0:T(8,128)(2,1)}, bf16[1184,256]{1,0:T(8,128)(2,1)}, u32[]{:S(2)}, u32[]{:S(2)}) %collective-permute-start.6) | collective-permute-done | bytes 606240 | tf_op jit(solution)/shard_map/ppermute | solution.py:679
  79.1 6.8 %collective-permute-done.3 = bf16[3616,256]{1,0:T(8,128)(2,1)} collective-permute-done((bf16[3616,256]{1,0:T(8,128)(2,1)}, bf16[3616,256]{1,0:T(8,128)(2,1)}, u32[]{:S(2)}, u32[]{:S(2)}) %collective-permute-start.3) | collective-permute-done | bytes 1851424 | tf_op jit(solution)/shard_map/ppermute | solution.py:663
  85.9 5.3 %collective-permute-done.4 = bf16[3616,256]{1,0:T(8,128)(2,1)} collective-permute-done((bf16[3616,256]{1,0:T(8,128)(2,1)}, bf16[3616,256]{1,0:T(8,128)(2,1)}, u32[]{:S(2)}, u32[]{:S(2)}) %collective-permute-start.4) | collective-permute-done | bytes 1851424 | tf_op jit(solution)/shard_map/ppermute | solution.py:664
  91.3 3.5 collective-permute-start.8
  103.7 4.5 project.5
  108.2 2.6 slice_select_fusion.x_ref
  110.8 4.5 project.6
  116.9 10.1 %collective-permute-done.11.refs_6_ = bf16[1184,256]{1,0:T(8,128)(2,1)S(1)} collective-permute-done((bf16[1184,256]{1,0:T(8,128)(2,1)S(1)}, bf16[1184,256]{1,0:T(8,128)(2,1)S(1)}, u32[]{:S(2)}, u32[]{:S(2)}) %collective-permute-start.11) | collective-permute-done | bytes 606240 | tf_op jit(solution)/shard_map/ppermute | solution.py:679
  126.9 3.9 collective-permute-done.8
  130.8 5.4 %collective-permute-done.9 = bf16[3616,256]{1,0:T(8,128)(2,1)} collective-permute-done((bf16[3616,256]{1,0:T(8,128)(2,1)}, bf16[3616,256]{1,0:T(8,128)(2,1)}, u32[]{:S(2)}, u32[]{:S(2)}) %collective-permute-start.9) | collective-permute-done | bytes 1851424 | tf_op jit(solution)/shard_map/ppermute | solution.py:664
  136.2 2.6 broadcast_select_fusion.4
  142.4 2.4 collective-permute-start.13
  146.1 2.9 select_select_fusion.x_ref
  148.9 4.5 project.7
  153.5 12.1 %attend.2 = (bf16[2048,128]{1,0:T(8,128)(2,1)}, f32[2048,128]{1,0:T(8,128)}, f32[8,2048]{1,0:T(8,128)}) custom-call(s32[1]{0:T(128)S(6)} %copy.79.len_ref, bf16[2048,256]{1,0:T(8,128)(2,1)} %get-tuple-element.213.q_ref, bf16[2048,256]{1,0:T(8,128)(2,1)} %get-tuple-element.214.k_ref, bf16[2048,256]{1,0:T(8,128)(2,1)} %get-tuple-element.215.v_ref), custom_call_target="tpu_custom_call" | custom-call | flops 4294967296 | bytes 4194304 | tf_op jit(solution)/shard_map/attend/pallas_call | solution.py:200
  165.6 3.9 all-to-all-start
  169.5 1.8 select_select_fusion.1
  178.2 12.1 %attend.3 = (bf16[2048,128]{1,0:T(8,128)(2,1)}, f32[2048,128]{1,0:T(8,128)}, f32[8,2048]{1,0:T(8,128)}) custom-call(s32[1]{0:T(128)S(6)} %copy.79.len_ref, bf16[2048,256]{1,0:T(8,128)(2,1)} %get-tuple-element.213.q_ref, bf16[2048,256]{1,0:T(8,128)(2,1)} %get-tuple-element.214.k_ref, bf16[2048,256]{1,0:T(8,128)(2,1)} %get-tuple-element.215.v_ref), custom_call_target="tpu_custom_call" | custom-call | flops 4294967296 | bytes 4194304 | tf_op jit(solution)/shard_map/attend/pallas_call | solution.py:200
  190.3 5.6 %collective-permute-done.19.refs_14_ = bf16[1184,256]{1,0:T(8,128)(2,1)} collective-permute-done((bf16[1184,256]{1,0:T(8,128)(2,1)S(1)}, bf16[1184,256]{1,0:T(8,128)(2,1)}, u32[]{:S(2)}, u32[]{:S(2)}) %collective-permute-start.19) | collective-permute-done | bytes 606240 | tf_op jit(solution)/shard_map/ppermute | solution.py:679
  195.9 3.0 collect.1
  198.9 3.0 line_up.1
  202.1 4.7 all-to-all-start.1
  207.8 2.5 broadcast_select_fusion.2
  210.2 11.8 %all-to-all-done.1 = bf16[4,512,128]{2,1,0:T(8,128)(2,1)} async-done(((bf16[4,512,128]{2,1,0:T(8,128)(2,1)}), bf16[4,512,128]{2,1,0:T(8,128)(2,1)}, u32[]{:S(2)}, u32[]{:S(2)}) %all-to-all-start.1) | async-done | bytes 524320 | tf_op jit(solution)/shard_map/all_to_all | solution.py:725
  222.1 3.1 multiply_reduce_fusion
  226.6 4.3 collective-permute-done.22.refs_17_
  230.9 38.7 %feed.1 = (f32[512,1024]{1,0:T(8,128)}, f32[512,1024]{1,0:T(8,128)}, f32[512,1024]{1,0:T(8,128)}, f32[512,1024]{1,0:T(8,128)}, bf16[4,4,832,256]{3,2,1,0:T(8,128)(2,1)}, /*index=5*/bf16[4,4,352,256]{3,2,1,0:T(8,128)(2,1)}) custom-call(s32[4]{0:T(128)} %pad_add_fusion.1.order, s32[4]{0:T(128)} %iota_xor_fusion.which, ...), custom_call_target="tpu_custom_call" | custom-call | flops 26575110144 | bytes 31457280 | tf_op jit(solution)/shard_map/feed/pallas_call | solution.py:425
  270.8 2.2 maximum_bitcast_fusion
  273.0 2.5 copy.55
  277.0 7.2 %turn.1 = (f32[512,1024]{1,0:T(8,128)}, bf16[512,1024]{1,0:T(8,128)(2,1)}, bf16[4,512,128]{2,1,0:T(8,128)(2,1)}, bf16[4,512,128]{2,1,0:T(8,128)(2,1)}) custom-call(s32[2]{0:T(128)} %pad_add_fusion.facts, f32[512,1024]{1,0:T(8,128)} %get-tuple-element.239.own_ref, f32[512,1024]{1,0:T(8,128)} %collective-permute-done.24.came_ref, f32[512,1024]{1,0:T(8,128)} %copy-done, ...), custom_call_target="tpu_custom_call" | custom-call | flops 1073741824 | bytes 13631488 | tf_op jit(solution)/shard_map/turn/pallas_call | solution.py:561
  284.2 2.6 convolution_convert_fusion
  289.0 2.5 broadcast_select_fusion
  291.4 4.1 all-to-all-start.2
  295.7 4.0 add_convert_fusion
  303.1 5.8 %reduce-scatter.7.cloned.1.call-done = bf16[1,4,352,256]{3,2,1,0:T(8,128)(2,1)} async-done(((bf16[4,4,352,256]{3,2,1,0:T(8,128)(2,1)}), bf16[1,4,352,256]{3,2,1,0:T(8,128)(2,1)}) %reduce-scatter.7.cloned.1.call-update) | async-done | bytes 720912
  308.9 2.2 all-to-all-done.2
  312.3 2.0 collective-permute-start.28
  314.3 1.8 collective-permute-start.29
  316.1 3.5 all-to-all-start.3
  319.7 21.1 %attend_back.2 = (bf16[2048,384]{1,0:T(8,128)(2,1)}, f32[2048,128]{1,0:T(8,128)}) custom-call(s32[1]{0:T(128)S(6)} %copy.79.len_ref, bf16[2048,256]{1,0:T(8,128)(2,1)} %get-tuple-element.213.q_ref, bf16[2048,256]{1,0:T(8,128)(2,1)} %get-tuple-element.214.k_ref, bf16[2048,256]{1,0:T(8,128)(2,1)} %get-tuple-element.215.v_ref, ...), custom_call_target="tpu_custom_call" | custom-call | flops 10737418240 | bytes 6291456 | tf_op jit(solution)/shard_map/attend_back/pallas_call | solution.py:309
  342.3 3.6 all-to-all-start.4
  345.9 21.1 %attend_back.3 = (bf16[2048,384]{1,0:T(8,128)(2,1)}, f32[2048,128]{1,0:T(8,128)}) custom-call(s32[1]{0:T(128)S(6)} %copy.79.len_ref, bf16[2048,256]{1,0:T(8,128)(2,1)} %get-tuple-element.213.q_ref, bf16[2048,256]{1,0:T(8,128)(2,1)} %get-tuple-element.214.k_ref, bf16[2048,256]{1,0:T(8,128)(2,1)} %get-tuple-element.215.v_ref, bf16[2048,128]{1,0:T(8,128)(2,1)} %bitcast.134, ...), custom_call_target="tpu_custom_call" | custom-call | flops 10737418240 | bytes 6291456 | tf_op jit(solution)/shard_map/attend_back/pallas_call | solution.py:309
  367.0 15.4 %all-to-all-done.4 = bf16[4,512,384]{2,1,0:T(8,128)(2,1)S(1)} async-done(((bf16[4,512,384]{2,1,0:T(8,128)(2,1)}), bf16[4,512,384]{2,1,0:T(8,128)(2,1)S(1)}, u32[]{:S(2)}, u32[]{:S(2)}) %all-to-all-start.4) | async-done | bytes 1572896 | tf_op jit(solution)/shard_map/all_to_all | solution.py:725
  383.6 3.6 all-to-all-start.5
  389.6 7.6 %unproject.1 = bf16[768,1024]{1,0:T(8,128)(2,1)} custom-call(bf16[2048,1024]{1,0:T(8,128)(2,1)} %get-tuple-element.269.normed_ref, bf16[2048,384]{1,0:T(8,128)(2,1)} %get-tuple-element.261.refs_0_, bf16[2048,384]{1,0:T(8,128)(2,1)} %get-tuple-element.267.refs_1_), custom_call_target="tpu_custom_call" | custom-call | tf_op jit(solution)/shard_map/unproject/pallas_call | solution.py:600
  399.1 5.0 %fusion.1.part_ref = f32[512,1024]{1,0:T(8,128)} fusion(bf16[4,512,384]{2,1,0:T(8,128)(2,1)S(1)} %copy-done.23, bf16[4,2,384,1024]{3,2,1,0:T(8,128)(2,1)} %bitcast.142), kind=kOutput, calls=%fused_computation.10 | convolution fusion | flops 1610612736 | bytes 6815744 | tf_op jit(solution)/shard_map/ztc,zcd->td/dot_general | solution.py:907
  404.2 2.6 dynamic-slice_bitcast_fusion
  406.8 2.0 collective-permute-start.30
  408.7 2.4 collective-permute-start.31
  411.1 1.6 collective-permute-start.32
  415.8 27.1 %all-to-all-done.5.came_ref = bf16[4,512,384]{2,1,0:T(8,128)(2,1)S(1)} async-done(((bf16[4,512,384]{2,1,0:T(8,128)(2,1)}), bf16[4,512,384]{2,1,0:T(8,128)(2,1)S(1)}, u32[]{:S(2)}, u32[]{:S(2)}) %all-to-all-start.5) | async-done | bytes 1572896 | tf_op jit(solution)/shard_map/all_to_all | solution.py:725
  442.9 9.2 %collective-permute-done.31 = bf16[832,256]{1,0:T(8,128)(2,1)} collective-permute-done((bf16[832,256]{1,0:T(8,128)(2,1)}, bf16[832,256]{1,0:T(8,128)(2,1)}, u32[]{:S(2)}, u32[]{:S(2)}) %collective-permute-start.31) | collective-permute-done | bytes 426016 | tf_op jit(solution)/shard_map/ppermute | solution.py:734
  459.7 7.0 %finish.1 = f32[512,1024]{1,0:T(8,128)} custom-call(bf16[4,512,384]{2,1,0:T(8,128)(2,1)} %copy-done.21, bf16[4,2,384,1024]{3,2,1,0:T(8,128)(2,1)} %bitcast.143, f32[512,1024]{1,0:T(8,128)} %fusion.1.part_ref, bf16[512,1024]{1,0:T(8,128)(2,1)} %x_ref.3, bf16[784,1024]{1,0:T(8,128)(2,1)} %all-gather.3.cloned.1.call-done.w_ref.gain_ref, ...), custom_call_target="tpu_custom_call" | custom-call | flops 274877906944 | bytes 10485760 | tf_op jit(solution)/shard_map/finish/pallas_call | solution.py:628
  473.0 8.7 %collective-permute-start.41 = (f32[2,128]{1,0:T(2,128)S(1)}, f32[2,128]{1,0:T(2,128)S(1)}, u32[]{:S(2)}, u32[]{:S(2)}) collective-permute-start(f32[2,128]{1,0:T(2,128)S(1)} %pad_maximum_fusion.12), channel_id=1, source_target_pairs={{0,1},{1,2},{2,3},{3,0},{4,5},{5,6},{6,7},{7,4},{8,9},{9,10},{10,1... | collective-permute-start | bytes 3080 | tf_op jit(solution)/shard_map/ppermute | solution.py:734
  (221 shorter events, 78.7 us)
Async XLA Ops:
  7.2 12.2 %copy-start.24 = (f32[3,128,256]{2,1,0:T(8,128)S(1)}, f32[3,128,256]{2,1,0:T(8,128)}, u32[]{:S(2)}) copy-start(f32[3,128,256]{2,1,0:T(8,128)} %param.13) | copy-start | bytes 1179652
  7.2 54.1 %all-gather.3.cloned.1.call-start = ((), (), s32[]{:S(2)}) async-start(), calls=%async_computation.8 | async-start | bytes 1806336 | tf_op jit(solution)/shard_map/all_gather | solution.py:779
  7.2 27.8 %collective-permute-start = (bf16[512,1024]{1,0:T(8,128)(2,1)}, bf16[512,1024]{1,0:T(8,128)(2,1)S(1)}, u32[]{:S(2)}, u32[]{:S(2)}) collective-permute-start(bf16[512,1024]{1,0:T(8,128)(2,1)} %x_ref.3), channel_id=1, source_target_pairs={{0,1},{1,2},{2,3},{4,5},{5,6},{6,7},{8,9},{9,10},{10,11},{12,13},{... | collective-permute-start | bytes 3145736 | tf_op jit(solution)/shard_map/ppermute | solution.py:663
  12.4 26.7 %collective-permute-start.1 = (bf16[512,1024]{1,0:T(8,128)(2,1)}, bf16[512,1024]{1,0:T(8,128)(2,1)S(1)}, u32[]{:S(2)}, u32[]{:S(2)}) collective-permute-start(bf16[512,1024]{1,0:T(8,128)(2,1)} %x_ref.3), channel_id=1, source_target_pairs={{1,0},{2,1},{3,2},{5,4},{6,5},{7,6},{9,8},{10,9},{11,10},{13,12},{... | collective-permute-start | bytes 3145736 | tf_op jit(solution)/shard_map/ppermute | solution.py:664
  19.4 1.9 collective-permute-start.2
  44.0 41.9 %collective-permute-start.3 = (bf16[3616,256]{1,0:T(8,128)(2,1)}, bf16[3616,256]{1,0:T(8,128)(2,1)}, u32[]{:S(2)}, u32[]{:S(2)}) collective-permute-start(bf16[3616,256]{1,0:T(8,128)(2,1)} %get-tuple-element.154), channel_id=1, source_target_pairs={{0,1},{1,2},{2,3},{4,5},{5,6},{6,7},{8,9},{9,10},{10,11},{12,13},{... | collective-permute-start | bytes 5554184 | tf_op jit(solution)/shard_map/ppermute | solution.py:663
  48.7 42.6 %collective-permute-start.4 = (bf16[3616,256]{1,0:T(8,128)(2,1)}, bf16[3616,256]{1,0:T(8,128)(2,1)}, u32[]{:S(2)}, u32[]{:S(2)}) collective-permute-start(bf16[3616,256]{1,0:T(8,128)(2,1)} %get-tuple-element.155), channel_id=1, source_target_pairs={{1,0},{2,1},{3,2},{5,4},{6,5},{7,6},{9,8},{10,9},{11,10},{13,12},{... | collective-permute-start | bytes 5554184 | tf_op jit(solution)/shard_map/ppermute | solution.py:664
  50.9 16.9 %collective-permute-start.5 = (bf16[1184,256]{1,0:T(8,128)(2,1)}, bf16[1184,256]{1,0:T(8,128)(2,1)}, u32[]{:S(2)}, u32[]{:S(2)}) collective-permute-start(bf16[1184,256]{1,0:T(8,128)(2,1)} %pad_maximum_fusion.5.refs_0_), channel_id=1, source_target_pairs={{0,8},{8,0},{16,24},{24,16},{1,9},{9,1},{17,25},{25,17},{2,10},{10... | collective-permute-start | bytes 1818632 | tf_op jit(solution)/shard_map/ppermute | solution.py:679
  52.4 26.7 %collective-permute-start.6 = (bf16[1184,256]{1,0:T(8,128)(2,1)}, bf16[1184,256]{1,0:T(8,128)(2,1)}, u32[]{:S(2)}, u32[]{:S(2)}) collective-permute-start(bf16[1184,256]{1,0:T(8,128)(2,1)} %pad_maximum_fusion.5.refs_0_), channel_id=1, source_target_pairs={{0,16},{8,24},{16,0},{24,8},{1,17},{9,25},{17,1},{25,9},{2,18},{10... | collective-permute-start | bytes 1818632 | tf_op jit(solution)/shard_map/ppermute | solution.py:679
  53.9 25.2 %collective-permute-start.7 = (bf16[1184,256]{1,0:T(8,128)(2,1)}, bf16[1184,256]{1,0:T(8,128)(2,1)}, u32[]{:S(2)}, u32[]{:S(2)}) collective-permute-start(bf16[1184,256]{1,0:T(8,128)(2,1)} %pad_maximum_fusion.5.refs_0_), channel_id=1, source_target_pairs={{0,24},{8,16},{16,8},{24,0},{1,25},{9,17},{17,9},{25,1},{2,26},{10... | collective-permute-start | bytes 1818632 | tf_op jit(solution)/shard_map/ppermute | solution.py:679
  61.3 36.3 %copy-start.8 = (bf16[512,1024]{1,0:T(8,128)(2,1)S(1)}, bf16[512,1024]{1,0:T(8,128)(2,1)}, u32[]{:S(2)}) copy-start(bf16[512,1024]{1,0:T(8,128)(2,1)} %copy-done.7) | copy-start | bytes 3145732
  61.3 36.3 %copy-start.10 = (bf16[512,1024]{1,0:T(8,128)(2,1)S(1)}, bf16[512,1024]{1,0:T(8,128)(2,1)}, u32[]{:S(2)}) copy-start(bf16[512,1024]{1,0:T(8,128)(2,1)} %copy-done.9) | copy-start | bytes 3145732
  91.3 39.5 %collective-permute-start.8 = (bf16[3616,256]{1,0:T(8,128)(2,1)}, bf16[3616,256]{1,0:T(8,128)(2,1)}, u32[]{:S(2)}, u32[]{:S(2)}) collective-permute-start(bf16[3616,256]{1,0:T(8,128)(2,1)} %collective-permute-done.3), channel_id=1, source_target_pairs={{0,1},{1,2},{2,3},{4,5},{5,6},{6,7},{8,9},{9,10},{10,11},{12,13},{... | collective-permute-start | bytes 5554184 | tf_op jit(solution)/shard_map/ppermute | solution.py:663
  94.8 41.4 %collective-permute-start.9 = (bf16[3616,256]{1,0:T(8,128)(2,1)}, bf16[3616,256]{1,0:T(8,128)(2,1)}, u32[]{:S(2)}, u32[]{:S(2)}) collective-permute-start(bf16[3616,256]{1,0:T(8,128)(2,1)} %collective-permute-done.4), channel_id=1, source_target_pairs={{1,0},{2,1},{3,2},{5,4},{6,5},{7,6},{9,8},{10,9},{11,10},{13,12},{... | collective-permute-start | bytes 5554184 | tf_op jit(solution)/shard_map/ppermute | solution.py:664
  100.2 16.7 %collective-permute-start.10 = (bf16[1184,256]{1,0:T(8,128)(2,1)S(1)}, bf16[1184,256]{1,0:T(8,128)(2,1)S(1)}, u32[]{:S(2)}, u32[]{:S(2)}) collective-permute-start(bf16[1184,256]{1,0:T(8,128)(2,1)S(1)} %slice.139.refs_4_), channel_id=1, source_target_pairs={{0,8},{8,0},{16,24},{24,16},{1,9},{9,1},{17,25},{25,17},{2,10},{10... | collective-permute-start | bytes 1818632 | tf_op jit(solution)/shard_map/ppermute | solution.py:679
  101.7 25.2 %collective-permute-start.11 = (bf16[1184,256]{1,0:T(8,128)(2,1)S(1)}, bf16[1184,256]{1,0:T(8,128)(2,1)S(1)}, u32[]{:S(2)}, u32[]{:S(2)}) collective-permute-start(bf16[1184,256]{1,0:T(8,128)(2,1)S(1)} %slice.139.refs_4_), channel_id=1, source_target_pairs={{0,16},{8,24},{16,0},{24,8},{1,17},{9,25},{17,1},{25,9},{2,18},{10... | collective-permute-start | bytes 1818632 | tf_op jit(solution)/shard_map/ppermute | solution.py:679
  103.2 23.7 %collective-permute-start.12 = (bf16[1184,256]{1,0:T(8,128)(2,1)S(1)}, bf16[1184,256]{1,0:T(8,128)(2,1)}, u32[]{:S(2)}, u32[]{:S(2)}) collective-permute-start(bf16[1184,256]{1,0:T(8,128)(2,1)S(1)} %slice.139.refs_4_), channel_id=1, source_target_pairs={{0,24},{8,16},{16,8},{24,0},{1,25},{9,17},{17,9},{25,1},{2,26},{10... | collective-permute-start | bytes 1818632 | tf_op jit(solution)/shard_map/ppermute | solution.py:679
  116.8 19.4 %copy-start.32 = (bf16[1184,256]{1,0:T(8,128)(2,1)}, bf16[1184,256]{1,0:T(8,128)(2,1)S(1)}, u32[]{:S(2)}) copy-start(bf16[1184,256]{1,0:T(8,128)(2,1)S(1)} %collective-permute-done.10.refs_5_) | copy-start | bytes 1818628
  138.8 26.7 %collective-permute-start.15 = (bf16[1184,256]{1,0:T(8,128)(2,1)S(1)}, bf16[1184,256]{1,0:T(8,128)(2,1)}, u32[]{:S(2)}, u32[]{:S(2)}) collective-permute-start(bf16[1184,256]{1,0:T(8,128)(2,1)S(1)} %slice.140.refs_8_), channel_id=1, source_target_pairs={{0,8},{8,0},{16,24},{24,16},{1,9},{9,1},{17,25},{25,17},{2,10},{10... | collective-permute-start | bytes 1818632 | tf_op jit(solution)/shard_map/ppermute | solution.py:679
  140.4 25.1 %collective-permute-start.16 = (bf16[1184,256]{1,0:T(8,128)(2,1)S(1)}, bf16[1184,256]{1,0:T(8,128)(2,1)}, u32[]{:S(2)}, u32[]{:S(2)}) collective-permute-start(bf16[1184,256]{1,0:T(8,128)(2,1)S(1)} %slice.140.refs_8_), channel_id=1, source_target_pairs={{0,16},{8,24},{16,0},{24,8},{1,17},{9,25},{17,1},{25,9},{2,18},{10... | collective-permute-start | bytes 1818632 | tf_op jit(solution)/shard_map/ppermute | solution.py:679
  141.9 23.6 %collective-permute-start.17 = (bf16[1184,256]{1,0:T(8,128)(2,1)S(1)}, bf16[1184,256]{1,0:T(8,128)(2,1)}, u32[]{:S(2)}, u32[]{:S(2)}) collective-permute-start(bf16[1184,256]{1,0:T(8,128)(2,1)S(1)} %slice.140.refs_8_), channel_id=1, source_target_pairs={{0,24},{8,16},{16,8},{24,0},{1,25},{9,17},{17,9},{25,1},{2,26},{10... | collective-permute-start | bytes 1818632 | tf_op jit(solution)/shard_map/ppermute | solution.py:679
  142.4 23.2 %collective-permute-start.13 = (bf16[1568,256]{1,0:T(8,128)(2,1)}, bf16[1568,256]{1,0:T(8,128)(2,1)}, u32[]{:S(2)}, u32[]{:S(2)}) collective-permute-start(bf16[1568,256]{1,0:T(8,128)(2,1)} %get-tuple-element.289), channel_id=1, source_target_pairs={{0,1},{1,2},{2,3},{4,5},{5,6},{6,7},{8,9},{9,10},{10,11},{12,13},{... | collective-permute-start | bytes 2408456 | tf_op jit(solution)/shard_map/ppermute | solution.py:663
  144.8 20.8 %collective-permute-start.14 = (bf16[1568,256]{1,0:T(8,128)(2,1)S(1)}, bf16[1568,256]{1,0:T(8,128)(2,1)}, u32[]{:S(2)}, u32[]{:S(2)}) collective-permute-start(bf16[1568,256]{1,0:T(8,128)(2,1)S(1)} %get-tuple-element.290), channel_id=1, source_target_pairs={{1,0},{2,1},{3,2},{5,4},{6,5},{7,6},{9,8},{10,9},{11,10},{13,12},{... | collective-permute-start | bytes 2408456 | tf_op jit(solution)/shard_map/ppermute | solution.py:664
  165.6 30.3 %all-to-all-start = ((bf16[4,512,128]{2,1,0:T(8,128)(2,1)}), bf16[4,512,128]{2,1,0:T(8,128)(2,1)S(1)}, u32[]{:S(2)}, u32[]{:S(2)}) async-start(bf16[4,512,128]{2,1,0:T(8,128)(2,1)} %bitcast.133), calls=%async_computation | async-start | bytes 1048576 | tf_op jit(solution)/shard_map/all_to_all | solution.py:725
  169.5 107.5 %all-gather.5.cloned.1.call-start = ((), (), s32[]{:S(2)}) async-start(), calls=%async_computation.9 | async-start | bytes 7077888 | tf_op jit(solution)/shard_map/all_gather | solution.py:832
  171.3 19.0 %copy-start.18 = (bf16[1184,256]{1,0:T(8,128)(2,1)}, bf16[1184,256]{1,0:T(8,128)(2,1)S(1)}, u32[]{:S(2)}) copy-start(bf16[1184,256]{1,0:T(8,128)(2,1)S(1)} %slice.141.refs_12_) | copy-start | bytes 1818628
  171.3 19.0 %collective-permute-start.18 = (bf16[1184,256]{1,0:T(8,128)(2,1)S(1)}, bf16[1184,256]{1,0:T(8,128)(2,1)}, u32[]{:S(2)}, u32[]{:S(2)}) collective-permute-start(bf16[1184,256]{1,0:T(8,128)(2,1)S(1)} %slice.141.refs_12_), channel_id=1, source_target_pairs={{0,8},{8,0},{16,24},{24,16},{1,9},{9,1},{17,25},{25,17},{2,10},{10... | collective-permute-start | bytes 1818632 | tf_op jit(solution)/shard_map/ppermute | solution.py:679
  172.8 23.1 %collective-permute-start.19 = (bf16[1184,256]{1,0:T(8,128)(2,1)S(1)}, bf16[1184,256]{1,0:T(8,128)(2,1)}, u32[]{:S(2)}, u32[]{:S(2)}) collective-permute-start(bf16[1184,256]{1,0:T(8,128)(2,1)S(1)} %slice.141.refs_12_), channel_id=1, source_target_pairs={{0,16},{8,24},{16,0},{24,8},{1,17},{9,25},{17,1},{25,9},{2,18},{10... | collective-permute-start | bytes 1818632 | tf_op jit(solution)/shard_map/ppermute | solution.py:679
  174.4 21.5 %collective-permute-start.20 = (bf16[1184,256]{1,0:T(8,128)(2,1)S(1)}, bf16[1184,256]{1,0:T(8,128)(2,1)}, u32[]{:S(2)}, u32[]{:S(2)}) collective-permute-start(bf16[1184,256]{1,0:T(8,128)(2,1)S(1)} %slice.141.refs_12_), channel_id=1, source_target_pairs={{0,24},{8,16},{16,8},{24,0},{1,25},{9,17},{17,9},{25,1},{2,26},{10... | collective-permute-start | bytes 1818632 | tf_op jit(solution)/shard_map/ppermute | solution.py:679
  202.0 5.7 %collective-permute-start.21 = (bf16[4,1,128,1024]{3,2,1,0:T(8,128)(2,1)S(1)}, bf16[4,1,128,1024]{3,2,1,0:T(8,128)(2,1)}, u32[]{:S(2)}, u32[]{:S(2)}) collective-permute-start(bf16[4,1,128,1024]{3,2,1,0:T(8,128)(2,1)S(1)} %bitcast.110), channel_id=1, source_target_pairs={{0,4},{4,0},{1,5},{5,1},{2,6},{6,2},{3,7},{7,3},{8,12},{12,8},{9,1... | collective-permute-start | bytes 3145736 | tf_op jit(solution)/shard_map/ppermute | solution.py:740
  202.1 20.0 %all-to-all-start.1 = ((bf16[4,512,128]{2,1,0:T(8,128)(2,1)}), bf16[4,512,128]{2,1,0:T(8,128)(2,1)}, u32[]{:S(2)}, u32[]{:S(2)}) async-start(bf16[4,512,128]{2,1,0:T(8,128)(2,1)} %bitcast.16), calls=%async_computation.1 | async-start | bytes 1048576 | tf_op jit(solution)/shard_map/all_to_all | solution.py:725
  206.8 102.1 %reduce-scatter.7.cloned.1.call-start = ((), (), s32[]{:S(2)}) async-start(), calls=%async_computation.10 | async-start | bytes 3604480
  206.8 19.8 %collective-permute-start.23 = (bf16[512,1024]{1,0:T(8,128)(2,1)}, bf16[512,1024]{1,0:T(8,128)(2,1)}, u32[]{:S(2)}, u32[]{:S(2)}) collective-permute-start(bf16[512,1024]{1,0:T(8,128)(2,1)} %c_ref.1), channel_id=1, source_target_pairs={{0,4},{4,0},{1,5},{5,1},{2,6},{6,2},{3,7},{7,3},{8,12},{12,8},{9,1... | collective-permute-start | bytes 3145736 | tf_op jit(solution)/shard_map/ppermute | solution.py:740
  207.7 14.3 %copy-start.20 = (bf16[4,512,128]{2,1,0:T(8,128)(2,1)S(1)}, bf16[4,512,128]{2,1,0:T(8,128)(2,1)}, u32[]{:S(2)}) copy-start(bf16[4,512,128]{2,1,0:T(8,128)(2,1)} %copy-done.19) | copy-start | bytes 1572868
  225.1 44.5 %copy-start = (f32[512,1024]{1,0:T(8,128)}, f32[512,1024]{1,0:T(8,128)S(1)}, u32[]{:S(2)}) copy-start(f32[512,1024]{1,0:T(8,128)S(1)} %get-tuple-element.322.state_ref) | copy-start | bytes 6291460
  226.6 4.3 collective-permute-start.22
  269.7 7.3 %collective-permute-start.24 = (f32[512,1024]{1,0:T(8,128)}, f32[512,1024]{1,0:T(8,128)}, u32[]{:S(2)}, u32[]{:S(2)}) collective-permute-start(f32[512,1024]{1,0:T(8,128)} %get-tuple-element.240), channel_id=1, source_target_pairs={{0,4},{4,0},{1,5},{5,1},{2,6},{6,2},{3,7},{7,3},{8,12},{12,8},{9,1... | collective-permute-start | bytes 6291464 | tf_op jit(solution)/shard_map/ppermute | solution.py:740
  269.9 25.8 %collective-permute-start.26 = (f32[512,1024]{1,0:T(8,128)}, f32[512,1024]{1,0:T(8,128)}, u32[]{:S(2)}, u32[]{:S(2)}) collective-permute-start(f32[512,1024]{1,0:T(8,128)} %get-tuple-element.252), channel_id=1, source_target_pairs={{0,4},{4,0},{1,5},{5,1},{2,6},{6,2},{3,7},{7,3},{8,12},{12,8},{9,1... | collective-permute-start | bytes 6291464 | tf_op jit(solution)/shard_map/ppermute | solution.py:740
  291.4 8.2 %collective-permute-start.25 = (bf16[4,128,1024]{1,2,0:T(8,128)(2,1)}, bf16[4,128,1024]{1,2,0:T(8,128)(2,1)}, u32[]{:S(2)}, u32[]{:S(2)}) collective-permute-start(bf16[4,128,1024]{1,2,0:T(8,128)(2,1)} %broadcast_select_fusion), channel_id=1, source_target_pairs={{0,4},{4,0},{1,5},{5,1},{2,6},{6,2},{3,7},{7,3},{8,12},{12,8},{9,1... | collective-permute-start | bytes 3145736 | tf_op jit(solution)/shard_map/ppermute | solution.py:740
  291.4 19.7 %all-to-all-start.2 = ((bf16[4,512,128]{2,1,0:T(8,128)(2,1)}), bf16[4,512,128]{2,1,0:T(8,128)(2,1)}, u32[]{:S(2)}, u32[]{:S(2)}) async-start(bf16[4,512,128]{2,1,0:T(8,128)(2,1)} %get-tuple-element.246), calls=%async_computation.2 | async-start | bytes 1048576 | tf_op jit(solution)/shard_map/all_to_all | solution.py:725
  295.6 108.6 %reduce-scatter.9.cloned.1.call-start = ((), (), s32[]{:S(2)}) async-start(), calls=%async_computation.11 | async-start | bytes 8519680
  312.2 28.5 %collective-permute-start.27 = (bf16[352,256]{1,0:T(8,128)(2,1)S(1)}, bf16[352,256]{1,0:T(8,128)(2,1)S(1)}, u32[]{:S(2)}, u32[]{:S(2)}) collective-permute-start(bf16[352,256]{1,0:T(8,128)(2,1)S(1)} %get-tuple-element.306), channel_id=1, source_target_pairs={{0,1},{1,2},{2,3},{3,0},{4,5},{5,6},{6,7},{7,4},{8,9},{9,10},{10,1... | collective-permute-start | bytes 540680 | tf_op jit(solution)/shard_map/ppermute | solution.py:734
  312.3 28.4 %collective-permute-start.28 = (bf16[352,256]{1,0:T(8,128)(2,1)S(1)}, bf16[352,256]{1,0:T(8,128)(2,1)S(1)}, u32[]{:S(2)}, u32[]{:S(2)}) collective-permute-start(bf16[352,256]{1,0:T(8,128)(2,1)S(1)} %get-tuple-element.305), channel_id=1, source_target_pairs={{0,2},{1,3},{2,0},{3,1},{4,6},{5,7},{6,4},{7,5},{8,10},{9,11},{10,... | collective-permute-start | bytes 540680 | tf_op jit(solution)/shard_map/ppermute | solution.py:734
  314.3 26.4 %collective-permute-start.29 = (bf16[352,256]{1,0:T(8,128)(2,1)S(1)}, bf16[352,256]{1,0:T(8,128)(2,1)S(1)}, u32[]{:S(2)}, u32[]{:S(2)}) collective-permute-start(bf16[352,256]{1,0:T(8,128)(2,1)S(1)} %get-tuple-element.304), channel_id=1, source_target_pairs={{0,3},{1,0},{2,1},{3,2},{4,7},{5,4},{6,5},{7,6},{8,11},{9,8},{10,9... | collective-permute-start | bytes 540680 | tf_op jit(solution)/shard_map/ppermute | solution.py:734
  316.1 26.2 %all-to-all-start.3 = ((bf16[4,512,128]{2,1,0:T(8,128)(2,1)}), bf16[4,512,128]{2,1,0:T(8,128)(2,1)S(1)}, u32[]{:S(2)}, u32[]{:S(2)}) async-start(bf16[4,512,128]{2,1,0:T(8,128)(2,1)} %get-tuple-element.254), calls=%async_computation.3 | async-start | bytes 1048576 | tf_op jit(solution)/shard_map/all_to_all | solution.py:725
  342.3 40.1 %all-to-all-start.4 = ((bf16[4,512,384]{2,1,0:T(8,128)(2,1)}), bf16[4,512,384]{2,1,0:T(8,128)(2,1)S(1)}, u32[]{:S(2)}, u32[]{:S(2)}) async-start(bf16[4,512,384]{2,1,0:T(8,128)(2,1)} %bitcast.108), calls=%async_computation.4 | async-start | bytes 3145728 | tf_op jit(solution)/shard_map/all_to_all | solution.py:725
  383.6 59.3 %all-to-all-start.5 = ((bf16[4,512,384]{2,1,0:T(8,128)(2,1)}), bf16[4,512,384]{2,1,0:T(8,128)(2,1)S(1)}, u32[]{:S(2)}, u32[]{:S(2)}) async-start(bf16[4,512,384]{2,1,0:T(8,128)(2,1)} %bitcast.107), calls=%async_computation.5 | async-start | bytes 3145728 | tf_op jit(solution)/shard_map/all_to_all | solution.py:725
  387.3 1.5 collective-permute-start.40
  398.8 15.4 %collective-permute-start.33 = (bf16[384,1024]{1,0:T(8,128)(2,1)S(1)}, bf16[384,1024]{1,0:T(8,128)(2,1)}, u32[]{:S(2)}, u32[]{:S(2)}) collective-permute-start(bf16[384,1024]{1,0:T(8,128)(2,1)S(1)} %broadcast_select_fusion.6), channel_id=1, source_target_pairs={{0,4},{4,0},{1,5},{5,1},{2,6},{6,2},{3,7},{7,3},{8,12},{12,8},{9,1... | collective-permute-start | bytes 2359304 | tf_op jit(solution)/shard_map/ppermute | solution.py:740
  406.8 36.2 %collective-permute-start.30 = (bf16[832,256]{1,0:T(8,128)(2,1)}, bf16[832,256]{1,0:T(8,128)(2,1)S(1)}, u32[]{:S(2)}, u32[]{:S(2)}) collective-permute-start(bf16[832,256]{1,0:T(8,128)(2,1)} %get-tuple-element.293), channel_id=1, source_target_pairs={{0,1},{1,2},{2,3},{3,0},{4,5},{5,6},{6,7},{7,4},{8,9},{9,10},{10,1... | collective-permute-start | bytes 1277960 | tf_op jit(solution)/shard_map/ppermute | solution.py:734
  408.7 43.4 %collective-permute-start.31 = (bf16[832,256]{1,0:T(8,128)(2,1)}, bf16[832,256]{1,0:T(8,128)(2,1)}, u32[]{:S(2)}, u32[]{:S(2)}) collective-permute-start(bf16[832,256]{1,0:T(8,128)(2,1)} %get-tuple-element.292), channel_id=1, source_target_pairs={{0,2},{1,3},{2,0},{3,1},{4,6},{5,7},{6,4},{7,5},{8,10},{9,11},{10,... | collective-permute-start | bytes 1277960 | tf_op jit(solution)/shard_map/ppermute | solution.py:734
  411.1 41.1 %collective-permute-start.32 = (bf16[832,256]{1,0:T(8,128)(2,1)}, bf16[832,256]{1,0:T(8,128)(2,1)}, u32[]{:S(2)}, u32[]{:S(2)}) collective-permute-start(bf16[832,256]{1,0:T(8,128)(2,1)} %get-tuple-element.291), channel_id=1, source_target_pairs={{0,3},{1,0},{2,1},{3,2},{4,7},{5,4},{6,5},{7,6},{8,11},{9,8},{10,9... | collective-permute-start | bytes 1277960 | tf_op jit(solution)/shard_map/ppermute | solution.py:734
  415.8 39.5 %copy-start.13 = (bf16[384,1024]{1,0:T(8,128)(2,1)}, bf16[384,1024]{1,0:T(8,128)(2,1)S(1)}, u32[]{:S(2)}) copy-start(bf16[384,1024]{1,0:T(8,128)(2,1)S(1)} %add_convert_fusion.2) | copy-start | bytes 2359300
  455.3 15.1 %collective-permute-start.39 = (f32[2,352,128]{2,1,0:T(8,128)}, f32[2,352,128]{2,1,0:T(8,128)}, u32[]{:S(2)}, u32[]{:S(2)}) collective-permute-start(f32[2,352,128]{2,1,0:T(8,128)} %slice_select_fusion.1), channel_id=1, source_target_pairs={{0,4},{4,0},{1,5},{5,1},{2,6},{6,2},{3,7},{7,3},{8,12},{12,8},{9,1... | collective-permute-start | bytes 1081352 | tf_op jit(solution)/shard_map/ppermute | solution.py:740
  456.2 11.4 %collective-permute-start.34 = (bf16[384,256]{1,0:T(8,128)(2,1)}, bf16[384,256]{1,0:T(8,128)(2,1)}, u32[]{:S(2)}, u32[]{:S(2)}) collective-permute-start(bf16[384,256]{1,0:T(8,128)(2,1)} %get-tuple-element.301), channel_id=1, source_target_pairs={{0,8},{8,0},{16,24},{24,16},{1,9},{9,1},{17,25},{25,17},{2,10},{10... | collective-permute-start | bytes 589832 | tf_op jit(solution)/shard_map/ppermute | solution.py:861
  457.2 10.5 %collective-permute-start.35 = (bf16[384,256]{1,0:T(8,128)(2,1)}, bf16[384,256]{1,0:T(8,128)(2,1)}, u32[]{:S(2)}, u32[]{:S(2)}) collective-permute-start(bf16[384,256]{1,0:T(8,128)(2,1)} %get-tuple-element.303), channel_id=1, source_target_pairs={{0,16},{8,24},{16,0},{24,8},{1,17},{9,25},{17,1},{25,9},{2,18},{10... | collective-permute-start | bytes 589832 | tf_op jit(solution)/shard_map/ppermute | solution.py:861
  458.0 10.9 %collective-permute-start.36 = (bf16[384,256]{1,0:T(8,128)(2,1)}, bf16[384,256]{1,0:T(8,128)(2,1)}, u32[]{:S(2)}, u32[]{:S(2)}) collective-permute-start(bf16[384,256]{1,0:T(8,128)(2,1)} %get-tuple-element.302), channel_id=1, source_target_pairs={{0,24},{8,16},{16,8},{24,0},{1,25},{9,17},{17,9},{25,1},{2,26},{10... | collective-permute-start | bytes 589832 | tf_op jit(solution)/shard_map/ppermute | solution.py:861
  459.7 7.0 %collective-permute-start.38 = (f32[128,128]{1,0:T(8,128)}, f32[128,128]{1,0:T(8,128)}, u32[]{:S(2)}, u32[]{:S(2)}) collective-permute-start(f32[128,128]{1,0:T(8,128)} %slice_select_fusion.7), channel_id=1, source_target_pairs={{0,4},{4,0},{1,5},{5,1},{2,6},{6,2},{3,7},{7,3},{8,12},{12,8},{9,1... | collective-permute-start | bytes 196616 | tf_op jit(solution)/shard_map/ppermute | solution.py:740
  470.3 1.5 collective-permute-start.37
  471.8 14.9 %copy-start.38 = (f32[2,128]{1,0:T(2,128)S(1)}, f32[2,128]{1,0:T(2,128)}, u32[]{:S(2)}) copy-start(f32[2,128]{1,0:T(2,128)} %param.17) | copy-start | bytes 3076
  472.9 14.4 %copy-start.26 = (f32[3,128,256]{2,1,0:T(8,128)}, f32[3,128,256]{2,1,0:T(8,128)S(1)}, u32[]{:S(2)}) copy-start(f32[3,128,256]{2,1,0:T(8,128)S(1)} %reshape.162) | copy-start | bytes 1179652
  473.0 11.8 %collective-permute-start.41 = (f32[2,128]{1,0:T(2,128)S(1)}, f32[2,128]{1,0:T(2,128)S(1)}, u32[]{:S(2)}, u32[]{:S(2)}) collective-permute-start(f32[2,128]{1,0:T(2,128)S(1)} %pad_maximum_fusion.12), channel_id=1, source_target_pairs={{0,1},{1,2},{2,3},{3,0},{4,5},{5,6},{6,7},{7,4},{8,9},{9,10},{10,1... | collective-permute-start | bytes 3080 | tf_op jit(solution)/shard_map/ppermute | solution.py:734
  481.7 4.5 collective-permute-start.42
  483.2 3.6 collective-permute-start.43
  (29 other events, 135.6 us)
Sparse Core Ops, SparseCore 0:
  20.5 28.4 all-gather.2
  202.1 46.8 all-gather.4
  269.8 39.0 reduce-scatter.6
  311.7 74.6 reduce-scatter.8

commit v2 on v1

--- a/solution.py
+++ b/solution.py
@@ -574,6 +574,38 @@
     )(facts, own, came, hidden_state, cotangent, pack, out_full)
 
 
+def outer_kernel(core, first_ref, second_ref, grad_ref, kept_ref, given_ref):
+    grad = grad_ref[...]
+    first = dot_tn(first_ref[0], grad).astype(low)
+    second = dot_tn(second_ref[0], grad).astype(low)
+    lower = core[0] == 0
+    kept_ref[0] = jnp.where(lower, first, second)
+    given_ref[0] = jnp.where(lower, second, first)
+
+
+def outer(core, attended_pieces, branch_grad):
+    line, rows, width = attended_pieces[0].shape
+    depth = branch_grad.shape[1]
+    piece = pl.BlockSpec((1, rows, width), lambda z, c: (z, 0, 0))
+    out = pl.BlockSpec((1, width, depth), lambda z, c: (z, 0, 0))
+    spec = pltpu.PrefetchScalarGridSpec(
+        num_scalar_prefetch=1,
+        grid=(line,),
+        in_specs=[piece, piece, pl.BlockSpec((rows, depth), lambda z, c: (0, 0))],
+        out_specs=[out, out],
+    )
+    return pl.pallas_call(
+        outer_kernel,
+        grid_spec=spec,
+        out_shape=[jax.ShapeDtypeStruct((line, width, depth), low)] * 2,
+        compiler_params=pltpu.CompilerParams(vmem_limit_bytes=VMEM_BYTES),
+        cost_estimate=pl.CostEstimate(
+            flops=4 * line * rows * width * depth, bytes_accessed=4 << 20, transcendentals=0
+        ),
+        name="outer",
+    )(core, *attended_pieces, branch_grad)
+
+
 def unproject_kernel(normed_ref, *refs):
     mixed_refs, (dw_ref, acc_ref) = refs[:-2], refs[-2:]
     step = pl.program_id(0)
@@ -716,8 +748,10 @@
     slots.append(farthest(weight_hops))
     planes.append(plane(slots[3]))
     more, used = then(1, used)
+    later = more[0]
     planes, more, sent = barrier((planes, more, sent))
-    sent.append(send(more[0]))
+    sent.append(send(barrier((later, sent[0]))[0]))
+    planes, sent = barrier((planes, sent))
     return planes, slots, used, [made, more], sent
 
 
@@ -876,8 +910,7 @@
         )
 
     came = exchange(asked[0])
-    out_grad = dot_tn(attended, branch_grad).astype(low).reshape(line, cols, depth)
-    kept, given = halves(out_grad, 1)
+    kept, given = outer(core[None].astype(jnp.int32), attended_pieces, branch_grad)
     out_grad = (kept.astype(wide) + other_core(given).astype(wide)).astype(low)
     out_grad = jnp.moveaxis(out_grad.reshape(line, cols // 2, chips, 2 * width), 2, 0)
     gate_grad = spread(gate_grad).at[:, :, : cols // 2].set(out_grad)

time: 503 us -> 501 us (level)
  other arithmetic: 59.8 us -> 51.4 us
  waiting for transfers between devices: 151 us -> 157 us
  local copies, waits for them, and re-layouts: 18.2 us -> 12.9 us
    unnamed x6, waiting for transfers between devices: 5.82 us -> 13.9 us
    all_to_all x6, waiting for transfers between devices: 58.1 us -> 50.3 us  [exchange(): return lax.all_to_all(pieces, 'head', split_axis=0, concat_axis=0)]
    pallas_call x0 -> x1, Pallas kernels: none -> 5.16 us  [outer(): pl.pallas_call(outer_kernel, grid_spec=spec, out_shape=[jax.ShapeDtypeStr...]
  transfers between devices with their start and end apart: 54 -> 54, of which waited for: 24 -> 26; matrix products, arithmetic and copies ran while one was open for 16% -> 12% of each run, Pallas kernels for 30% -> 31%
where the time goes in v2:
time: 501 us; the launch traced here: 493 us
  Pallas kernels  159 us (32%)
  waiting for transfers between devices  157 us (31%)
  starting transfers between devices  88 us (18%)
  other arithmetic  51.4 us (10%)
  between operations  15.7 us (3%)
  local copies, waits for them, and re-layouts  12.9 us (3%)
  matrix products  7.86 us (2%)
    all_to_all x6, waiting for transfers between devices, exchange(): return lax.all_to_all(pieces, 'head', split_axis=0, concat_axis=0)  50.3 us
    pallas_call x2, Pallas kernels, attend_back(): pl.pallas_call(attend_back_kernel, grid_spec=spec, out_shape=[jax.ShapeDt...  42.2 us
    pallas_call x1, Pallas kernels, feed(): pl.pallas_call(feed_kernel, grid_spec=spec, out_shape=[jax.ShapeDtypeStru...  38.4 us
    ppermute x12, waiting for transfers between devices, plane(): lax.ppermute(slot[:end], 'chip', [(c, c ^ away) for c in range(chips)])  34.1 us
    all_to_all x6, starting transfers between devices, exchange(): return lax.all_to_all(pieces, 'head', split_axis=0, concat_axis=0)  24.2 us
    pallas_call x2, Pallas kernels, attend(): pl.pallas_call(attend_kernel, grid_spec=spec, out_shape=[jax.ShapeDtypeSt...  24.1 us
    ppermute x4, waiting for transfers between devices, hop(): lax.ppermute(ends[0], 'head', [(0, 1), (1, 2), (2, 3)])  22.6 us
    ppermute x9, starting transfers between devices, exchange_turned(): lax.ppermute(piece, 'head', [(k, (k + j) % count) for k in range(count)])  22.5 us
  transfers between devices with their start and end apart: 54, of which 26 were waited for; matrix products, arithmetic and copies ran while one was open for 12% of the time, Pallas kernels for 31%

profile of v2, /device:TPU:0, one launch (start us, length us, event | category | flops | bytes accessed | tf_op | source)
XLA Modules:
  0.0 492.7 jit_solution(10567915715690575229)
XLA Ops:
  7.2 5.1 %collective-permute-start = (bf16[512,1024]{1,0:T(8,128)(2,1)}, bf16[512,1024]{1,0:T(8,128)(2,1)S(1)}, u32[]{:S(2)}, u32[]{:S(2)}) collective-permute-start(bf16[512,1024]{1,0:T(8,128)(2,1)} %x_ref.3), channel_id=1, source_target_pairs={{0,1},{1,2},{2,3},{4,5},{5,6},{6,7},{8,9},{9,10},{10,11},{12,13},{... | collective-permute-start | bytes 3145736 | tf_op jit(solution)/shard_map/ppermute | solution.py:695
  13.7 1.9 convert_element_type.92
  23.4 11.6 %collective-permute-done.right_ref = bf16[512,1024]{1,0:T(8,128)(2,1)S(1)} collective-permute-done((bf16[512,1024]{1,0:T(8,128)(2,1)}, bf16[512,1024]{1,0:T(8,128)(2,1)S(1)}, u32[]{:S(2)}, u32[]{:S(2)}) %collective-permute-start) | collective-permute-done | bytes 1048608 | tf_op jit(solution)/shard_map/ppermute | solution.py:695
  35.0 4.1 collective-permute-done.1.left_ref
  40.0 4.0 join.1
  44.0 4.7 collective-permute-start.3
  54.3 3.9 fusion.7
  58.2 3.0 pad_maximum_fusion.2
  61.3 4.6 project.4
  65.9 1.9 collective-permute-done.5.refs_1_
  67.8 11.3 %collective-permute-done.6.refs_2_ = bf16[1184,256]{1,0:T(8,128)(2,1)} collective-permute-done((bf16[1184,256]{1,0:T(8,128)(2,1)}, bf16[1184,256]{1,0:T(8,128)(2,1)}, u32[]{:S(2)}, u32[]{:S(2)}) %collective-permute-start.6) | collective-permute-done | bytes 606240 | tf_op jit(solution)/shard_map/ppermute | solution.py:711
  79.1 6.8 %collective-permute-done.3 = bf16[3616,256]{1,0:T(8,128)(2,1)} collective-permute-done((bf16[3616,256]{1,0:T(8,128)(2,1)}, bf16[3616,256]{1,0:T(8,128)(2,1)}, u32[]{:S(2)}, u32[]{:S(2)}) %collective-permute-start.3) | collective-permute-done | bytes 1851424 | tf_op jit(solution)/shard_map/ppermute | solution.py:695
  85.9 5.3 %collective-permute-done.4 = bf16[3616,256]{1,0:T(8,128)(2,1)} collective-permute-done((bf16[3616,256]{1,0:T(8,128)(2,1)}, bf16[3616,256]{1,0:T(8,128)(2,1)}, u32[]{:S(2)}, u32[]{:S(2)}) %collective-permute-start.4) | collective-permute-done | bytes 1851424 | tf_op jit(solution)/shard_map/ppermute | solution.py:696
  91.3 3.5 collective-permute-start.8
  94.8 1.7 collective-permute-start.9
  99.9 1.6 collective-permute-start.10
  103.4 4.5 project.5
  107.9 2.6 slice_select_fusion.x_ref
  110.5 4.5 project.6
  116.6 10.1 %collective-permute-done.11.refs_6_ = bf16[1184,256]{1,0:T(8,128)(2,1)S(1)} collective-permute-done((bf16[1184,256]{1,0:T(8,128)(2,1)S(1)}, bf16[1184,256]{1,0:T(8,128)(2,1)S(1)}, u32[]{:S(2)}, u32[]{:S(2)}) %collective-permute-start.11) | collective-permute-done | bytes 606240 | tf_op jit(solution)/shard_map/ppermute | solution.py:711
  126.7 4.2 collective-permute-done.8
  130.8 5.4 %collective-permute-done.9 = bf16[3616,256]{1,0:T(8,128)(2,1)} collective-permute-done((bf16[3616,256]{1,0:T(8,128)(2,1)}, bf16[3616,256]{1,0:T(8,128)(2,1)}, u32[]{:S(2)}, u32[]{:S(2)}) %collective-permute-start.9) | collective-permute-done | bytes 1851424 | tf_op jit(solution)/shard_map/ppermute | solution.py:696
  136.2 2.6 broadcast_select_fusion.3
  142.4 2.4 collective-permute-start.13
  146.1 2.9 select_select_fusion.x_ref
  148.9 4.5 project.7
  153.5 12.1 %attend.2 = (bf16[2048,128]{1,0:T(8,128)(2,1)}, f32[2048,128]{1,0:T(8,128)}, f32[8,2048]{1,0:T(8,128)}) custom-call(s32[1]{0:T(128)S(6)} %copy.71.len_ref, bf16[2048,256]{1,0:T(8,128)(2,1)} %get-tuple-element.233.q_ref, bf16[2048,256]{1,0:T(8,128)(2,1)} %get-tuple-element.234.k_ref, bf16[2048,256]{1,0:T(8,128)(2,1)} %get-tuple-element.235.v_ref), custom_call_target="tpu_custom_call" | custom-call | flops 4294967296 | bytes 4194304 | tf_op jit(solution)/shard_map/attend/pallas_call | solution.py:200
  165.6 4.1 all-to-all-start
  169.7 1.8 select_select_fusion.1
  175.1 12.1 %attend.3 = (bf16[2048,128]{1,0:T(8,128)(2,1)}, f32[2048,128]{1,0:T(8,128)}, f32[8,2048]{1,0:T(8,128)}) custom-call(s32[1]{0:T(128)S(6)} %copy.71.len_ref, bf16[2048,256]{1,0:T(8,128)(2,1)} %get-tuple-element.233.q_ref, bf16[2048,256]{1,0:T(8,128)(2,1)} %get-tuple-element.234.k_ref, bf16[2048,256]{1,0:T(8,128)(2,1)} %get-tuple-element.235.v_ref), custom_call_target="tpu_custom_call" | custom-call | flops 4294967296 | bytes 4194304 | tf_op jit(solution)/shard_map/attend/pallas_call | solution.py:200
  188.4 8.2 %collective-permute-done.19.refs_14_ = bf16[1184,256]{1,0:T(8,128)(2,1)} collective-permute-done((bf16[1184,256]{1,0:T(8,128)(2,1)S(1)}, bf16[1184,256]{1,0:T(8,128)(2,1)}, u32[]{:S(2)}, u32[]{:S(2)}) %collective-permute-start.19) | collective-permute-done | bytes 606240 | tf_op jit(solution)/shard_map/ppermute | solution.py:711
  196.5 4.8 all-to-all-start.1
  205.1 6.4 %all-to-all-done.1.second_ref = bf16[4,512,128]{2,1,0:T(8,128)(2,1)S(1)} async-done(((bf16[4,512,128]{2,1,0:T(8,128)(2,1)}), bf16[4,512,128]{2,1,0:T(8,128)(2,1)S(1)}, u32[]{:S(2)}, u32[]{:S(2)}) %all-to-all-start.1) | async-done | bytes 524320 | tf_op jit(solution)/shard_map/all_to_all | solution.py:759
  211.6 3.0 collect.1
  214.6 3.0 line_up.1
  219.2 2.1 collective-permute-done.21
  221.5 2.8 multiply_reduce_fusion
  225.9 2.7 collective-permute-done.22.refs_17_
  228.5 38.4 %feed.1 = (f32[512,1024]{1,0:T(8,128)}, f32[512,1024]{1,0:T(8,128)}, f32[512,1024]{1,0:T(8,128)}, f32[512,1024]{1,0:T(8,128)}, bf16[4,4,832,256]{3,2,1,0:T(8,128)(2,1)}, /*index=5*/bf16[4,4,352,256]{3,2,1,0:T(8,128)(2,1)}) custom-call(s32[4]{0:T(128)} %pad_add_fusion.1.order, s32[4]{0:T(128)} %iota_xor_fusion.which, ...), custom_call_target="tpu_custom_call" | custom-call | flops 26575110144 | bytes 31457280 | tf_op jit(solution)/shard_map/feed/pallas_call | solution.py:425
  269.6 1.9 collective-permute-done.24.came_ref
  271.5 6.9 %turn.1 = (f32[512,1024]{1,0:T(8,128)}, bf16[512,1024]{1,0:T(8,128)(2,1)}, bf16[4,512,128]{2,1,0:T(8,128)(2,1)}, bf16[4,512,128]{2,1,0:T(8,128)(2,1)}) custom-call(s32[2]{0:T(128)} %pad_add_fusion.facts, f32[512,1024]{1,0:T(8,128)} %get-tuple-element.277.own_ref, f32[512,1024]{1,0:T(8,128)} %collective-permute-done.24.came_ref, f32[512,1024]{1,0:T(8,128)} %copy-done, ...), custom_call_target="tpu_custom_call" | custom-call | flops 1073741824 | bytes 13631488 | tf_op jit(solution)/shard_map/turn/pallas_call | solution.py:561
  278.4 5.2 %outer.1 = (bf16[4,128,1024]{2,1,0:T(8,128)(2,1)}, bf16[4,128,1024]{2,1,0:T(8,128)(2,1)}) custom-call(s32[1]{0:T(128)} %bitcast.28.core, bf16[4,512,128]{2,1,0:T(8,128)(2,1)} %all-to-all-done.first_ref, bf16[4,512,128]{2,1,0:T(8,128)(2,1)} %copy-done.35, bf16[512,1024]{1,0:T(8,128)(2,1)} %get-tuple-element.286.grad_ref), custom_call_target="tpu_custom_call" | custom-call | flops 1073741824 | bytes 4194304 | tf_op jit(solution)/shard_map/outer/pallas_call | solution.py:597
  283.8 4.1 all-to-all-start.2
  288.2 3.9 add_convert_fusion
  293.7 13.8 %reduce-scatter.7.cloned.1.call-done = bf16[1,4,352,256]{3,2,1,0:T(8,128)(2,1)} async-done(((bf16[4,4,352,256]{3,2,1,0:T(8,128)(2,1)}), bf16[1,4,352,256]{3,2,1,0:T(8,128)(2,1)}) %reduce-scatter.7.cloned.1.call-update) | async-done | bytes 720912
  310.2 2.4 collective-permute-start.28
  314.1 3.5 all-to-all-start.3
  317.6 21.1 %attend_back.2 = (bf16[2048,384]{1,0:T(8,128)(2,1)}, f32[2048,128]{1,0:T(8,128)}) custom-call(s32[1]{0:T(128)S(6)} %copy.71.len_ref, bf16[2048,256]{1,0:T(8,128)(2,1)} %get-tuple-element.233.q_ref, bf16[2048,256]{1,0:T(8,128)(2,1)} %get-tuple-element.234.k_ref, bf16[2048,256]{1,0:T(8,128)(2,1)} %get-tuple-element.235.v_ref, ...), custom_call_target="tpu_custom_call" | custom-call | flops 10737418240 | bytes 6291456 | tf_op jit(solution)/shard_map/attend_back/pallas_call | solution.py:309
  339.7 4.1 all-to-all-start.4
  343.8 21.1 %attend_back.3 = (bf16[2048,384]{1,0:T(8,128)(2,1)}, f32[2048,128]{1,0:T(8,128)}) custom-call(s32[1]{0:T(128)S(6)} %copy.71.len_ref, bf16[2048,256]{1,0:T(8,128)(2,1)} %get-tuple-element.233.q_ref, bf16[2048,256]{1,0:T(8,128)(2,1)} %get-tuple-element.234.k_ref, bf16[2048,256]{1,0:T(8,128)(2,1)} %get-tuple-element.235.v_ref, bf16[2048,128]{1,0:T(8,128)(2,1)} %bitcast.134, ...), custom_call_target="tpu_custom_call" | custom-call | flops 10737418240 | bytes 6291456 | tf_op jit(solution)/shard_map/attend_back/pallas_call | solution.py:309
  364.9 15.8 %all-to-all-done.4 = bf16[4,512,384]{2,1,0:T(8,128)(2,1)S(1)} async-done(((bf16[4,512,384]{2,1,0:T(8,128)(2,1)}), bf16[4,512,384]{2,1,0:T(8,128)(2,1)S(1)}, u32[]{:S(2)}, u32[]{:S(2)}) %all-to-all-start.4) | async-done | bytes 1572896 | tf_op jit(solution)/shard_map/all_to_all | solution.py:759
  381.8 3.6 all-to-all-start.5
  387.8 7.6 %unproject.1 = bf16[768,1024]{1,0:T(8,128)(2,1)} custom-call(bf16[2048,1024]{1,0:T(8,128)(2,1)} %get-tuple-element.309.normed_ref, bf16[2048,384]{1,0:T(8,128)(2,1)} %get-tuple-element.301.refs_0_, bf16[2048,384]{1,0:T(8,128)(2,1)} %get-tuple-element.307.refs_1_), custom_call_target="tpu_custom_call" | custom-call | tf_op jit(solution)/shard_map/unproject/pallas_call | solution.py:632
  395.4 1.6 broadcast_select_fusion.5
  397.3 5.0 %fusion.1.part_ref = f32[512,1024]{1,0:T(8,128)} fusion(bf16[4,512,384]{2,1,0:T(8,128)(2,1)S(1)} %copy-done.21, bf16[4,2,384,1024]{3,2,1,0:T(8,128)(2,1)} %bitcast.142), kind=kOutput, calls=%fused_computation.9 | convolution fusion | flops 1610612736 | bytes 6815744 | tf_op jit(solution)/shard_map/ztc,zcd->td/dot_general | solution.py:940
  402.4 2.6 dynamic-slice_bitcast_fusion
  405.0 2.0 collective-permute-start.30
  406.9 2.4 collective-permute-start.31
  409.3 1.7 collective-permute-start.32
  412.5 1.6 add_convert_fusion.2
  414.1 27.1 %all-to-all-done.5.came_ref = bf16[4,512,384]{2,1,0:T(8,128)(2,1)S(1)} async-done(((bf16[4,512,384]{2,1,0:T(8,128)(2,1)}), bf16[4,512,384]{2,1,0:T(8,128)(2,1)S(1)}, u32[]{:S(2)}, u32[]{:S(2)}) %all-to-all-start.5) | async-done | bytes 1572896 | tf_op jit(solution)/shard_map/all_to_all | solution.py:759
  441.2 9.2 %collective-permute-done.31 = bf16[832,256]{1,0:T(8,128)(2,1)} collective-permute-done((bf16[832,256]{1,0:T(8,128)(2,1)}, bf16[832,256]{1,0:T(8,128)(2,1)}, u32[]{:S(2)}, u32[]{:S(2)}) %collective-permute-start.31) | collective-permute-done | bytes 426016 | tf_op jit(solution)/shard_map/ppermute | solution.py:768
  457.9 7.0 %finish.1 = f32[512,1024]{1,0:T(8,128)} custom-call(bf16[4,512,384]{2,1,0:T(8,128)(2,1)} %copy-done.19, bf16[4,2,384,1024]{3,2,1,0:T(8,128)(2,1)} %bitcast.143, f32[512,1024]{1,0:T(8,128)} %fusion.1.part_ref, bf16[512,1024]{1,0:T(8,128)(2,1)} %x_ref.3, bf16[784,1024]{1,0:T(8,128)(2,1)} %all-gather.3.cloned.1.call-done.w_ref.gain_ref, ...), custom_call_target="tpu_custom_call" | custom-call | flops 274877906944 | bytes 10485760 | tf_op jit(solution)/shard_map/finish/pallas_call | solution.py:660
  471.4 8.7 %collective-permute-start.41 = (f32[2,128]{1,0:T(2,128)S(1)}, f32[2,128]{1,0:T(2,128)S(1)}, u32[]{:S(2)}, u32[]{:S(2)}) collective-permute-start(f32[2,128]{1,0:T(2,128)S(1)} %pad_maximum_fusion.12), channel_id=1, source_target_pairs={{0,1},{1,2},{2,3},{3,0},{4,5},{5,6},{6,7},{7,4},{8,9},{9,10},{10,1... | collective-permute-start | bytes 3080 | tf_op jit(solution)/shard_map/ppermute | solution.py:768
  (214 shorter events, 73.2 us)
Async XLA Ops:
  7.2 12.2 %copy-start.22 = (f32[3,128,256]{2,1,0:T(8,128)S(1)}, f32[3,128,256]{2,1,0:T(8,128)}, u32[]{:S(2)}) copy-start(f32[3,128,256]{2,1,0:T(8,128)} %param.13) | copy-start | bytes 1179652
  7.2 54.1 %all-gather.3.cloned.1.call-start = ((), (), s32[]{:S(2)}) async-start(), calls=%async_computation.8 | async-start | bytes 1806336 | tf_op jit(solution)/shard_map/all_gather | solution.py:813
  7.2 27.8 %collective-permute-start = (bf16[512,1024]{1,0:T(8,128)(2,1)}, bf16[512,1024]{1,0:T(8,128)(2,1)S(1)}, u32[]{:S(2)}, u32[]{:S(2)}) collective-permute-start(bf16[512,1024]{1,0:T(8,128)(2,1)} %x_ref.3), channel_id=1, source_target_pairs={{0,1},{1,2},{2,3},{4,5},{5,6},{6,7},{8,9},{9,10},{10,11},{12,13},{... | collective-permute-start | bytes 3145736 | tf_op jit(solution)/shard_map/ppermute | solution.py:695
  12.4 26.7 %collective-permute-start.1 = (bf16[512,1024]{1,0:T(8,128)(2,1)}, bf16[512,1024]{1,0:T(8,128)(2,1)S(1)}, u32[]{:S(2)}, u32[]{:S(2)}) collective-permute-start(bf16[512,1024]{1,0:T(8,128)(2,1)} %x_ref.3), channel_id=1, source_target_pairs={{1,0},{2,1},{3,2},{5,4},{6,5},{7,6},{9,8},{10,9},{11,10},{13,12},{... | collective-permute-start | bytes 3145736 | tf_op jit(solution)/shard_map/ppermute | solution.py:696
  19.4 1.9 collective-permute-start.2
  44.0 41.9 %collective-permute-start.3 = (bf16[3616,256]{1,0:T(8,128)(2,1)}, bf16[3616,256]{1,0:T(8,128)(2,1)}, u32[]{:S(2)}, u32[]{:S(2)}) collective-permute-start(bf16[3616,256]{1,0:T(8,128)(2,1)} %get-tuple-element.174), channel_id=1, source_target_pairs={{0,1},{1,2},{2,3},{4,5},{5,6},{6,7},{8,9},{9,10},{10,11},{12,13},{... | collective-permute-start | bytes 5554184 | tf_op jit(solution)/shard_map/ppermute | solution.py:695
  48.7 42.6 %collective-permute-start.4 = (bf16[3616,256]{1,0:T(8,128)(2,1)}, bf16[3616,256]{1,0:T(8,128)(2,1)}, u32[]{:S(2)}, u32[]{:S(2)}) collective-permute-start(bf16[3616,256]{1,0:T(8,128)(2,1)} %get-tuple-element.175), channel_id=1, source_target_pairs={{1,0},{2,1},{3,2},{5,4},{6,5},{7,6},{9,8},{10,9},{11,10},{13,12},{... | collective-permute-start | bytes 5554184 | tf_op jit(solution)/shard_map/ppermute | solution.py:696
  50.9 16.9 %collective-permute-start.5 = (bf16[1184,256]{1,0:T(8,128)(2,1)}, bf16[1184,256]{1,0:T(8,128)(2,1)}, u32[]{:S(2)}, u32[]{:S(2)}) collective-permute-start(bf16[1184,256]{1,0:T(8,128)(2,1)} %pad_maximum_fusion.5.refs_0_), channel_id=1, source_target_pairs={{0,8},{8,0},{16,24},{24,16},{1,9},{9,1},{17,25},{25,17},{2,10},{10... | collective-permute-start | bytes 1818632 | tf_op jit(solution)/shard_map/ppermute | solution.py:711
  52.4 26.7 %collective-permute-start.6 = (bf16[1184,256]{1,0:T(8,128)(2,1)}, bf16[1184,256]{1,0:T(8,128)(2,1)}, u32[]{:S(2)}, u32[]{:S(2)}) collective-permute-start(bf16[1184,256]{1,0:T(8,128)(2,1)} %pad_maximum_fusion.5.refs_0_), channel_id=1, source_target_pairs={{0,16},{8,24},{16,0},{24,8},{1,17},{9,25},{17,1},{25,9},{2,18},{10... | collective-permute-start | bytes 1818632 | tf_op jit(solution)/shard_map/ppermute | solution.py:711
  53.9 25.2 %collective-permute-start.7 = (bf16[1184,256]{1,0:T(8,128)(2,1)}, bf16[1184,256]{1,0:T(8,128)(2,1)}, u32[]{:S(2)}, u32[]{:S(2)}) collective-permute-start(bf16[1184,256]{1,0:T(8,128)(2,1)} %pad_maximum_fusion.5.refs_0_), channel_id=1, source_target_pairs={{0,24},{8,16},{16,8},{24,0},{1,25},{9,17},{17,9},{25,1},{2,26},{10... | collective-permute-start | bytes 1818632 | tf_op jit(solution)/shard_map/ppermute | solution.py:711
  61.3 36.0 %copy-start.8 = (bf16[512,1024]{1,0:T(8,128)(2,1)S(1)}, bf16[512,1024]{1,0:T(8,128)(2,1)}, u32[]{:S(2)}) copy-start(bf16[512,1024]{1,0:T(8,128)(2,1)} %copy-done.7) | copy-start | bytes 3145732
  61.3 36.0 %copy-start.10 = (bf16[512,1024]{1,0:T(8,128)(2,1)S(1)}, bf16[512,1024]{1,0:T(8,128)(2,1)}, u32[]{:S(2)}) copy-start(bf16[512,1024]{1,0:T(8,128)(2,1)} %copy-done.9) | copy-start | bytes 3145732
  91.3 39.5 %collective-permute-start.8 = (bf16[3616,256]{1,0:T(8,128)(2,1)}, bf16[3616,256]{1,0:T(8,128)(2,1)}, u32[]{:S(2)}, u32[]{:S(2)}) collective-permute-start(bf16[3616,256]{1,0:T(8,128)(2,1)} %collective-permute-done.3), channel_id=1, source_target_pairs={{0,1},{1,2},{2,3},{4,5},{5,6},{6,7},{8,9},{9,10},{10,11},{12,13},{... | collective-permute-start | bytes 5554184 | tf_op jit(solution)/shard_map/ppermute | solution.py:695
  94.8 41.4 %collective-permute-start.9 = (bf16[3616,256]{1,0:T(8,128)(2,1)}, bf16[3616,256]{1,0:T(8,128)(2,1)}, u32[]{:S(2)}, u32[]{:S(2)}) collective-permute-start(bf16[3616,256]{1,0:T(8,128)(2,1)} %collective-permute-done.4), channel_id=1, source_target_pairs={{1,0},{2,1},{3,2},{5,4},{6,5},{7,6},{9,8},{10,9},{11,10},{13,12},{... | collective-permute-start | bytes 5554184 | tf_op jit(solution)/shard_map/ppermute | solution.py:696
  99.9 16.7 %collective-permute-start.10 = (bf16[1184,256]{1,0:T(8,128)(2,1)S(1)}, bf16[1184,256]{1,0:T(8,128)(2,1)S(1)}, u32[]{:S(2)}, u32[]{:S(2)}) collective-permute-start(bf16[1184,256]{1,0:T(8,128)(2,1)S(1)} %slice.139.refs_4_), channel_id=1, source_target_pairs={{0,8},{8,0},{16,24},{24,16},{1,9},{9,1},{17,25},{25,17},{2,10},{10... | collective-permute-start | bytes 1818632 | tf_op jit(solution)/shard_map/ppermute | solution.py:711
  101.4 25.2 %collective-permute-start.11 = (bf16[1184,256]{1,0:T(8,128)(2,1)S(1)}, bf16[1184,256]{1,0:T(8,128)(2,1)S(1)}, u32[]{:S(2)}, u32[]{:S(2)}) collective-permute-start(bf16[1184,256]{1,0:T(8,128)(2,1)S(1)} %slice.139.refs_4_), channel_id=1, source_target_pairs={{0,16},{8,24},{16,0},{24,8},{1,17},{9,25},{17,1},{25,9},{2,18},{10... | collective-permute-start | bytes 1818632 | tf_op jit(solution)/shard_map/ppermute | solution.py:711
  103.0 23.7 %collective-permute-start.12 = (bf16[1184,256]{1,0:T(8,128)(2,1)S(1)}, bf16[1184,256]{1,0:T(8,128)(2,1)}, u32[]{:S(2)}, u32[]{:S(2)}) collective-permute-start(bf16[1184,256]{1,0:T(8,128)(2,1)S(1)} %slice.139.refs_4_), channel_id=1, source_target_pairs={{0,24},{8,16},{16,8},{24,0},{1,25},{9,17},{17,9},{25,1},{2,26},{10... | collective-permute-start | bytes 1818632 | tf_op jit(solution)/shard_map/ppermute | solution.py:711
  116.6 19.6 %copy-start.31 = (bf16[1184,256]{1,0:T(8,128)(2,1)}, bf16[1184,256]{1,0:T(8,128)(2,1)S(1)}, u32[]{:S(2)}) copy-start(bf16[1184,256]{1,0:T(8,128)(2,1)S(1)} %collective-permute-done.10.refs_5_) | copy-start | bytes 1818628
  138.8 26.7 %collective-permute-start.15 = (bf16[1184,256]{1,0:T(8,128)(2,1)S(1)}, bf16[1184,256]{1,0:T(8,128)(2,1)}, u32[]{:S(2)}, u32[]{:S(2)}) collective-permute-start(bf16[1184,256]{1,0:T(8,128)(2,1)S(1)} %slice.140.refs_8_), channel_id=1, source_target_pairs={{0,8},{8,0},{16,24},{24,16},{1,9},{9,1},{17,25},{25,17},{2,10},{10... | collective-permute-start | bytes 1818632 | tf_op jit(solution)/shard_map/ppermute | solution.py:711
  140.4 25.1 %collective-permute-start.16 = (bf16[1184,256]{1,0:T(8,128)(2,1)S(1)}, bf16[1184,256]{1,0:T(8,128)(2,1)}, u32[]{:S(2)}, u32[]{:S(2)}) collective-permute-start(bf16[1184,256]{1,0:T(8,128)(2,1)S(1)} %slice.140.refs_8_), channel_id=1, source_target_pairs={{0,16},{8,24},{16,0},{24,8},{1,17},{9,25},{17,1},{25,9},{2,18},{10... | collective-permute-start | bytes 1818632 | tf_op jit(solution)/shard_map/ppermute | solution.py:711
  141.9 23.6 %collective-permute-start.17 = (bf16[1184,256]{1,0:T(8,128)(2,1)S(1)}, bf16[1184,256]{1,0:T(8,128)(2,1)}, u32[]{:S(2)}, u32[]{:S(2)}) collective-permute-start(bf16[1184,256]{1,0:T(8,128)(2,1)S(1)} %slice.140.refs_8_), channel_id=1, source_target_pairs={{0,24},{8,16},{16,8},{24,0},{1,25},{9,17},{17,9},{25,1},{2,26},{10... | collective-permute-start | bytes 1818632 | tf_op jit(solution)/shard_map/ppermute | solution.py:711
  142.4 23.2 %collective-permute-start.13 = (bf16[1568,256]{1,0:T(8,128)(2,1)}, bf16[1568,256]{1,0:T(8,128)(2,1)}, u32[]{:S(2)}, u32[]{:S(2)}) collective-permute-start(bf16[1568,256]{1,0:T(8,128)(2,1)} %get-tuple-element.327), channel_id=1, source_target_pairs={{0,1},{1,2},{2,3},{4,5},{5,6},{6,7},{8,9},{9,10},{10,11},{12,13},{... | collective-permute-start | bytes 2408456 | tf_op jit(solution)/shard_map/ppermute | solution.py:695
  144.8 20.8 %collective-permute-start.14 = (bf16[1568,256]{1,0:T(8,128)(2,1)S(1)}, bf16[1568,256]{1,0:T(8,128)(2,1)}, u32[]{:S(2)}, u32[]{:S(2)}) collective-permute-start(bf16[1568,256]{1,0:T(8,128)(2,1)S(1)} %get-tuple-element.328), channel_id=1, source_target_pairs={{1,0},{2,1},{3,2},{5,4},{6,5},{7,6},{9,8},{10,9},{11,10},{13,12},{... | collective-permute-start | bytes 2408456 | tf_op jit(solution)/shard_map/ppermute | solution.py:696
  165.6 30.9 %all-to-all-start = ((bf16[4,512,128]{2,1,0:T(8,128)(2,1)}), bf16[4,512,128]{2,1,0:T(8,128)(2,1)}, u32[]{:S(2)}, u32[]{:S(2)}) async-start(bf16[4,512,128]{2,1,0:T(8,128)(2,1)} %bitcast.132), calls=%async_computation | async-start | bytes 1048576 | tf_op jit(solution)/shard_map/all_to_all | solution.py:759
  171.6 15.6 %copy-start.18 = (bf16[1184,256]{1,0:T(8,128)(2,1)}, bf16[1184,256]{1,0:T(8,128)(2,1)S(1)}, u32[]{:S(2)}) copy-start(bf16[1184,256]{1,0:T(8,128)(2,1)S(1)} %slice.141.refs_12_) | copy-start | bytes 1818628
  171.6 16.8 %collective-permute-start.18 = (bf16[1184,256]{1,0:T(8,128)(2,1)S(1)}, bf16[1184,256]{1,0:T(8,128)(2,1)}, u32[]{:S(2)}, u32[]{:S(2)}) collective-permute-start(bf16[1184,256]{1,0:T(8,128)(2,1)S(1)} %slice.141.refs_12_), channel_id=1, source_target_pairs={{0,8},{8,0},{16,24},{24,16},{1,9},{9,1},{17,25},{25,17},{2,10},{10... | collective-permute-start | bytes 1818632 | tf_op jit(solution)/shard_map/ppermute | solution.py:711
  173.1 23.4 %collective-permute-start.19 = (bf16[1184,256]{1,0:T(8,128)(2,1)S(1)}, bf16[1184,256]{1,0:T(8,128)(2,1)}, u32[]{:S(2)}, u32[]{:S(2)}) collective-permute-start(bf16[1184,256]{1,0:T(8,128)(2,1)S(1)} %slice.141.refs_12_), channel_id=1, source_target_pairs={{0,16},{8,24},{16,0},{24,8},{1,17},{9,25},{17,1},{25,9},{2,18},{10... | collective-permute-start | bytes 1818632 | tf_op jit(solution)/shard_map/ppermute | solution.py:711
  174.6 21.9 %collective-permute-start.20 = (bf16[1184,256]{1,0:T(8,128)(2,1)S(1)}, bf16[1184,256]{1,0:T(8,128)(2,1)}, u32[]{:S(2)}, u32[]{:S(2)}) collective-permute-start(bf16[1184,256]{1,0:T(8,128)(2,1)S(1)} %slice.141.refs_12_), channel_id=1, source_target_pairs={{0,24},{8,16},{16,8},{24,0},{1,25},{9,17},{17,9},{25,1},{2,26},{10... | collective-permute-start | bytes 1818632 | tf_op jit(solution)/shard_map/ppermute | solution.py:711
  196.5 15.0 %all-to-all-start.1 = ((bf16[4,512,128]{2,1,0:T(8,128)(2,1)}), bf16[4,512,128]{2,1,0:T(8,128)(2,1)S(1)}, u32[]{:S(2)}, u32[]{:S(2)}) async-start(bf16[4,512,128]{2,1,0:T(8,128)(2,1)} %bitcast.133), calls=%async_computation.1 | async-start | bytes 1048576 | tf_op jit(solution)/shard_map/all_to_all | solution.py:759
  201.3 70.2 %all-gather.5.cloned.1.call-start = ((), (), s32[]{:S(2)}) async-start(), calls=%async_computation.9 | async-start | bytes 7077888 | tf_op jit(solution)/shard_map/all_gather | solution.py:866
  217.7 89.9 %reduce-scatter.7.cloned.1.call-start = ((), (), s32[]{:S(2)}) async-start(), calls=%async_computation.10 | async-start | bytes 3604480
  217.9 3.4 collective-permute-start.21
  218.0 7.9 %collective-permute-start.23 = (bf16[512,1024]{1,0:T(8,128)(2,1)}, bf16[512,1024]{1,0:T(8,128)(2,1)}, u32[]{:S(2)}, u32[]{:S(2)}) collective-permute-start(bf16[512,1024]{1,0:T(8,128)(2,1)} %c_ref.1), channel_id=1, source_target_pairs={{0,4},{4,0},{1,5},{5,1},{2,6},{6,2},{3,7},{7,3},{8,12},{12,8},{9,1... | collective-permute-start | bytes 3145736 | tf_op jit(solution)/shard_map/ppermute | solution.py:774
  224.3 42.6 %copy-start = (f32[512,1024]{1,0:T(8,128)}, f32[512,1024]{1,0:T(8,128)S(1)}, u32[]{:S(2)}) copy-start(f32[512,1024]{1,0:T(8,128)S(1)} %get-tuple-element.360.state_ref) | copy-start | bytes 6291460
  225.7 2.8 collective-permute-start.22
  266.9 4.6 collective-permute-start.24
  267.1 21.1 %collective-permute-start.26 = (f32[512,1024]{1,0:T(8,128)}, f32[512,1024]{1,0:T(8,128)}, u32[]{:S(2)}, u32[]{:S(2)}) collective-permute-start(f32[512,1024]{1,0:T(8,128)} %get-tuple-element.292), channel_id=1, source_target_pairs={{0,4},{4,0},{1,5},{5,1},{2,6},{6,2},{3,7},{7,3},{8,12},{12,8},{9,1... | collective-permute-start | bytes 6291464 | tf_op jit(solution)/shard_map/ppermute | solution.py:774
  283.5 8.6 %collective-permute-start.25 = (bf16[4,128,1024]{2,1,0:T(8,128)(2,1)}, bf16[4,128,1024]{2,1,0:T(8,128)(2,1)S(1)}, u32[]{:S(2)}, u32[]{:S(2)}) collective-permute-start(bf16[4,128,1024]{2,1,0:T(8,128)(2,1)} %get-tuple-element.288), channel_id=1, source_target_pairs={{0,4},{4,0},{1,5},{5,1},{2,6},{6,2},{3,7},{7,3},{8,12},{12,8},{9,1... | collective-permute-start | bytes 3145736 | tf_op jit(solution)/shard_map/ppermute | solution.py:774
  283.8 23.7 %all-to-all-start.2 = ((bf16[4,512,128]{2,1,0:T(8,128)(2,1)}), bf16[4,512,128]{2,1,0:T(8,128)(2,1)}, u32[]{:S(2)}, u32[]{:S(2)}) async-start(bf16[4,512,128]{2,1,0:T(8,128)(2,1)} %get-tuple-element.284), calls=%async_computation.2 | async-start | bytes 1048576 | tf_op jit(solution)/shard_map/all_to_all | solution.py:759
  287.9 114.4 %reduce-scatter.9.cloned.1.call-start = ((), (), s32[]{:S(2)}) async-start(), calls=%async_computation.11 | async-start | bytes 8519680
  308.7 30.0 %collective-permute-start.27 = (bf16[352,256]{1,0:T(8,128)(2,1)S(1)}, bf16[352,256]{1,0:T(8,128)(2,1)S(1)}, u32[]{:S(2)}, u32[]{:S(2)}) collective-permute-start(bf16[352,256]{1,0:T(8,128)(2,1)S(1)} %get-tuple-element.344), channel_id=1, source_target_pairs={{0,1},{1,2},{2,3},{3,0},{4,5},{5,6},{6,7},{7,4},{8,9},{9,10},{10,1... | collective-permute-start | bytes 540680 | tf_op jit(solution)/shard_map/ppermute | solution.py:768
  310.2 28.5 %collective-permute-start.28 = (bf16[352,256]{1,0:T(8,128)(2,1)S(1)}, bf16[352,256]{1,0:T(8,128)(2,1)S(1)}, u32[]{:S(2)}, u32[]{:S(2)}) collective-permute-start(bf16[352,256]{1,0:T(8,128)(2,1)S(1)} %get-tuple-element.343), channel_id=1, source_target_pairs={{0,2},{1,3},{2,0},{3,1},{4,6},{5,7},{6,4},{7,5},{8,10},{9,11},{10,... | collective-permute-start | bytes 540680 | tf_op jit(solution)/shard_map/ppermute | solution.py:768
  312.6 26.1 %collective-permute-start.29 = (bf16[352,256]{1,0:T(8,128)(2,1)S(1)}, bf16[352,256]{1,0:T(8,128)(2,1)S(1)}, u32[]{:S(2)}, u32[]{:S(2)}) collective-permute-start(bf16[352,256]{1,0:T(8,128)(2,1)S(1)} %get-tuple-element.342), channel_id=1, source_target_pairs={{0,3},{1,0},{2,1},{3,2},{4,7},{5,4},{6,5},{7,6},{8,11},{9,8},{10,9... | collective-permute-start | bytes 540680 | tf_op jit(solution)/shard_map/ppermute | solution.py:768
  314.1 25.6 %all-to-all-start.3 = ((bf16[4,512,128]{2,1,0:T(8,128)(2,1)}), bf16[4,512,128]{2,1,0:T(8,128)(2,1)S(1)}, u32[]{:S(2)}, u32[]{:S(2)}) async-start(bf16[4,512,128]{2,1,0:T(8,128)(2,1)} %get-tuple-element.294), calls=%async_computation.3 | async-start | bytes 1048576 | tf_op jit(solution)/shard_map/all_to_all | solution.py:759
  339.7 41.0 %all-to-all-start.4 = ((bf16[4,512,384]{2,1,0:T(8,128)(2,1)}), bf16[4,512,384]{2,1,0:T(8,128)(2,1)S(1)}, u32[]{:S(2)}, u32[]{:S(2)}) async-start(bf16[4,512,384]{2,1,0:T(8,128)(2,1)} %bitcast.110), calls=%async_computation.4 | async-start | bytes 3145728 | tf_op jit(solution)/shard_map/all_to_all | solution.py:759
  381.8 59.3 %all-to-all-start.5 = ((bf16[4,512,384]{2,1,0:T(8,128)(2,1)}), bf16[4,512,384]{2,1,0:T(8,128)(2,1)S(1)}, u32[]{:S(2)}, u32[]{:S(2)}) async-start(bf16[4,512,384]{2,1,0:T(8,128)(2,1)} %bitcast.109), calls=%async_computation.5 | async-start | bytes 3145728 | tf_op jit(solution)/shard_map/all_to_all | solution.py:759
  385.5 1.5 collective-permute-start.40
  397.0 15.5 %collective-permute-start.33 = (bf16[384,1024]{1,0:T(8,128)(2,1)S(1)}, bf16[384,1024]{1,0:T(8,128)(2,1)}, u32[]{:S(2)}, u32[]{:S(2)}) collective-permute-start(bf16[384,1024]{1,0:T(8,128)(2,1)S(1)} %broadcast_select_fusion.5), channel_id=1, source_target_pairs={{0,4},{4,0},{1,5},{5,1},{2,6},{6,2},{3,7},{7,3},{8,12},{12,8},{9,1... | collective-permute-start | bytes 2359304 | tf_op jit(solution)/shard_map/ppermute | solution.py:774
  405.0 36.2 %collective-permute-start.30 = (bf16[832,256]{1,0:T(8,128)(2,1)}, bf16[832,256]{1,0:T(8,128)(2,1)S(1)}, u32[]{:S(2)}, u32[]{:S(2)}) collective-permute-start(bf16[832,256]{1,0:T(8,128)(2,1)} %get-tuple-element.331), channel_id=1, source_target_pairs={{0,1},{1,2},{2,3},{3,0},{4,5},{5,6},{6,7},{7,4},{8,9},{9,10},{10,1... | collective-permute-start | bytes 1277960 | tf_op jit(solution)/shard_map/ppermute | solution.py:768
  406.9 43.4 %collective-permute-start.31 = (bf16[832,256]{1,0:T(8,128)(2,1)}, bf16[832,256]{1,0:T(8,128)(2,1)}, u32[]{:S(2)}, u32[]{:S(2)}) collective-permute-start(bf16[832,256]{1,0:T(8,128)(2,1)} %get-tuple-element.330), channel_id=1, source_target_pairs={{0,2},{1,3},{2,0},{3,1},{4,6},{5,7},{6,4},{7,5},{8,10},{9,11},{10,... | collective-permute-start | bytes 1277960 | tf_op jit(solution)/shard_map/ppermute | solution.py:768
  409.3 41.1 %collective-permute-start.32 = (bf16[832,256]{1,0:T(8,128)(2,1)}, bf16[832,256]{1,0:T(8,128)(2,1)}, u32[]{:S(2)}, u32[]{:S(2)}) collective-permute-start(bf16[832,256]{1,0:T(8,128)(2,1)} %get-tuple-element.329), channel_id=1, source_target_pairs={{0,3},{1,0},{2,1},{3,2},{4,7},{5,4},{6,5},{7,6},{8,11},{9,8},{10,9... | collective-permute-start | bytes 1277960 | tf_op jit(solution)/shard_map/ppermute | solution.py:768
  414.0 39.5 %copy-start.13 = (bf16[384,1024]{1,0:T(8,128)(2,1)}, bf16[384,1024]{1,0:T(8,128)(2,1)S(1)}, u32[]{:S(2)}) copy-start(bf16[384,1024]{1,0:T(8,128)(2,1)S(1)} %add_convert_fusion.2) | copy-start | bytes 2359300
  441.2 11.4 %copy-start.19 = (bf16[4,512,384]{2,1,0:T(8,128)(2,1)}, bf16[4,512,384]{2,1,0:T(8,128)(2,1)S(1)}, u32[]{:S(2)}) copy-start(bf16[4,512,384]{2,1,0:T(8,128)(2,1)S(1)} %all-to-all-done.5.came_ref) | copy-start | bytes 4718596
  453.5 15.3 %collective-permute-start.39 = (f32[2,352,128]{2,1,0:T(8,128)}, f32[2,352,128]{2,1,0:T(8,128)}, u32[]{:S(2)}, u32[]{:S(2)}) collective-permute-start(f32[2,352,128]{2,1,0:T(8,128)} %slice_select_fusion.1), channel_id=1, source_target_pairs={{0,4},{4,0},{1,5},{5,1},{2,6},{6,2},{3,7},{7,3},{8,12},{12,8},{9,1... | collective-permute-start | bytes 1081352 | tf_op jit(solution)/shard_map/ppermute | solution.py:774
  454.4 11.4 %collective-permute-start.34 = (bf16[384,256]{1,0:T(8,128)(2,1)}, bf16[384,256]{1,0:T(8,128)(2,1)}, u32[]{:S(2)}, u32[]{:S(2)}) collective-permute-start(bf16[384,256]{1,0:T(8,128)(2,1)} %get-tuple-element.339), channel_id=1, source_target_pairs={{0,8},{8,0},{16,24},{24,16},{1,9},{9,1},{17,25},{25,17},{2,10},{10... | collective-permute-start | bytes 589832 | tf_op jit(solution)/shard_map/ppermute | solution.py:895
  455.8 11.5 %collective-permute-start.35 = (bf16[384,256]{1,0:T(8,128)(2,1)}, bf16[384,256]{1,0:T(8,128)(2,1)}, u32[]{:S(2)}, u32[]{:S(2)}) collective-permute-start(bf16[384,256]{1,0:T(8,128)(2,1)} %get-tuple-element.341), channel_id=1, source_target_pairs={{0,16},{8,24},{16,0},{24,8},{1,17},{9,25},{17,1},{25,9},{2,18},{10... | collective-permute-start | bytes 589832 | tf_op jit(solution)/shard_map/ppermute | solution.py:895
  456.4 10.9 %collective-permute-start.36 = (bf16[384,256]{1,0:T(8,128)(2,1)}, bf16[384,256]{1,0:T(8,128)(2,1)}, u32[]{:S(2)}, u32[]{:S(2)}) collective-permute-start(bf16[384,256]{1,0:T(8,128)(2,1)} %get-tuple-element.340), channel_id=1, source_target_pairs={{0,24},{8,16},{16,8},{24,0},{1,25},{9,17},{17,9},{25,1},{2,26},{10... | collective-permute-start | bytes 589832 | tf_op jit(solution)/shard_map/ppermute | solution.py:895
  457.9 7.0 %collective-permute-start.38 = (f32[128,128]{1,0:T(8,128)}, f32[128,128]{1,0:T(8,128)}, u32[]{:S(2)}, u32[]{:S(2)}) collective-permute-start(f32[128,128]{1,0:T(8,128)} %slice_select_fusion.7), channel_id=1, source_target_pairs={{0,4},{4,0},{1,5},{5,1},{2,6},{6,2},{3,7},{7,3},{8,12},{12,8},{9,1... | collective-permute-start | bytes 196616 | tf_op jit(solution)/shard_map/ppermute | solution.py:774
  468.7 1.5 collective-permute-start.37
  470.2 14.9 %copy-start.38 = (f32[2,128]{1,0:T(2,128)S(1)}, f32[2,128]{1,0:T(2,128)}, u32[]{:S(2)}) copy-start(f32[2,128]{1,0:T(2,128)} %param.17) | copy-start | bytes 3076
  471.3 14.4 %copy-start.24 = (f32[3,128,256]{2,1,0:T(8,128)}, f32[3,128,256]{2,1,0:T(8,128)S(1)}, u32[]{:S(2)}) copy-start(f32[3,128,256]{2,1,0:T(8,128)S(1)} %reshape.155) | copy-start | bytes 1179652
  471.4 11.8 %collective-permute-start.41 = (f32[2,128]{1,0:T(2,128)S(1)}, f32[2,128]{1,0:T(2,128)S(1)}, u32[]{:S(2)}, u32[]{:S(2)}) collective-permute-start(f32[2,128]{1,0:T(2,128)S(1)} %pad_maximum_fusion.12), channel_id=1, source_target_pairs={{0,1},{1,2},{2,3},{3,0},{4,5},{5,6},{6,7},{7,4},{8,9},{9,10},{10,1... | collective-permute-start | bytes 3080 | tf_op jit(solution)/shard_map/ppermute | solution.py:768
  480.1 4.5 collective-permute-start.42
  481.6 3.6 collective-permute-start.43
  (29 other events, 129.9 us)
Sparse Core Ops, SparseCore 0:
  20.5 28.4 all-gather.2
  217.8 44.8 all-gather.4
  267.1 40.4 reduce-scatter.6
  310.4 74.5 reduce-scatter.8

commit v3 on v2

--- a/solution.py
+++ b/solution.py
@@ -18,7 +18,6 @@
 low = jnp.bfloat16
 wide = jnp.float32
 VMEM_BYTES = 60 * 1024 * 1024
-FINISH_FLOPS = 1 << 38
 
 
 def dot_nn(a, b):
@@ -599,9 +598,7 @@
         grid_spec=spec,
         out_shape=[jax.ShapeDtypeStruct((line, width, depth), low)] * 2,
         compiler_params=pltpu.CompilerParams(vmem_limit_bytes=VMEM_BYTES),
-        cost_estimate=pl.CostEstimate(
-            flops=4 * line * rows * width * depth, bytes_accessed=4 << 20, transcendentals=0
-        ),
+        cost_estimate=pl.CostEstimate(flops=0, bytes_accessed=0, transcendentals=0),
         name="outer",
     )(core, *attended_pieces, branch_grad)
 
@@ -672,7 +669,7 @@
         out_shape=jax.ShapeDtypeStruct((rows, depth), wide),
         compiler_params=pltpu.CompilerParams(vmem_limit_bytes=VMEM_BYTES),
         cost_estimate=pl.CostEstimate(
-            flops=FINISH_FLOPS, bytes_accessed=10 << 20, transcendentals=0
+            flops=2 * line * rows * height * depth, bytes_accessed=10 << 20, transcendentals=0
         ),
         name="finish",
     )(came, qkv_full, part, tokens, pack, state_grad)

time: 501 us -> 498 us (level)
  transfers between devices with their start and end apart: 54 -> 54, of which waited for: 26 -> 27; matrix products, arithmetic and copies ran while one was open for 12% -> 13% of each run, Pallas kernels for 31% -> 31%
where the time goes in v3:
time: 498 us; the launch traced here: 489 us
  Pallas kernels  160 us (32%)
  waiting for transfers between devices  154 us (31%)
  starting transfers between devices  88 us (18%)
  other arithmetic  52.4 us (11%)
  between operations  15.6 us (3%)
  local copies, waits for them, and re-layouts  11.9 us (2%)
  matrix products  7.8 us (2%)
    all_to_all x6, waiting for transfers between devices, exchange(): return lax.all_to_all(pieces, 'head', split_axis=0, concat_axis=0)  45.6 us
    pallas_call x2, Pallas kernels, attend_back(): pl.pallas_call(attend_back_kernel, grid_spec=spec, out_shape=[jax.ShapeDt...  42.2 us
    pallas_call x1, Pallas kernels, feed(): pl.pallas_call(feed_kernel, grid_spec=spec, out_shape=[jax.ShapeDtypeStru...  38.5 us
    ppermute x12, waiting for transfers between devices, plane(): lax.ppermute(slot[:end], 'chip', [(c, c ^ away) for c in range(chips)])  34.2 us
    all_to_all x6, starting transfers between devices, exchange(): return lax.all_to_all(pieces, 'head', split_axis=0, concat_axis=0)  24.3 us
    pallas_call x2, Pallas kernels, attend(): pl.pallas_call(attend_kernel, grid_spec=spec, out_shape=[jax.ShapeDtypeSt...  24.1 us
    ppermute x4, waiting for transfers between devices, hop(): lax.ppermute(ends[0], 'head', [(0, 1), (1, 2), (2, 3)])  22.6 us
    ppermute x9, starting transfers between devices, exchange_turned(): lax.ppermute(piece, 'head', [(k, (k + j) % count) for k in range(count)])  22.5 us
  transfers between devices with their start and end apart: 54, of which 27 were waited for; matrix products, arithmetic and copies ran while one was open for 13% of the time, Pallas kernels for 31%

profile of v3, /device:TPU:0, one launch (start us, length us, event | category | flops | bytes accessed | tf_op | source)
XLA Modules:
  0.0 489.2 jit_solution(16516707476238567345)
XLA Ops:
  7.2 5.1 %collective-permute-start = (bf16[512,1024]{1,0:T(8,128)(2,1)}, bf16[512,1024]{1,0:T(8,128)(2,1)S(1)}, u32[]{:S(2)}, u32[]{:S(2)}) collective-permute-start(bf16[512,1024]{1,0:T(8,128)(2,1)} %x_ref.3), channel_id=1, source_target_pairs={{0,1},{1,2},{2,3},{4,5},{5,6},{6,7},{8,9},{9,10},{10,11},{12,13},{... | collective-permute-start | bytes 3145736 | tf_op jit(solution)/shard_map/ppermute | solution.py:692
  13.7 1.9 convert_element_type.92
  23.4 11.6 %collective-permute-done.right_ref = bf16[512,1024]{1,0:T(8,128)(2,1)S(1)} collective-permute-done((bf16[512,1024]{1,0:T(8,128)(2,1)}, bf16[512,1024]{1,0:T(8,128)(2,1)S(1)}, u32[]{:S(2)}, u32[]{:S(2)}) %collective-permute-start) | collective-permute-done | bytes 1048608 | tf_op jit(solution)/shard_map/ppermute | solution.py:692
  35.0 4.1 collective-permute-done.1.left_ref
  40.1 4.0 join.1
  44.0 4.7 collective-permute-start.3
  54.4 3.9 fusion.7
  58.3 3.0 pad_maximum_fusion.2
  61.3 4.6 project.4
  65.9 1.9 collective-permute-done.5.refs_1_
  67.8 11.3 %collective-permute-done.6.refs_2_ = bf16[1184,256]{1,0:T(8,128)(2,1)} collective-permute-done((bf16[1184,256]{1,0:T(8,128)(2,1)}, bf16[1184,256]{1,0:T(8,128)(2,1)}, u32[]{:S(2)}, u32[]{:S(2)}) %collective-permute-start.6) | collective-permute-done | bytes 606240 | tf_op jit(solution)/shard_map/ppermute | solution.py:708
  79.1 6.8 %collective-permute-done.3 = bf16[3616,256]{1,0:T(8,128)(2,1)} collective-permute-done((bf16[3616,256]{1,0:T(8,128)(2,1)}, bf16[3616,256]{1,0:T(8,128)(2,1)}, u32[]{:S(2)}, u32[]{:S(2)}) %collective-permute-start.3) | collective-permute-done | bytes 1851424 | tf_op jit(solution)/shard_map/ppermute | solution.py:692
  85.9 5.3 %collective-permute-done.4 = bf16[3616,256]{1,0:T(8,128)(2,1)} collective-permute-done((bf16[3616,256]{1,0:T(8,128)(2,1)}, bf16[3616,256]{1,0:T(8,128)(2,1)}, u32[]{:S(2)}, u32[]{:S(2)}) %collective-permute-start.4) | collective-permute-done | bytes 1851424 | tf_op jit(solution)/shard_map/ppermute | solution.py:693
  91.3 3.6 collective-permute-start.8
  94.8 1.7 collective-permute-start.9
  103.5 4.5 project.5
  107.9 2.6 slice_select_fusion.x_ref
  110.5 4.5 project.6
  116.6 10.1 %collective-permute-done.11.refs_6_ = bf16[1184,256]{1,0:T(8,128)(2,1)S(1)} collective-permute-done((bf16[1184,256]{1,0:T(8,128)(2,1)S(1)}, bf16[1184,256]{1,0:T(8,128)(2,1)S(1)}, u32[]{:S(2)}, u32[]{:S(2)}) %collective-permute-start.11) | collective-permute-done | bytes 606240 | tf_op jit(solution)/shard_map/ppermute | solution.py:708
  126.7 4.2 collective-permute-done.8
  130.8 5.4 %collective-permute-done.9 = bf16[3616,256]{1,0:T(8,128)(2,1)} collective-permute-done((bf16[3616,256]{1,0:T(8,128)(2,1)}, bf16[3616,256]{1,0:T(8,128)(2,1)}, u32[]{:S(2)}, u32[]{:S(2)}) %collective-permute-start.9) | collective-permute-done | bytes 1851424 | tf_op jit(solution)/shard_map/ppermute | solution.py:693
  136.2 2.6 broadcast_select_fusion.3
  142.5 2.3 collective-permute-start.13
  146.1 2.9 select_select_fusion.x_ref
  149.0 4.5 project.7
  153.5 12.1 %attend.2 = (bf16[2048,128]{1,0:T(8,128)(2,1)}, f32[2048,128]{1,0:T(8,128)}, f32[8,2048]{1,0:T(8,128)}) custom-call(s32[1]{0:T(128)S(6)} %copy.71.len_ref, bf16[2048,256]{1,0:T(8,128)(2,1)} %get-tuple-element.233.q_ref, bf16[2048,256]{1,0:T(8,128)(2,1)} %get-tuple-element.234.k_ref, bf16[2048,256]{1,0:T(8,128)(2,1)} %get-tuple-element.235.v_ref), custom_call_target="tpu_custom_call" | custom-call | flops 4294967296 | bytes 4194304 | tf_op jit(solution)/shard_map/attend/pallas_call | solution.py:199
  165.6 4.2 all-to-all-start
  169.8 1.8 select_select_fusion.1
  175.2 12.1 %attend.3 = (bf16[2048,128]{1,0:T(8,128)(2,1)}, f32[2048,128]{1,0:T(8,128)}, f32[8,2048]{1,0:T(8,128)}) custom-call(s32[1]{0:T(128)S(6)} %copy.71.len_ref, bf16[2048,256]{1,0:T(8,128)(2,1)} %get-tuple-element.233.q_ref, bf16[2048,256]{1,0:T(8,128)(2,1)} %get-tuple-element.234.k_ref, bf16[2048,256]{1,0:T(8,128)(2,1)} %get-tuple-element.235.v_ref), custom_call_target="tpu_custom_call" | custom-call | flops 4294967296 | bytes 4194304 | tf_op jit(solution)/shard_map/attend/pallas_call | solution.py:199
  188.4 8.2 %collective-permute-done.19.refs_14_ = bf16[1184,256]{1,0:T(8,128)(2,1)} collective-permute-done((bf16[1184,256]{1,0:T(8,128)(2,1)S(1)}, bf16[1184,256]{1,0:T(8,128)(2,1)}, u32[]{:S(2)}, u32[]{:S(2)}) %collective-permute-start.19) | collective-permute-done | bytes 606240 | tf_op jit(solution)/shard_map/ppermute | solution.py:708
  196.6 4.8 all-to-all-start.1
  205.3 6.3 %all-to-all-done.1.second_ref = bf16[4,512,128]{2,1,0:T(8,128)(2,1)S(1)} async-done(((bf16[4,512,128]{2,1,0:T(8,128)(2,1)}), bf16[4,512,128]{2,1,0:T(8,128)(2,1)S(1)}, u32[]{:S(2)}, u32[]{:S(2)}) %all-to-all-start.1) | async-done | bytes 524320 | tf_op jit(solution)/shard_map/all_to_all | solution.py:756
  211.6 3.0 collect.1
  214.6 3.1 line_up.1
  219.2 2.1 collective-permute-done.21
  221.6 2.8 multiply_reduce_fusion
  225.9 2.7 collective-permute-done.22.refs_17_
  228.6 38.5 %feed.1 = (f32[512,1024]{1,0:T(8,128)}, f32[512,1024]{1,0:T(8,128)}, f32[512,1024]{1,0:T(8,128)}, f32[512,1024]{1,0:T(8,128)}, bf16[4,4,832,256]{3,2,1,0:T(8,128)(2,1)}, /*index=5*/bf16[4,4,352,256]{3,2,1,0:T(8,128)(2,1)}) custom-call(s32[4]{0:T(128)} %pad_add_fusion.1.order, s32[4]{0:T(128)} %iota_xor_fusion.which, ...), custom_call_target="tpu_custom_call" | custom-call | flops 26575110144 | bytes 31457280 | tf_op jit(solution)/shard_map/feed/pallas_call | solution.py:424
  269.8 1.9 collective-permute-done.24.came_ref
  271.7 6.9 %turn.1 = (f32[512,1024]{1,0:T(8,128)}, bf16[512,1024]{1,0:T(8,128)(2,1)}, bf16[4,512,128]{2,1,0:T(8,128)(2,1)}, bf16[4,512,128]{2,1,0:T(8,128)(2,1)}) custom-call(s32[2]{0:T(128)} %pad_add_fusion.facts, f32[512,1024]{1,0:T(8,128)} %get-tuple-element.277.own_ref, f32[512,1024]{1,0:T(8,128)} %collective-permute-done.24.came_ref, f32[512,1024]{1,0:T(8,128)} %copy-done, ...), custom_call_target="tpu_custom_call" | custom-call | flops 1073741824 | bytes 13631488 | tf_op jit(solution)/shard_map/turn/pallas_call | solution.py:560
  278.6 5.2 %outer.1 = (bf16[4,128,1024]{2,1,0:T(8,128)(2,1)}, bf16[4,128,1024]{2,1,0:T(8,128)(2,1)}) custom-call(s32[1]{0:T(128)} %bitcast.28.core, bf16[4,512,128]{2,1,0:T(8,128)(2,1)} %all-to-all-done.first_ref, bf16[4,512,128]{2,1,0:T(8,128)(2,1)} %copy-done.18, bf16[512,1024]{1,0:T(8,128)(2,1)} %get-tuple-element.286.grad_ref), custom_call_target="tpu_custom_call" | custom-call | tf_op jit(solution)/shard_map/outer/pallas_call | solution.py:596
  283.9 4.2 all-to-all-start.2
  288.4 3.9 add_convert_fusion
  293.8 13.8 %reduce-scatter.7.cloned.1.call-done = bf16[1,4,352,256]{3,2,1,0:T(8,128)(2,1)} async-done(((bf16[4,4,352,256]{3,2,1,0:T(8,128)(2,1)}), bf16[1,4,352,256]{3,2,1,0:T(8,128)(2,1)}) %reduce-scatter.7.cloned.1.call-update) | async-done | bytes 720912
  310.9 2.4 collective-permute-start.28
  314.7 3.5 all-to-all-start.3
  318.3 21.1 %attend_back.2 = (bf16[2048,384]{1,0:T(8,128)(2,1)}, f32[2048,128]{1,0:T(8,128)}) custom-call(s32[1]{0:T(128)S(6)} %copy.71.len_ref, bf16[2048,256]{1,0:T(8,128)(2,1)} %get-tuple-element.233.q_ref, bf16[2048,256]{1,0:T(8,128)(2,1)} %get-tuple-element.234.k_ref, bf16[2048,256]{1,0:T(8,128)(2,1)} %get-tuple-element.235.v_ref, ...), custom_call_target="tpu_custom_call" | custom-call | flops 10737418240 | bytes 6291456 | tf_op jit(solution)/shard_map/attend_back/pallas_call | solution.py:308
  340.4 4.1 all-to-all-start.4
  344.5 21.1 %attend_back.3 = (bf16[2048,384]{1,0:T(8,128)(2,1)}, f32[2048,128]{1,0:T(8,128)}) custom-call(s32[1]{0:T(128)S(6)} %copy.71.len_ref, bf16[2048,256]{1,0:T(8,128)(2,1)} %get-tuple-element.233.q_ref, bf16[2048,256]{1,0:T(8,128)(2,1)} %get-tuple-element.234.k_ref, bf16[2048,256]{1,0:T(8,128)(2,1)} %get-tuple-element.235.v_ref, bf16[2048,128]{1,0:T(8,128)(2,1)} %bitcast.136, ...), custom_call_target="tpu_custom_call" | custom-call | flops 10737418240 | bytes 6291456 | tf_op jit(solution)/shard_map/attend_back/pallas_call | solution.py:308
  365.6 15.7 %all-to-all-done.4 = bf16[4,512,384]{2,1,0:T(8,128)(2,1)S(1)} async-done(((bf16[4,512,384]{2,1,0:T(8,128)(2,1)}), bf16[4,512,384]{2,1,0:T(8,128)(2,1)S(1)}, u32[]{:S(2)}, u32[]{:S(2)}) %all-to-all-start.4) | async-done | bytes 1572896 | tf_op jit(solution)/shard_map/all_to_all | solution.py:756
  381.3 3.6 all-to-all-start.5
  386.9 1.8 collective-permute-done.40
  390.3 7.6 %unproject.1 = bf16[768,1024]{1,0:T(8,128)(2,1)} custom-call(bf16[2048,1024]{1,0:T(8,128)(2,1)} %get-tuple-element.309.normed_ref, bf16[2048,384]{1,0:T(8,128)(2,1)} %get-tuple-element.301.refs_0_, bf16[2048,384]{1,0:T(8,128)(2,1)} %get-tuple-element.307.refs_1_), custom_call_target="tpu_custom_call" | custom-call | tf_op jit(solution)/shard_map/unproject/pallas_call | solution.py:629
  398.0 2.4 broadcast_select_fusion.5
  400.5 5.0 %fusion.1.part_ref = f32[512,1024]{1,0:T(8,128)} fusion(bf16[4,512,384]{2,1,0:T(8,128)(2,1)S(1)} %all-to-all-done.4, bf16[4,2,384,1024]{3,2,1,0:T(8,128)(2,1)} %bitcast.109), kind=kOutput, calls=%fused_computation.9 | convolution fusion | flops 1610612736 | bytes 6815744 | tf_op jit(solution)/shard_map/ztc,zcd->td/dot_general | solution.py:937
  405.5 2.6 dynamic-slice_bitcast_fusion
  408.1 2.0 collective-permute-start.30
  410.1 2.4 collective-permute-start.31
  415.6 2.5 add_convert_fusion.2
  418.1 22.6 %all-to-all-done.5.came_ref = bf16[4,512,384]{2,1,0:T(8,128)(2,1)S(1)} async-done(((bf16[4,512,384]{2,1,0:T(8,128)(2,1)}), bf16[4,512,384]{2,1,0:T(8,128)(2,1)S(1)}, u32[]{:S(2)}, u32[]{:S(2)}) %all-to-all-start.5) | async-done | bytes 1572896 | tf_op jit(solution)/shard_map/all_to_all | solution.py:756
  440.7 9.2 %collective-permute-done.31 = bf16[832,256]{1,0:T(8,128)(2,1)} collective-permute-done((bf16[832,256]{1,0:T(8,128)(2,1)}, bf16[832,256]{1,0:T(8,128)(2,1)}, u32[]{:S(2)}, u32[]{:S(2)}) %collective-permute-start.31) | collective-permute-done | bytes 426016 | tf_op jit(solution)/shard_map/ppermute | solution.py:765
  455.3 7.0 %finish.1 = f32[512,1024]{1,0:T(8,128)} custom-call(bf16[4,512,384]{2,1,0:T(8,128)(2,1)} %copy-done.3, bf16[4,2,384,1024]{3,2,1,0:T(8,128)(2,1)} %bitcast.110, f32[512,1024]{1,0:T(8,128)} %fusion.1.part_ref, bf16[512,1024]{1,0:T(8,128)(2,1)} %x_ref.3, bf16[784,1024]{1,0:T(8,128)(2,1)} %all-gather.3.cloned.1.call-done.w_ref.gain_ref, ...), custom_call_target="tpu_custom_call" | custom-call | flops 1610612736 | bytes 10485760 | tf_op jit(solution)/shard_map/finish/pallas_call | solution.py:657
  462.3 2.1 collective-permute-done.35
  468.0 8.7 %collective-permute-start.41 = (f32[2,128]{1,0:T(2,128)S(1)}, f32[2,128]{1,0:T(2,128)S(1)}, u32[]{:S(2)}, u32[]{:S(2)}) collective-permute-start(f32[2,128]{1,0:T(2,128)S(1)} %pad_maximum_fusion.12), channel_id=1, source_target_pairs={{0,1},{1,2},{2,3},{3,0},{4,5},{5,6},{6,7},{7,4},{8,9},{9,10},{10,1... | collective-permute-start | bytes 3080 | tf_op jit(solution)/shard_map/ppermute | solution.py:765
  (210 shorter events, 72.0 us)
Async XLA Ops:
  7.2 12.2 %copy-start.19 = (f32[3,128,256]{2,1,0:T(8,128)S(1)}, f32[3,128,256]{2,1,0:T(8,128)}, u32[]{:S(2)}) copy-start(f32[3,128,256]{2,1,0:T(8,128)} %param.13) | copy-start | bytes 1179652
  7.2 54.1 %all-gather.3.cloned.1.call-start = ((), (), s32[]{:S(2)}) async-start(), calls=%async_computation.8 | async-start | bytes 1806336 | tf_op jit(solution)/shard_map/all_gather | solution.py:810
  7.2 27.8 %collective-permute-start = (bf16[512,1024]{1,0:T(8,128)(2,1)}, bf16[512,1024]{1,0:T(8,128)(2,1)S(1)}, u32[]{:S(2)}, u32[]{:S(2)}) collective-permute-start(bf16[512,1024]{1,0:T(8,128)(2,1)} %x_ref.3), channel_id=1, source_target_pairs={{0,1},{1,2},{2,3},{4,5},{5,6},{6,7},{8,9},{9,10},{10,11},{12,13},{... | collective-permute-start | bytes 3145736 | tf_op jit(solution)/shard_map/ppermute | solution.py:692
  12.4 26.7 %collective-permute-start.1 = (bf16[512,1024]{1,0:T(8,128)(2,1)}, bf16[512,1024]{1,0:T(8,128)(2,1)S(1)}, u32[]{:S(2)}, u32[]{:S(2)}) collective-permute-start(bf16[512,1024]{1,0:T(8,128)(2,1)} %x_ref.3), channel_id=1, source_target_pairs={{1,0},{2,1},{3,2},{5,4},{6,5},{7,6},{9,8},{10,9},{11,10},{13,12},{... | collective-permute-start | bytes 3145736 | tf_op jit(solution)/shard_map/ppermute | solution.py:693
  19.4 1.9 collective-permute-start.2
  44.0 41.9 %collective-permute-start.3 = (bf16[3616,256]{1,0:T(8,128)(2,1)}, bf16[3616,256]{1,0:T(8,128)(2,1)}, u32[]{:S(2)}, u32[]{:S(2)}) collective-permute-start(bf16[3616,256]{1,0:T(8,128)(2,1)} %get-tuple-element.174), channel_id=1, source_target_pairs={{0,1},{1,2},{2,3},{4,5},{5,6},{6,7},{8,9},{9,10},{10,11},{12,13},{... | collective-permute-start | bytes 5554184 | tf_op jit(solution)/shard_map/ppermute | solution.py:692
  48.7 42.6 %collective-permute-start.4 = (bf16[3616,256]{1,0:T(8,128)(2,1)}, bf16[3616,256]{1,0:T(8,128)(2,1)}, u32[]{:S(2)}, u32[]{:S(2)}) collective-permute-start(bf16[3616,256]{1,0:T(8,128)(2,1)} %get-tuple-element.175), channel_id=1, source_target_pairs={{1,0},{2,1},{3,2},{5,4},{6,5},{7,6},{9,8},{10,9},{11,10},{13,12},{... | collective-permute-start | bytes 5554184 | tf_op jit(solution)/shard_map/ppermute | solution.py:693
  50.9 16.9 %collective-permute-start.5 = (bf16[1184,256]{1,0:T(8,128)(2,1)}, bf16[1184,256]{1,0:T(8,128)(2,1)}, u32[]{:S(2)}, u32[]{:S(2)}) collective-permute-start(bf16[1184,256]{1,0:T(8,128)(2,1)} %pad_maximum_fusion.5.refs_0_), channel_id=1, source_target_pairs={{0,8},{8,0},{16,24},{24,16},{1,9},{9,1},{17,25},{25,17},{2,10},{10... | collective-permute-start | bytes 1818632 | tf_op jit(solution)/shard_map/ppermute | solution.py:708
  52.4 26.7 %collective-permute-start.6 = (bf16[1184,256]{1,0:T(8,128)(2,1)}, bf16[1184,256]{1,0:T(8,128)(2,1)}, u32[]{:S(2)}, u32[]{:S(2)}) collective-permute-start(bf16[1184,256]{1,0:T(8,128)(2,1)} %pad_maximum_fusion.5.refs_0_), channel_id=1, source_target_pairs={{0,16},{8,24},{16,0},{24,8},{1,17},{9,25},{17,1},{25,9},{2,18},{10... | collective-permute-start | bytes 1818632 | tf_op jit(solution)/shard_map/ppermute | solution.py:708
  53.9 25.2 %collective-permute-start.7 = (bf16[1184,256]{1,0:T(8,128)(2,1)}, bf16[1184,256]{1,0:T(8,128)(2,1)}, u32[]{:S(2)}, u32[]{:S(2)}) collective-permute-start(bf16[1184,256]{1,0:T(8,128)(2,1)} %pad_maximum_fusion.5.refs_0_), channel_id=1, source_target_pairs={{0,24},{8,16},{16,8},{24,0},{1,25},{9,17},{17,9},{25,1},{2,26},{10... | collective-permute-start | bytes 1818632 | tf_op jit(solution)/shard_map/ppermute | solution.py:708
  61.3 36.0 %copy-start.7 = (bf16[512,1024]{1,0:T(8,128)(2,1)S(1)}, bf16[512,1024]{1,0:T(8,128)(2,1)}, u32[]{:S(2)}) copy-start(bf16[512,1024]{1,0:T(8,128)(2,1)} %copy-done.6) | copy-start | bytes 3145732
  61.3 36.0 %copy-start.9 = (bf16[512,1024]{1,0:T(8,128)(2,1)S(1)}, bf16[512,1024]{1,0:T(8,128)(2,1)}, u32[]{:S(2)}) copy-start(bf16[512,1024]{1,0:T(8,128)(2,1)} %copy-done.8) | copy-start | bytes 3145732
  91.3 39.5 %collective-permute-start.8 = (bf16[3616,256]{1,0:T(8,128)(2,1)}, bf16[3616,256]{1,0:T(8,128)(2,1)}, u32[]{:S(2)}, u32[]{:S(2)}) collective-permute-start(bf16[3616,256]{1,0:T(8,128)(2,1)} %collective-permute-done.3), channel_id=1, source_target_pairs={{0,1},{1,2},{2,3},{4,5},{5,6},{6,7},{8,9},{9,10},{10,11},{12,13},{... | collective-permute-start | bytes 5554184 | tf_op jit(solution)/shard_map/ppermute | solution.py:692
  94.8 41.4 %collective-permute-start.9 = (bf16[3616,256]{1,0:T(8,128)(2,1)}, bf16[3616,256]{1,0:T(8,128)(2,1)}, u32[]{:S(2)}, u32[]{:S(2)}) collective-permute-start(bf16[3616,256]{1,0:T(8,128)(2,1)} %collective-permute-done.4), channel_id=1, source_target_pairs={{1,0},{2,1},{3,2},{5,4},{6,5},{7,6},{9,8},{10,9},{11,10},{13,12},{... | collective-permute-start | bytes 5554184 | tf_op jit(solution)/shard_map/ppermute | solution.py:693
  99.9 16.7 %collective-permute-start.10 = (bf16[1184,256]{1,0:T(8,128)(2,1)S(1)}, bf16[1184,256]{1,0:T(8,128)(2,1)S(1)}, u32[]{:S(2)}, u32[]{:S(2)}) collective-permute-start(bf16[1184,256]{1,0:T(8,128)(2,1)S(1)} %slice.139.refs_4_), channel_id=1, source_target_pairs={{0,8},{8,0},{16,24},{24,16},{1,9},{9,1},{17,25},{25,17},{2,10},{10... | collective-permute-start | bytes 1818632 | tf_op jit(solution)/shard_map/ppermute | solution.py:708
  101.5 25.2 %collective-permute-start.11 = (bf16[1184,256]{1,0:T(8,128)(2,1)S(1)}, bf16[1184,256]{1,0:T(8,128)(2,1)S(1)}, u32[]{:S(2)}, u32[]{:S(2)}) collective-permute-start(bf16[1184,256]{1,0:T(8,128)(2,1)S(1)} %slice.139.refs_4_), channel_id=1, source_target_pairs={{0,16},{8,24},{16,0},{24,8},{1,17},{9,25},{17,1},{25,9},{2,18},{10... | collective-permute-start | bytes 1818632 | tf_op jit(solution)/shard_map/ppermute | solution.py:708
  103.0 23.7 %collective-permute-start.12 = (bf16[1184,256]{1,0:T(8,128)(2,1)S(1)}, bf16[1184,256]{1,0:T(8,128)(2,1)}, u32[]{:S(2)}, u32[]{:S(2)}) collective-permute-start(bf16[1184,256]{1,0:T(8,128)(2,1)S(1)} %slice.139.refs_4_), channel_id=1, source_target_pairs={{0,24},{8,16},{16,8},{24,0},{1,25},{9,17},{17,9},{25,1},{2,26},{10... | collective-permute-start | bytes 1818632 | tf_op jit(solution)/shard_map/ppermute | solution.py:708
  116.6 19.6 %copy-start.27 = (bf16[1184,256]{1,0:T(8,128)(2,1)}, bf16[1184,256]{1,0:T(8,128)(2,1)S(1)}, u32[]{:S(2)}) copy-start(bf16[1184,256]{1,0:T(8,128)(2,1)S(1)} %collective-permute-done.10.refs_5_) | copy-start | bytes 1818628
  138.9 26.7 %collective-permute-start.15 = (bf16[1184,256]{1,0:T(8,128)(2,1)S(1)}, bf16[1184,256]{1,0:T(8,128)(2,1)}, u32[]{:S(2)}, u32[]{:S(2)}) collective-permute-start(bf16[1184,256]{1,0:T(8,128)(2,1)S(1)} %slice.140.refs_8_), channel_id=1, source_target_pairs={{0,8},{8,0},{16,24},{24,16},{1,9},{9,1},{17,25},{25,17},{2,10},{10... | collective-permute-start | bytes 1818632 | tf_op jit(solution)/shard_map/ppermute | solution.py:708
  140.5 25.1 %collective-permute-start.16 = (bf16[1184,256]{1,0:T(8,128)(2,1)S(1)}, bf16[1184,256]{1,0:T(8,128)(2,1)}, u32[]{:S(2)}, u32[]{:S(2)}) collective-permute-start(bf16[1184,256]{1,0:T(8,128)(2,1)S(1)} %slice.140.refs_8_), channel_id=1, source_target_pairs={{0,16},{8,24},{16,0},{24,8},{1,17},{9,25},{17,1},{25,9},{2,18},{10... | collective-permute-start | bytes 1818632 | tf_op jit(solution)/shard_map/ppermute | solution.py:708
  142.0 23.6 %collective-permute-start.17 = (bf16[1184,256]{1,0:T(8,128)(2,1)S(1)}, bf16[1184,256]{1,0:T(8,128)(2,1)}, u32[]{:S(2)}, u32[]{:S(2)}) collective-permute-start(bf16[1184,256]{1,0:T(8,128)(2,1)S(1)} %slice.140.refs_8_), channel_id=1, source_target_pairs={{0,24},{8,16},{16,8},{24,0},{1,25},{9,17},{17,9},{25,1},{2,26},{10... | collective-permute-start | bytes 1818632 | tf_op jit(solution)/shard_map/ppermute | solution.py:708
  142.5 23.1 %collective-permute-start.13 = (bf16[1568,256]{1,0:T(8,128)(2,1)}, bf16[1568,256]{1,0:T(8,128)(2,1)}, u32[]{:S(2)}, u32[]{:S(2)}) collective-permute-start(bf16[1568,256]{1,0:T(8,128)(2,1)} %get-tuple-element.327), channel_id=1, source_target_pairs={{0,1},{1,2},{2,3},{4,5},{5,6},{6,7},{8,9},{9,10},{10,11},{12,13},{... | collective-permute-start | bytes 2408456 | tf_op jit(solution)/shard_map/ppermute | solution.py:692
  144.8 20.8 %collective-permute-start.14 = (bf16[1568,256]{1,0:T(8,128)(2,1)S(1)}, bf16[1568,256]{1,0:T(8,128)(2,1)}, u32[]{:S(2)}, u32[]{:S(2)}) collective-permute-start(bf16[1568,256]{1,0:T(8,128)(2,1)S(1)} %get-tuple-element.328), channel_id=1, source_target_pairs={{1,0},{2,1},{3,2},{5,4},{6,5},{7,6},{9,8},{10,9},{11,10},{13,12},{... | collective-permute-start | bytes 2408456 | tf_op jit(solution)/shard_map/ppermute | solution.py:693
  165.6 31.0 %all-to-all-start = ((bf16[4,512,128]{2,1,0:T(8,128)(2,1)}), bf16[4,512,128]{2,1,0:T(8,128)(2,1)}, u32[]{:S(2)}, u32[]{:S(2)}) async-start(bf16[4,512,128]{2,1,0:T(8,128)(2,1)} %bitcast.134), calls=%async_computation | async-start | bytes 1048576 | tf_op jit(solution)/shard_map/all_to_all | solution.py:756
  171.6 15.6 %copy-start.17 = (bf16[1184,256]{1,0:T(8,128)(2,1)}, bf16[1184,256]{1,0:T(8,128)(2,1)S(1)}, u32[]{:S(2)}) copy-start(bf16[1184,256]{1,0:T(8,128)(2,1)S(1)} %slice.141.refs_12_) | copy-start | bytes 1818628
  171.6 16.8 %collective-permute-start.18 = (bf16[1184,256]{1,0:T(8,128)(2,1)S(1)}, bf16[1184,256]{1,0:T(8,128)(2,1)}, u32[]{:S(2)}, u32[]{:S(2)}) collective-permute-start(bf16[1184,256]{1,0:T(8,128)(2,1)S(1)} %slice.141.refs_12_), channel_id=1, source_target_pairs={{0,8},{8,0},{16,24},{24,16},{1,9},{9,1},{17,25},{25,17},{2,10},{10... | collective-permute-start | bytes 1818632 | tf_op jit(solution)/shard_map/ppermute | solution.py:708
  173.2 23.4 %collective-permute-start.19 = (bf16[1184,256]{1,0:T(8,128)(2,1)S(1)}, bf16[1184,256]{1,0:T(8,128)(2,1)}, u32[]{:S(2)}, u32[]{:S(2)}) collective-permute-start(bf16[1184,256]{1,0:T(8,128)(2,1)S(1)} %slice.141.refs_12_), channel_id=1, source_target_pairs={{0,16},{8,24},{16,0},{24,8},{1,17},{9,25},{17,1},{25,9},{2,18},{10... | collective-permute-start | bytes 1818632 | tf_op jit(solution)/shard_map/ppermute | solution.py:708
  174.7 21.9 %collective-permute-start.20 = (bf16[1184,256]{1,0:T(8,128)(2,1)S(1)}, bf16[1184,256]{1,0:T(8,128)(2,1)}, u32[]{:S(2)}, u32[]{:S(2)}) collective-permute-start(bf16[1184,256]{1,0:T(8,128)(2,1)S(1)} %slice.141.refs_12_), channel_id=1, source_target_pairs={{0,24},{8,16},{16,8},{24,0},{1,25},{9,17},{17,9},{25,1},{2,26},{10... | collective-permute-start | bytes 1818632 | tf_op jit(solution)/shard_map/ppermute | solution.py:708
  196.6 15.0 %all-to-all-start.1 = ((bf16[4,512,128]{2,1,0:T(8,128)(2,1)}), bf16[4,512,128]{2,1,0:T(8,128)(2,1)S(1)}, u32[]{:S(2)}, u32[]{:S(2)}) async-start(bf16[4,512,128]{2,1,0:T(8,128)(2,1)} %bitcast.135), calls=%async_computation.1 | async-start | bytes 1048576 | tf_op jit(solution)/shard_map/all_to_all | solution.py:756
  201.3 70.4 %all-gather.5.cloned.1.call-start = ((), (), s32[]{:S(2)}) async-start(), calls=%async_computation.9 | async-start | bytes 7077888 | tf_op jit(solution)/shard_map/all_gather | solution.py:863
  217.7 89.8 %reduce-scatter.7.cloned.1.call-start = ((), (), s32[]{:S(2)}) async-start(), calls=%async_computation.10 | async-start | bytes 3604480
  217.9 3.4 collective-permute-start.21
  218.0 7.9 %collective-permute-start.23 = (bf16[512,1024]{1,0:T(8,128)(2,1)}, bf16[512,1024]{1,0:T(8,128)(2,1)}, u32[]{:S(2)}, u32[]{:S(2)}) collective-permute-start(bf16[512,1024]{1,0:T(8,128)(2,1)} %c_ref.1), channel_id=1, source_target_pairs={{0,4},{4,0},{1,5},{5,1},{2,6},{6,2},{3,7},{7,3},{8,12},{12,8},{9,1... | collective-permute-start | bytes 3145736 | tf_op jit(solution)/shard_map/ppermute | solution.py:771
  224.4 42.7 %copy-start = (f32[512,1024]{1,0:T(8,128)}, f32[512,1024]{1,0:T(8,128)S(1)}, u32[]{:S(2)}) copy-start(f32[512,1024]{1,0:T(8,128)S(1)} %get-tuple-element.360.state_ref) | copy-start | bytes 6291460
  225.8 2.8 collective-permute-start.22
  267.1 4.6 collective-permute-start.24
  267.3 21.0 %collective-permute-start.26 = (f32[512,1024]{1,0:T(8,128)}, f32[512,1024]{1,0:T(8,128)}, u32[]{:S(2)}, u32[]{:S(2)}) collective-permute-start(f32[512,1024]{1,0:T(8,128)} %get-tuple-element.292), channel_id=1, source_target_pairs={{0,4},{4,0},{1,5},{5,1},{2,6},{6,2},{3,7},{7,3},{8,12},{12,8},{9,1... | collective-permute-start | bytes 6291464 | tf_op jit(solution)/shard_map/ppermute | solution.py:771
  283.8 8.5 %collective-permute-start.25 = (bf16[4,128,1024]{2,1,0:T(8,128)(2,1)}, bf16[4,128,1024]{2,1,0:T(8,128)(2,1)S(1)}, u32[]{:S(2)}, u32[]{:S(2)}) collective-permute-start(bf16[4,128,1024]{2,1,0:T(8,128)(2,1)} %get-tuple-element.288), channel_id=1, source_target_pairs={{0,4},{4,0},{1,5},{5,1},{2,6},{6,2},{3,7},{7,3},{8,12},{12,8},{9,1... | collective-permute-start | bytes 3145736 | tf_op jit(solution)/shard_map/ppermute | solution.py:771
  283.9 23.6 %all-to-all-start.2 = ((bf16[4,512,128]{2,1,0:T(8,128)(2,1)}), bf16[4,512,128]{2,1,0:T(8,128)(2,1)}, u32[]{:S(2)}, u32[]{:S(2)}) async-start(bf16[4,512,128]{2,1,0:T(8,128)(2,1)} %get-tuple-element.284), calls=%async_computation.2 | async-start | bytes 1048576 | tf_op jit(solution)/shard_map/all_to_all | solution.py:756
  288.1 117.4 %reduce-scatter.9.cloned.1.call-start = ((), (), s32[]{:S(2)}) async-start(), calls=%async_computation.11 | async-start | bytes 8519680
  309.4 30.0 %collective-permute-start.27 = (bf16[352,256]{1,0:T(8,128)(2,1)S(1)}, bf16[352,256]{1,0:T(8,128)(2,1)S(1)}, u32[]{:S(2)}, u32[]{:S(2)}) collective-permute-start(bf16[352,256]{1,0:T(8,128)(2,1)S(1)} %get-tuple-element.344), channel_id=1, source_target_pairs={{0,1},{1,2},{2,3},{3,0},{4,5},{5,6},{6,7},{7,4},{8,9},{9,10},{10,1... | collective-permute-start | bytes 540680 | tf_op jit(solution)/shard_map/ppermute | solution.py:765
  310.9 28.5 %collective-permute-start.28 = (bf16[352,256]{1,0:T(8,128)(2,1)S(1)}, bf16[352,256]{1,0:T(8,128)(2,1)S(1)}, u32[]{:S(2)}, u32[]{:S(2)}) collective-permute-start(bf16[352,256]{1,0:T(8,128)(2,1)S(1)} %get-tuple-element.343), channel_id=1, source_target_pairs={{0,2},{1,3},{2,0},{3,1},{4,6},{5,7},{6,4},{7,5},{8,10},{9,11},{10,... | collective-permute-start | bytes 540680 | tf_op jit(solution)/shard_map/ppermute | solution.py:765
  313.3 26.1 %collective-permute-start.29 = (bf16[352,256]{1,0:T(8,128)(2,1)S(1)}, bf16[352,256]{1,0:T(8,128)(2,1)S(1)}, u32[]{:S(2)}, u32[]{:S(2)}) collective-permute-start(bf16[352,256]{1,0:T(8,128)(2,1)S(1)} %get-tuple-element.342), channel_id=1, source_target_pairs={{0,3},{1,0},{2,1},{3,2},{4,7},{5,4},{6,5},{7,6},{8,11},{9,8},{10,9... | collective-permute-start | bytes 540680 | tf_op jit(solution)/shard_map/ppermute | solution.py:765
  314.7 25.6 %all-to-all-start.3 = ((bf16[4,512,128]{2,1,0:T(8,128)(2,1)}), bf16[4,512,128]{2,1,0:T(8,128)(2,1)S(1)}, u32[]{:S(2)}, u32[]{:S(2)}) async-start(bf16[4,512,128]{2,1,0:T(8,128)(2,1)} %get-tuple-element.294), calls=%async_computation.3 | async-start | bytes 1048576 | tf_op jit(solution)/shard_map/all_to_all | solution.py:756
  339.4 26.2 %copy-start.33 = (bf16[352,256]{1,0:T(8,128)(2,1)}, bf16[352,256]{1,0:T(8,128)(2,1)S(1)}, u32[]{:S(2)}) copy-start(bf16[352,256]{1,0:T(8,128)(2,1)S(1)} %collective-permute-done.27) | copy-start | bytes 540676
  339.4 26.2 %copy-start.34 = (bf16[352,256]{1,0:T(8,128)(2,1)}, bf16[352,256]{1,0:T(8,128)(2,1)S(1)}, u32[]{:S(2)}) copy-start(bf16[352,256]{1,0:T(8,128)(2,1)S(1)} %collective-permute-done.28) | copy-start | bytes 540676
  339.4 26.2 %copy-start.35 = (bf16[352,256]{1,0:T(8,128)(2,1)}, bf16[352,256]{1,0:T(8,128)(2,1)S(1)}, u32[]{:S(2)}) copy-start(bf16[352,256]{1,0:T(8,128)(2,1)S(1)} %collective-permute-done.29) | copy-start | bytes 540676
  340.4 41.0 %all-to-all-start.4 = ((bf16[4,512,384]{2,1,0:T(8,128)(2,1)}), bf16[4,512,384]{2,1,0:T(8,128)(2,1)S(1)}, u32[]{:S(2)}, u32[]{:S(2)}) async-start(bf16[4,512,384]{2,1,0:T(8,128)(2,1)} %bitcast.112), calls=%async_computation.4 | async-start | bytes 3145728 | tf_op jit(solution)/shard_map/all_to_all | solution.py:756
  381.3 59.3 %all-to-all-start.5 = ((bf16[4,512,384]{2,1,0:T(8,128)(2,1)}), bf16[4,512,384]{2,1,0:T(8,128)(2,1)S(1)}, u32[]{:S(2)}, u32[]{:S(2)}) async-start(bf16[4,512,384]{2,1,0:T(8,128)(2,1)} %bitcast.111), calls=%async_computation.5 | async-start | bytes 3145728 | tf_op jit(solution)/shard_map/all_to_all | solution.py:756
  386.9 1.8 collective-permute-start.40
  400.3 15.3 %collective-permute-start.33 = (bf16[384,1024]{1,0:T(8,128)(2,1)}, bf16[384,1024]{1,0:T(8,128)(2,1)}, u32[]{:S(2)}, u32[]{:S(2)}) collective-permute-start(bf16[384,1024]{1,0:T(8,128)(2,1)} %broadcast_select_fusion.5), channel_id=1, source_target_pairs={{0,4},{4,0},{1,5},{5,1},{2,6},{6,2},{3,7},{7,3},{8,12},{12,8},{9,1... | collective-permute-start | bytes 2359304 | tf_op jit(solution)/shard_map/ppermute | solution.py:771
  408.1 32.6 %collective-permute-start.30 = (bf16[832,256]{1,0:T(8,128)(2,1)}, bf16[832,256]{1,0:T(8,128)(2,1)S(1)}, u32[]{:S(2)}, u32[]{:S(2)}) collective-permute-start(bf16[832,256]{1,0:T(8,128)(2,1)} %get-tuple-element.331), channel_id=1, source_target_pairs={{0,1},{1,2},{2,3},{3,0},{4,5},{5,6},{6,7},{7,4},{8,9},{9,10},{10,1... | collective-permute-start | bytes 1277960 | tf_op jit(solution)/shard_map/ppermute | solution.py:765
  410.1 39.8 %collective-permute-start.31 = (bf16[832,256]{1,0:T(8,128)(2,1)}, bf16[832,256]{1,0:T(8,128)(2,1)}, u32[]{:S(2)}, u32[]{:S(2)}) collective-permute-start(bf16[832,256]{1,0:T(8,128)(2,1)} %get-tuple-element.330), channel_id=1, source_target_pairs={{0,2},{1,3},{2,0},{3,1},{4,6},{5,7},{6,4},{7,5},{8,10},{9,11},{10,... | collective-permute-start | bytes 1277960 | tf_op jit(solution)/shard_map/ppermute | solution.py:765
  412.4 37.5 %collective-permute-start.32 = (bf16[832,256]{1,0:T(8,128)(2,1)}, bf16[832,256]{1,0:T(8,128)(2,1)}, u32[]{:S(2)}, u32[]{:S(2)}) collective-permute-start(bf16[832,256]{1,0:T(8,128)(2,1)} %get-tuple-element.329), channel_id=1, source_target_pairs={{0,3},{1,0},{2,1},{3,2},{4,7},{5,4},{6,5},{7,6},{8,11},{9,8},{10,9... | collective-permute-start | bytes 1277960 | tf_op jit(solution)/shard_map/ppermute | solution.py:765
  451.6 14.0 %collective-permute-start.39 = (f32[2,352,128]{2,1,0:T(8,128)S(1)}, f32[2,352,128]{2,1,0:T(8,128)S(1)}, u32[]{:S(2)}, u32[]{:S(2)}) collective-permute-start(f32[2,352,128]{2,1,0:T(8,128)S(1)} %slice_select_fusion.1), channel_id=1, source_target_pairs={{0,4},{4,0},{1,5},{5,1},{2,6},{6,2},{3,7},{7,3},{8,12},{12,8},{9,1... | collective-permute-start | bytes 1081352 | tf_op jit(solution)/shard_map/ppermute | solution.py:771
  451.8 10.5 %collective-permute-start.34 = (bf16[384,256]{1,0:T(8,128)(2,1)S(1)}, bf16[384,256]{1,0:T(8,128)(2,1)S(1)}, u32[]{:S(2)}, u32[]{:S(2)}) collective-permute-start(bf16[384,256]{1,0:T(8,128)(2,1)S(1)} %get-tuple-element.339), channel_id=1, source_target_pairs={{0,8},{8,0},{16,24},{24,16},{1,9},{9,1},{17,25},{25,17},{2,10},{10... | collective-permute-start | bytes 589832 | tf_op jit(solution)/shard_map/ppermute | solution.py:892
  453.2 11.2 %collective-permute-start.35 = (bf16[384,256]{1,0:T(8,128)(2,1)S(1)}, bf16[384,256]{1,0:T(8,128)(2,1)S(1)}, u32[]{:S(2)}, u32[]{:S(2)}) collective-permute-start(bf16[384,256]{1,0:T(8,128)(2,1)S(1)} %get-tuple-element.341), channel_id=1, source_target_pairs={{0,16},{8,24},{16,0},{24,8},{1,17},{9,25},{17,1},{25,9},{2,18},{10... | collective-permute-start | bytes 589832 | tf_op jit(solution)/shard_map/ppermute | solution.py:892
  453.9 10.6 %collective-permute-start.36 = (bf16[384,256]{1,0:T(8,128)(2,1)S(1)}, bf16[384,256]{1,0:T(8,128)(2,1)S(1)}, u32[]{:S(2)}, u32[]{:S(2)}) collective-permute-start(bf16[384,256]{1,0:T(8,128)(2,1)S(1)} %get-tuple-element.340), channel_id=1, source_target_pairs={{0,24},{8,16},{16,8},{24,0},{1,25},{9,17},{17,9},{25,1},{2,26},{10... | collective-permute-start | bytes 589832 | tf_op jit(solution)/shard_map/ppermute | solution.py:892
  455.3 7.0 %collective-permute-start.38 = (f32[128,128]{1,0:T(8,128)S(1)}, f32[128,128]{1,0:T(8,128)S(1)}, u32[]{:S(2)}, u32[]{:S(2)}) collective-permute-start(f32[128,128]{1,0:T(8,128)S(1)} %slice_select_fusion.7), channel_id=1, source_target_pairs={{0,4},{4,0},{1,5},{5,1},{2,6},{6,2},{3,7},{7,3},{8,12},{12,8},{9,1... | collective-permute-start | bytes 196616 | tf_op jit(solution)/shard_map/ppermute | solution.py:771
  465.5 1.5 collective-permute-start.37
  467.8 14.4 %copy-start.21 = (f32[3,128,256]{2,1,0:T(8,128)}, f32[3,128,256]{2,1,0:T(8,128)S(1)}, u32[]{:S(2)}) copy-start(f32[3,128,256]{2,1,0:T(8,128)S(1)} %reshape.155) | copy-start | bytes 1179652
  468.0 11.8 %collective-permute-start.41 = (f32[2,128]{1,0:T(2,128)S(1)}, f32[2,128]{1,0:T(2,128)S(1)}, u32[]{:S(2)}, u32[]{:S(2)}) collective-permute-start(f32[2,128]{1,0:T(2,128)S(1)} %pad_maximum_fusion.12), channel_id=1, source_target_pairs={{0,1},{1,2},{2,3},{3,0},{4,5},{5,6},{6,7},{7,4},{8,9},{9,10},{10,1... | collective-permute-start | bytes 3080 | tf_op jit(solution)/shard_map/ppermute | solution.py:765
  476.7 4.5 collective-permute-start.42
  478.1 3.6 collective-permute-start.43
  (27 other events, 142.0 us)
Sparse Core Ops, SparseCore 0:
  20.5 28.4 all-gather.2
  217.8 44.8 all-gather.4
  267.3 40.2 reduce-scatter.6
  310.4 74.5 reduce-scatter.8
